TPU v7x, 128 devices: a whole 4x4x4 slice. The times are simulated.
128 devices in a mesh: seq: 16 (over z, x), req: 8 (over y, core).
Axes of the slice: x: 4, y: 4, z: 4, core: 2. Of those that a mesh axis runs over, the one named last changes fastest.
Arguments:
- given_token_index: int32 [128], replicated, may hold values from 0 to 31999
- hidden: bfloat16 [128, 3584], P('req'), may hold values from -6 to 6
- token_embedding_table: bfloat16 [32000, 3584], P(('seq', 'req')), may hold values from -6 to 6
- attention_norm_gain: bfloat16 [7168], replicated, may hold values from 0.099609375 to 1.8984375
- query_key_value_weight: bfloat16 [7168, 10752], P('req', 'seq'), may hold values from -0.0625 to 0.0625
- rotated_key_cache: bfloat16 [96, 8, 128, 3584], P('seq', 'req'), may hold values from -240 to 240
- cached_value_pages: bfloat16 [96, 8, 128, 3584], P('seq', 'req'), may hold values from -6 to 6
- lengths: int32 [32], P('req'), may hold values from 1 to 6144, as said below
- request_page_slots: int32 [32, 48], P('req'), may hold values from 0 to 95, as said below
- attention_output_weight: bfloat16 [3584, 7168], P('seq'), may hold values from -0.375 to 0.375
- feedforward_norm_gain: bfloat16 [7168], replicated, may hold values from 0.099609375 to 1.8984375
- gate_weight: bfloat16 [7168, 14336], P('req', 'seq'), may hold values from -0.0625 to 0.0625
- up_weight: bfloat16 [7168, 14336], P('req', 'seq'), may hold values from -0.0625 to 0.0625
- adapter_down_map: bfloat16 [7168, 128], P('req'), may hold values from -0.0625 to 0.0625
- adapter_gate_map: bfloat16 [128, 14336], P(None, 'seq'), may hold values from -0.5 to 0.5
- adapter_up_map: bfloat16 [128, 14336], P(None, 'seq'), may hold values from -0.5 to 0.5
- down_weight: bfloat16 [14336, 7168], P('seq', 'req'), may hold values from -0.046875 to 0.046875
Outputs:
- block_out: bfloat16 [128, 7168], P('seq', 'req')
Inputs may be any that keep to these rules, and one draw needn't show every extreme that they name: `lengths`: in each group of 4 requests exactly one has 6144 tokens, and the pages of a group's requests number at most 96 together. `request_page_slots`: entry p of request i names a slot of its group, 0 to 95; the entries with p * 128 below lengths[i] are distinct within a group, the others name any slot. Slot g of a group lies on the seq index g // 6, at place g % 6.
All inputs are finite; a program needn't handle non-finite values.
Results may differ from a plain program's by a relative error of at most 0.028.
The roundings to bfloat16 on the way count: a program that leaves them out, or rounds other values in their place, can miss the bound.
Values may be sent and summed in bfloat16 or wider, within the bound.
A program may use at most 128 MiB of HBM per device.

v0:
```python
import math

import jax
import jax.numpy as jnp
from jax import lax
from jax.sharding import PartitionSpec as P

HEADS = 16
HD = 224


NEGATIVE = -1e30
EPSILON = 1e-05
ROTARY_BASE = 10000.0


def merged_2(array, axis, combine):
    everything = jax.tree.map(lambda part: lax.all_gather(part, axis), array)
    first = jax.tree.map(lambda part: part[0], everything)

    def hop(k, so_far):
        return combine(so_far, jax.tree.map(lambda part: part[k], everything))

    return lax.fori_loop(1, lax.axis_size(axis), hop, first)


def rms_norm(matrix, gain_vec):
    widened = matrix.astype(jnp.float32)
    factor = lax.rsqrt(jnp.mean(widened * widened, axis=-1, keepdims=True) + EPSILON)
    return (widened * factor * gain_vec.astype(jnp.float32)).astype(jnp.bfloat16)


def rotate(vectors, positions):
    half_dim = vectors.shape[-1] // 2
    frequency = ROTARY_BASE ** (-2.0 * jnp.arange(half_dim, dtype=jnp.float32) / vectors.shape[-1])
    angles = positions.astype(jnp.float32)[..., None, None] * frequency
    cosine = jnp.cos(angles)
    sine_part = jnp.sin(angles)
    front_half = vectors[..., :half_dim]
    back_half = vectors[..., half_dim:]
    return jnp.concatenate(
        [front_half * cosine - back_half * sine_part, back_half * cosine + front_half * sine_part],
        axis=-1,
    )


def softmax_join(earlier, later):
    first_max, first_sum, first_out = earlier
    second_max, second_sum, second_out = later
    overall = jnp.maximum(first_max, second_max)
    first_factor = jnp.exp(first_max - overall)
    second_factor = jnp.exp(second_max - overall)
    return (
        overall,
        first_sum * first_factor + second_sum * second_factor,
        first_out * first_factor[..., None] + second_out * second_factor[..., None],
    )


def body(
    given_token_index,
    hidden,
    token_embedding_table,
    attention_norm_gain,
    query_key_value_weight,
    rotated_key_cache,
    cached_value_pages,
    lengths,
    request_page_slots,
    attention_output_weight,
    feedforward_norm_gain,
    gate_weight,
    up_weight,
    adapter_down_map,
    adapter_gate_map,
    adapter_up_map,
    down_weight,
):
    seq_devices = lax.axis_size("seq")
    req_devices = lax.axis_size("req")
    seq_index = lax.axis_index("seq")
    req_index = lax.axis_index("req")
    group_rows = hidden.shape[0]
    requests = lengths.shape[0]
    steps_each = group_rows // requests
    vocab_rows = token_embedding_table.shape[0]
    first_id = (seq_index * req_devices + req_index) * vocab_rows
    local_ids = given_token_index - first_id
    present = (local_ids >= 0) & (local_ids < vocab_rows)
    looked = jnp.take(token_embedding_table, jnp.clip(local_ids, 0, vocab_rows - 1), axis=0).astype(
        jnp.float32
    )
    looked = jnp.where(present[:, None], looked, 0.0)
    everywhere = lax.psum(looked, ("seq", "req"))
    embedded = lax.dynamic_slice_in_dim(everywhere, req_index * group_rows, group_rows, 0)
    joined = jnp.concatenate([hidden, embedded.astype(jnp.bfloat16)], axis=1)
    normed = rms_norm(joined, attention_norm_gain)
    spread = lax.all_to_all(normed, "req", split_axis=1, concat_axis=0, tiled=True)
    block_rows = spread
    qkv_part = lax.psum_scatter(
        jnp.dot(block_rows, query_key_value_weight, preferred_element_type=jnp.float32),
        "req",
        scatter_dimension=0,
        tiled=True,
    )
    projected = lax.all_gather(qkv_part.astype(jnp.bfloat16), "seq", axis=1, tiled=True)
    head_cols = HEADS * HD
    queries = projected[:, :head_cols].reshape(requests, steps_each, HEADS, HD)
    new_keys = projected[:, head_cols : 2 * head_cols].reshape(requests, steps_each, HEADS, HD)
    new_values = projected[:, 2 * head_cols :].reshape(requests, steps_each, HEADS, HD)
    positions = lengths[:, None] + jnp.arange(steps_each, dtype=jnp.int32)[None, :]
    queries = rotate(queries.astype(jnp.float32), positions).astype(jnp.bfloat16)
    new_keys = rotate(new_keys.astype(jnp.float32), positions).astype(jnp.bfloat16)
    slots = rotated_key_cache.shape[0]
    page_len = rotated_key_cache.shape[2]
    cache_k = rotated_key_cache.reshape(slots * page_len, HEADS, HD)
    cache_v = cached_value_pages.reshape(slots * page_len, HEADS, HD)
    slot_ids = seq_index * slots + jnp.arange(slots, dtype=jnp.int32)
    page_ids = jnp.arange(request_page_slots.shape[1], dtype=jnp.int32)
    is_live = page_ids[None, :] < ((lengths + page_len - 1) // page_len)[:, None]
    matches = (request_page_slots[:, :, None] == slot_ids[None, None, :]) & is_live[:, :, None]
    is_owned = jnp.any(matches, axis=1)
    page_of = jnp.sum(jnp.where(matches, page_ids[None, :, None], 0), axis=1)
    token_pos = (
        page_of[:, :, None] * page_len + jnp.arange(page_len, dtype=jnp.int32)[None, None, :]
    )
    is_valid = (is_owned[:, :, None] & (token_pos < lengths[:, None, None])).reshape(
        requests, slots * page_len
    )
    score_scale = 1.0 / math.sqrt(HD)
    scores = (
        jnp.einsum("rthd,khd->rthk", queries, cache_k, preferred_element_type=jnp.float32)
        * score_scale
    )
    mask_b = is_valid[:, None, None, :]
    local_max = jnp.max(jnp.where(mask_b, scores, NEGATIVE), axis=-1)
    weights = jnp.where(mask_b, jnp.exp(scores - local_max[..., None]), 0.0)
    local_sum = jnp.sum(weights, axis=-1)
    local_out = jnp.einsum(
        "rthk,khd->rthd", weights.astype(jnp.bfloat16), cache_v, preferred_element_type=jnp.float32
    )
    fresh_scores = (
        jnp.einsum("rthd,rshd->rths", queries, new_keys, preferred_element_type=jnp.float32)
        * score_scale
    )
    causal = jnp.arange(steps_each)[:, None] >= jnp.arange(steps_each)[None, :]
    fresh_mask = causal[None, :, None, :]
    fresh_max = jnp.max(jnp.where(fresh_mask, fresh_scores, NEGATIVE), axis=-1)
    fresh_w = jnp.where(fresh_mask, jnp.exp(fresh_scores - fresh_max[..., None]), 0.0)
    fresh_sum = jnp.sum(fresh_w, axis=-1)
    fresh_out = jnp.einsum(
        "rths,rshd->rthd",
        fresh_w.astype(jnp.bfloat16),
        new_values,
        preferred_element_type=jnp.float32,
    )
    own_heads = HEADS // seq_devices
    first_head = seq_index * own_heads

    def own_slice(member):
        return lax.dynamic_slice_in_dim(member, first_head, own_heads, 2)

    fresh_part = (own_slice(fresh_max), own_slice(fresh_sum), own_slice(fresh_out))
    merged = merged_2((local_max, local_sum, local_out), "seq", softmax_join)
    combined = softmax_join(tuple((own_slice(member) for member in merged)), fresh_part)
    attention = (
        (combined[2] / combined[1][..., None])
        .astype(jnp.bfloat16)
        .reshape(group_rows, own_heads * HD)
    )
    projected_out = jnp.dot(attention, attention_output_weight, preferred_element_type=jnp.float32)
    mixed_sum = lax.psum(projected_out, "seq")
    after_attn = (joined.astype(jnp.float32) + mixed_sum).astype(jnp.bfloat16)
    second_normed_state = rms_norm(after_attn, feedforward_norm_gain)
    residual_cols, second_spread_state = (
        lax.all_to_all(after_attn, "req", split_axis=1, concat_axis=0, tiled=True),
        lax.all_to_all(second_normed_state, "req", split_axis=1, concat_axis=0, tiled=True),
    )
    gate_total, up_total, low_sum = lax.psum(
        (
            jnp.dot(second_spread_state, gate_weight, preferred_element_type=jnp.float32),
            jnp.dot(second_spread_state, up_weight, preferred_element_type=jnp.float32),
            jnp.dot(second_spread_state, adapter_down_map, preferred_element_type=jnp.float32),
        ),
        "req",
    )
    adapter_hidden = low_sum.astype(jnp.bfloat16)
    gate_preactivation = gate_total + jnp.dot(
        adapter_hidden, adapter_gate_map, preferred_element_type=jnp.float32
    )
    up_projection_part = up_total + jnp.dot(
        adapter_hidden, adapter_up_map, preferred_element_type=jnp.float32
    )
    inner_act = (jax.nn.silu(gate_preactivation) * up_projection_part).astype(jnp.bfloat16)
    out_rows = residual_cols.shape[0] // seq_devices
    block_rows = inner_act
    down_sum = lax.psum_scatter(
        jnp.dot(block_rows, down_weight, preferred_element_type=jnp.float32),
        "seq",
        scatter_dimension=0,
        tiled=True,
    )
    residual_rows = lax.dynamic_slice_in_dim(residual_cols, seq_index * out_rows, out_rows, 0)
    return (residual_rows.astype(jnp.float32) + down_sum).astype(jnp.bfloat16)


def solution(mesh):
    placed = (
        P(),
        P("req", None),
        P(("seq", "req"), None),
        P(),
        P("req", "seq"),
        P("seq", "req", None, None),
        P("seq", "req", None, None),
        P("req"),
        P("req", None),
        P("seq", None),
        P(),
        P("req", "seq"),
        P("req", "seq"),
        P("req", None),
        P(None, "seq"),
        P(None, "seq"),
        P("seq", "req"),
    )
    return jax.shard_map(
        body, mesh=mesh, in_specs=placed, out_specs=P("seq", "req"), check_vma=False
    )
```

profile of v0, /device:TPU:1, one launch (start us, length us, event | category | flops | bytes accessed | tf_op | source)
XLA Modules:
  0.0 528.4 jit_solution(585776612457046075)
XLA Ops:
  7.4 4.9 gather_fusion
  12.2 2.8 convert_select_fusion
  15.0 75.4 %all-reduce.12 = bf16[128,3584]{1,0:T(8,128)(2,1)} all-reduce(f32[128,3584]{1,0:T(8,128)} %convert_select_fusion), channel_id=1, replica_groups=mesh['seq'=16,'req'=8] {'seq','req'}, use_global_device_ids=true, to_apply=%region_0.1 | all-reduce | flops 458752 | bytes 2752512 | tf_op jit(solution)/shard_map/psum | solution.py:94
  90.4 0.9 dynamic-slice_convert_fusion
  94.1 1.0 multiply_convert_fusion
  95.9 4.0 all-to-all-start
  100.6 0.9 select_reduce_fusion.1
  101.6 1.5 fusion.55
  104.3 1.3 copy.111
  105.5 1.3 broadcast_bitcast_fusion.1
  106.8 1.3 add_convert_fusion.2
  108.1 2.6 fusion.67
  111.5 13.1 %reshape.185 = bf16[768,16,224]{2,1,0:T(8,128)(2,1)} reshape(bf16[6,1,128,3584]{3,2,1,0:T(8,128)(2,1)} %param.24) | data formatting | bytes 11010048 | tf_op jit(solution)/shard_map/reshape | solution.py:116
  124.7 13.2 %reshape.186 = bf16[768,16,224]{2,1,0:T(8,128)(2,1)} reshape(bf16[6,1,128,3584]{3,2,1,0:T(8,128)(2,1)} %param.25) | data formatting | bytes 11010048 | tf_op jit(solution)/shard_map/reshape | solution.py:117
  140.1 17.7 %all-gather.3 = bf16[16,672,16]{1,2,0:T(8,128)(2,1)S(1)} all-gather(bf16[1,672,16]{1,2,0:T(8,128)(2,1)S(1)} %convert_bitcast_fusion), channel_id=1, replica_groups=mesh['seq'=16,'req'=8] {'seq'}, dimensions={0}, use_global_device_ids=true | all-gather | bytes 365568 | tf_op jit(solution)/shard_map/all_gather | solution.py:106
  157.8 0.9 copy.114
  158.7 1.5 reshape.211
  160.2 0.9 fusion.64
  161.1 1.1 reshape.191
  163.0 1.1 reshape.190
  164.2 1.3 subtract_convert_fusion
  165.6 6.8 %select_reduce_fusion = (f32[4,4,16]{1,0,2:T(4,128)S(1)}, f32[4,4,16,768]{3,1,0,2:T(4,128)S(1)}) fusion(pred[4,768]{1,0:T(4,128)(4,1)} %fusion.54, bf16[768,16,224,1]{2,1,0,3:T(8,128)(2,1)} %bitcast.116, bf16[4,4,16,112]{3,1,0,2:T(4,128)(2,1)S(1)} %get-tuple-element.268, bf16[4,4,16,112]{3,1,0,2:T(4,128)(2,1)S(1)} %get-tuple-element.269), kind=kOutput, calls=%fused_computation.25 | convolution fusion | flops 88899328 | bytes 6410240 | tf_op jit(solution)/shard_map/rthd,khd->rthk/dot_general | solution.py:132
  172.5 0.9 copy-done.9
  173.4 4.6 fusion.16
  179.3 2.3 fusion.21
  182.4 16.6 %all-gather.1 = f32[64,4,16]{2,1,0:T(4,128)S(1)} all-gather(f32[4,4,16]{2,1,0:T(4,128)S(1)} %copy.119), channel_id=3, replica_groups=mesh['seq'=16,'req'=8] {'seq'}, dimensions={0}, use_global_device_ids=true | all-gather | bytes 17408 | tf_op jit(solution)/shard_map/all_gather | solution.py:18
  199.0 17.6 %all-gather = f32[64,4,16]{2,1,0:T(4,128)S(1)} all-gather(f32[4,4,16]{2,1,0:T(4,128)} %copy.118), channel_id=2, replica_groups=mesh['seq'=16,'req'=8] {'seq'}, dimensions={0}, use_global_device_ids=true | all-gather | bytes 17408 | tf_op jit(solution)/shard_map/all_gather | solution.py:18
  216.6 1.2 pad_maximum_fusion.1
  217.8 0.9 fusion.39
  218.7 1.1 copy.129
  223.2 0.9 fusion.37
  224.1 10.1 %all-gather.6.cloned.1.call-done = f32[64,4,16,224]{3,1,0,2:T(4,128)} async-done(((f32[4,4,16,224]{3,1,0,2:T(4,128)}), f32[64,4,16,224]{3,1,0,2:T(4,128)}) %all-gather.6.cloned.1.call-update) | async-done | bytes 3670032 | tf_op jit(solution)/shard_map/all_gather | solution.py:18
  234.2 1.0 slice.50
  235.3 29.8 %while.19 = (s32[]{:T(128)}, f32[4,4,16]{2,1,0:T(4,128)S(1)}, f32[4,4,16]{2,1,0:T(4,128)S(1)}, f32[4,4,16,224]{3,2,1,0:T(8,128)S(1)}, f32[16,4,4,16]{3,2,1,0:T(4...) while((s32[]{:T(128)}, f32[4,4,16]{2,1,0:T(4,128)S(1)}, ...), condition=%wide.region_8.9_spmd, body=%wide.region_7.8_spmd.sunk | while | flops 173573 | bytes 1157271 | solution.py:24
  236.1 1.0 constant_dynamic-slice_fusion.5
  238.1 1.0 constant_dynamic-slice_fusion.5
  240.1 1.0 constant_dynamic-slice_fusion.5
  242.1 1.0 constant_dynamic-slice_fusion.5
  244.1 1.0 constant_dynamic-slice_fusion.5
  246.0 1.0 constant_dynamic-slice_fusion.5
  248.0 1.0 constant_dynamic-slice_fusion.5
  250.0 1.0 constant_dynamic-slice_fusion.5
  252.0 1.0 constant_dynamic-slice_fusion.5
  254.0 1.0 constant_dynamic-slice_fusion.5
  256.0 1.0 constant_dynamic-slice_fusion.5
  258.0 1.0 constant_dynamic-slice_fusion.5
  260.0 1.0 constant_dynamic-slice_fusion.5
  262.0 1.0 constant_dynamic-slice_fusion.5
  263.9 1.0 constant_dynamic-slice_fusion.5
  267.1 1.3 fusion.68
  268.5 87.6 %all-reduce.7.cloned.1.call-done = f32[16,7168]{1,0:T(8,128)} async-done(((f32[16,7168]{1,0:T(8,128)}), f32[16,7168]{1,0:T(8,128)}) %all-reduce.7.cloned.1.call-update) | async-done | bytes 458768 | tf_op jit(solution)/shard_map/psum | solution.py:172
  356.1 1.3 fusion.24
  357.6 12.5 %all_to_all.54 = bf16[16,8,896]{2,0,1:T(8,128)(2,1)S(1)} all-to-all(bf16[16,8,896]{2,0,1:T(8,128)(2,1)S(1)} %bitcast.125), channel_id=1, replica_groups=mesh['seq'=16,'req'=8] {'req'}, dimensions={1} | all-to-all | bytes 458752 | tf_op jit(solution)/shard_map/all_to_all | solution.py:177
  370.1 1.2 fusion.69
  371.3 1.3 fusion.71
  372.7 1.2 fusion.70
  373.8 22.2 %psum.38 = bf16[128,128]{1,0:T(8,128)(2,1)S(1)} all-reduce(f32[128,128]{1,0:T(8,128)S(1)} %fusion.70), channel_id=1, replica_groups=mesh['seq'=16,'req'=8] {'req'}, use_global_device_ids=true, to_apply=%region_14.15 | all-reduce | flops 16384 | bytes 98304 | tf_op jit(solution)/shard_map/psum | solution.py:179
  396.0 34.5 %all-reduce.11.cloned.1.call-done = (f32[128,896]{1,0:T(8,128)}, f32[128,896]{1,0:T(8,128)}) async-done(((f32[128,896]{1,0:T(8,128)}, f32[128,896]{1,0:T(8,128)}), (f32[128,896]{1,0:T(8,128)}, f32[128,896]{1,0:T(8,128)})) %all-reduce.11.cloned.1.call-update) | async-done | bytes 917520 | tf_op jit(solution)/shard_map/psum | solution.py:179
  430.5 2.1 convolution_add_fusion.1
  432.7 3.2 fusion.19
  436.6 6.0 %all-to-all-start.1 = ((bf16[16,8,896]{2,0,1:T(8,128)(2,1)}), bf16[16,8,896]{2,0,1:T(8,128)(2,1)S(1)}, u32[]{:S(2)}, u32[]{:S(2)}) async-start(bf16[16,8,896]{2,0,1:T(8,128)(2,1)} %bitcast.123), calls=%async_computation.2 | async-start | bytes 458752 | tf_op jit(solution)/shard_map/all_to_all | solution.py:176
  443.8 5.0 all-to-all-done.1
  448.8 71.7 %all-reduce.9.cloned.1.call-done = f32[128,896]{1,0:T(8,128)} async-done(((f32[128,896]{1,0:T(8,128)}), f32[128,896]{1,0:T(8,128)}) %all-reduce.9.cloned.1.call-update) | async-done | bytes 458768
  520.5 1.4 fusion.45
  (139 shorter events, 34.4 us)
Async XLA Ops:
  6.5 260.6 %copy-start = (bf16[224,7168]{1,0:T(8,128)(2,1)S(1)}, bf16[224,7168]{1,0:T(8,128)(2,1)}, u32[]{:S(2)}) copy-start(bf16[224,7168]{1,0:T(8,128)(2,1)} %param.28) | copy-start | bytes 9633796
  15.0 76.3 %copy-start.7 = (bf16[16,3584]{1,0:T(8,128)(2,1)S(1)}, bf16[16,3584]{1,0:T(8,128)(2,1)}, u32[]{:S(2)}) copy-start(bf16[16,3584]{1,0:T(8,128)(2,1)} %param.20) | copy-start | bytes 344068
  91.3 19.4 %copy-start.3 = (bf16[16,3584]{1,0:T(8,128)(2,1)}, bf16[16,3584]{1,0:T(8,128)(2,1)S(1)}, u32[]{:S(2)}) copy-start(bf16[16,3584]{1,0:T(8,128)(2,1)S(1)} %dynamic-slice_convert_fusion) | copy-start | bytes 344068
  95.9 12.2 %all-to-all-start = ((bf16[16,8,896]{2,0,1:T(8,128)(2,1)}), bf16[16,8,896]{2,0,1:T(8,128)(2,1)S(1)}, u32[]{:S(2)}, u32[]{:S(2)}) async-start(bf16[16,8,896]{2,0,1:T(8,128)(2,1)} %copy.113), calls=%async_computation | async-start | bytes 458752 | tf_op jit(solution)/shard_map/all_to_all | solution.py:98
  99.9 39.4 %reduce-scatter.2.cloned.1.call-start = ((), (), s32[]{:S(2)}) async-start(), calls=%async_computation.4 | async-start | bytes 442368 | tf_op jit(solution)/shard_map/reduce_scatter | solution.py:100
  110.7 123.5 %all-gather.6.cloned.1.call-start = ((), (), s32[]{:S(2)}) async-start(), calls=%async_computation.6 | async-start | bytes 4456448 | tf_op jit(solution)/shard_map/all_gather | solution.py:18
  124.7 13.2 %copy-start.20 = (f32[4,4]{1,0:T(4,128)S(1)}, f32[4,4]{1,0:T(4,128)}, u32[]{:S(2)}) copy-start(f32[4,4]{1,0:T(4,128)} %add_convert_fusion.2) | copy-start | bytes 196
  124.7 14.0 %copy-start.16 = (s32[768]{0:T(1024)S(1)}, s32[768]{0:T(1024)}, u32[]{:S(2)}) copy-start(s32[768]{0:T(1024)} %iota_bitcast_fusion) | copy-start | bytes 9220
  124.7 14.0 %copy-start.17 = (pred[1,4,6,128]{3,2,1,0:T(8,128)(4,1)S(1)}, pred[1,4,6,128]{3,2,1,0:T(8,128)(4,1)}, u32[]{:S(2)}) copy-start(pred[1,4,6,128]{3,2,1,0:T(8,128)(4,1)} %broadcast_bitcast_fusion.1) | copy-start | bytes 9220
  124.7 14.0 %copy-start.21 = (s32[4]{0:T(128)S(1)}, s32[4]{0:T(128)}, u32[]{:S(2)}) copy-start(s32[4]{0:T(128)} %param.26) | copy-start | bytes 52
  161.1 3.1 copy-start.14
  161.1 3.1 copy-start.15
  164.2 9.2 %slice-start = ((s8[6291456]{0:T(1024)(128)(4,1)}), s8[4194304]{0:T(1024)(128)(4,1)S(1)}, s32[]{:S(2)}) async-start(s8[6291456]{0:T(1024)(128)(4,1)} %bitcast.113), calls=%async_computation.9 | async-start | bytes 8388608
  165.6 6.9 %copy-start.11 = (bf16[4,4,16,112]{3,1,0,2:T(4,128)(2,1)}, bf16[4,4,16,112]{3,1,0,2:T(4,128)(2,1)S(1)}, u32[]{:S(2)}) copy-start(bf16[4,4,16,112]{3,1,0,2:T(4,128)(2,1)S(1)} %get-tuple-element.269) | copy-start | bytes 172036
  165.6 7.8 %slice-start.1 = ((s8[6291456]{0:T(1024)(128)(4,1)}), s8[2097152]{0:T(1024)(128)(4,1)S(1)}, s32[]{:S(2)}) async-start(s8[6291456]{0:T(1024)(128)(4,1)} %bitcast.113), calls=%async_computation.10 | async-start | bytes 4194304
  165.6 7.8 %copy-start.19 = (pred[4,768]{1,0:T(4,128)(4,1)S(1)}, pred[4,768]{1,0:T(4,128)(4,1)}, u32[]{:S(2)}) copy-start(pred[4,768]{1,0:T(4,128)(4,1)} %fusion.54) | copy-start | bytes 9220
  172.5 0.9 copy-start.9
  178.0 45.0 %copy-start.10 = (bf16[16,3584]{1,0:T(8,128)(2,1)S(1)}, bf16[16,3584]{1,0:T(8,128)(2,1)}, u32[]{:S(2)}) copy-start(bf16[16,3584]{1,0:T(8,128)(2,1)} %get-tuple-element.255) | copy-start | bytes 344068
  178.0 178.1 %all-reduce.7.cloned.1.call-start = ((), (), s32[]{:S(2)}) async-start(), calls=%async_computation.5 | async-start | bytes 917504 | tf_op jit(solution)/shard_map/psum | solution.py:172
  199.0 18.7 %copy-start.12 = (f32[64,4,16]{2,1,0:T(4,128)}, f32[64,4,16]{2,1,0:T(4,128)S(1)}, u32[]{:S(2)}) copy-start(f32[64,4,16]{2,1,0:T(4,128)S(1)} %all-gather.1) | copy-start | bytes 49156
  216.6 1.2 copy-start.13
  267.1 1.4 copy-start.18
  267.1 89.0 %copy-start.4 = (bf16[16,3584]{1,0:T(8,128)(2,1)S(1)}, bf16[16,3584]{1,0:T(8,128)(2,1)}, u32[]{:S(2)}) copy-start(bf16[16,3584]{1,0:T(8,128)(2,1)} %copy-done.3) | copy-start | bytes 344068
  267.1 89.0 %copy-start.8 = (bf16[16,3584]{1,0:T(8,128)(2,1)S(1)}, bf16[16,3584]{1,0:T(8,128)(2,1)}, u32[]{:S(2)}) copy-start(bf16[16,3584]{1,0:T(8,128)(2,1)} %param.20) | copy-start | bytes 344068
  268.5 162.1 %all-reduce.11.cloned.1.call-start = ((), (), s32[]{:S(2)}) async-start(), calls=%async_computation.8 | async-start | bytes 1835008 | tf_op jit(solution)/shard_map/psum | solution.py:179
  356.1 14.0 %copy-start.5 = (bf16[896,896]{1,0:T(8,128)(2,1)S(1)}, bf16[896,896]{1,0:T(8,128)(2,1)}, u32[]{:S(2)}) copy-start(bf16[896,896]{1,0:T(8,128)(2,1)} %param.30) | copy-start | bytes 4816900
  357.5 13.9 %copy-start.1 = (bf16[16,7168]{1,0:T(8,128)(2,1)}, bf16[16,7168]{1,0:T(8,128)(2,1)S(1)}, u32[]{:S(2)}) copy-start(bf16[16,7168]{1,0:T(8,128)(2,1)S(1)} %get-tuple-element.249) | copy-start | bytes 688132
  357.5 13.9 %copy-start.6 = (bf16[896,896]{1,0:T(8,128)(2,1)S(1)}, bf16[896,896]{1,0:T(8,128)(2,1)}, u32[]{:S(2)}) copy-start(bf16[896,896]{1,0:T(8,128)(2,1)} %param.31) | copy-start | bytes 4816900
  372.6 147.9 %all-reduce.9.cloned.1.call-start = ((), (), s32[]{:S(2)}) async-start(), calls=%async_computation.7 | async-start | bytes 917504
  432.7 3.2 copy-start.2
  432.7 9.9 %copy-start.22 = (u32[128]{0:T(128)S(1)}, u32[128]{0:T(128)}, u32[]{:S(2)}) copy-start(u32[128]{0:T(128)} %constant.127) | copy-start | bytes 1540
  436.6 12.2 %all-to-all-start.1 = ((bf16[16,8,896]{2,0,1:T(8,128)(2,1)}), bf16[16,8,896]{2,0,1:T(8,128)(2,1)S(1)}, u32[]{:S(2)}, u32[]{:S(2)}) async-start(bf16[16,8,896]{2,0,1:T(8,128)(2,1)} %bitcast.123), calls=%async_computation.2 | async-start | bytes 458752 | tf_op jit(solution)/shard_map/all_to_all | solution.py:176
Sparse Core Ops, SparseCore 0:
  110.8 26.2 reduce-scatter.1
  178.1 56.0 all-gather.5
  268.6 87.5 all-reduce.6
  372.7 57.7 all-reduce.10
  436.0 84.4 all-reduce.8
where the time goes:
time: 532 us; the launch traced here: 528 us
  waiting for transfers between devices  209 us (39%)
  blocking collectives  162 us (30%)
  local copies, waits for them, and re-layouts  66.7 us (13%)
  other arithmetic  40.1 us (8%)
  matrix products  26 us (5%)
  between operations  14.1 us (3%)
  starting transfers between devices  10.1 us (2%)
    psum x1, waiting for transfers between devices, body(): mixed_sum = lax.psum(projected_out, 'seq')  87.6 us
    psum x1, blocking collectives, body(): everywhere = lax.psum(looked, ('seq', 'req'))  75.4 us
    unnamed x6, waiting for transfers between devices  71.8 us
    psum x1, waiting for transfers between devices, body(): lax.psum((jnp.dot(second_spread_state, gate_weight, preferred_element_typ...  34.5 us
    all_gather x2, blocking collectives, merged_2(): everything = jax.tree.map(lambda part: lax.all_gather(part, axis), array)  34.2 us
    psum x1, blocking collectives, body(): lax.psum((jnp.dot(second_spread_state, gate_weight, preferred_element_typ...  22.2 us
    all_gather x1, blocking collectives, body(): lax.all_gather(qkv_part.astype(jnp.bfloat16), 'seq', axis=1, tiled=True)  17.7 us
    dynamic_slice x15, local copies, waits for them, and re-layouts, hop(): return combine(so_far, jax.tree.map(lambda part: part[k], everything))  14.7 us
  transfers between devices with their start and end apart: 7, of which 5 were waited for; matrix products, arithmetic and copies ran while one was open for 10% of the time, Pallas kernels for 0%

commit v1 on v0

--- a/solution.py
+++ b/solution.py
@@ -1,8 +1,11 @@
+import functools
 import math
 
 import jax
 import jax.numpy as jnp
 from jax import lax
+from jax.experimental import pallas as pl
+from jax.experimental.pallas import tpu as pltpu
 from jax.sharding import PartitionSpec as P
 
 HEADS = 16
@@ -12,6 +15,54 @@
 NEGATIVE = -1e30
 EPSILON = 1e-05
 ROTARY_BASE = 10000.0
+
+
+MESH_ID = pl.DeviceIdType.MESH
+
+
+def _exchange_kernel(axis, n, gather, x_ref, y_ref, send_sem, recv_sem, local_sem):
+    me = lax.axis_index(axis)
+    barrier = pltpu.get_barrier_semaphore()
+    for k in range(1, n):
+        peer = lax.rem(me + k, n)
+        pl.semaphore_signal(barrier, 1, device_id={axis: peer}, device_id_type=MESH_ID)
+    pl.semaphore_wait(barrier, n - 1)
+    copies = []
+    for k in range(1, n):
+        peer = lax.rem(me + k, n)
+        source = x_ref if gather else x_ref.at[peer]
+        copy = pltpu.make_async_remote_copy(
+            src_ref=source,
+            dst_ref=y_ref.at[me],
+            send_sem=send_sem.at[k],
+            recv_sem=recv_sem.at[k],
+            device_id={axis: peer},
+            device_id_type=MESH_ID,
+        )
+        copy.start()
+        copies.append(copy)
+    local = pltpu.make_async_copy(x_ref if gather else x_ref.at[me], y_ref.at[me], local_sem)
+    local.start()
+    local.wait()
+    for copy in copies:
+        copy.wait()
+
+
+def exchange(x, axis, cid, gather=False):
+    n = lax.axis_size(axis)
+    out_shape = (n,) + x.shape if gather else x.shape
+    return pl.pallas_call(
+        functools.partial(_exchange_kernel, axis, n, gather),
+        out_shape=jax.ShapeDtypeStruct(out_shape, x.dtype),
+        in_specs=[pl.BlockSpec(memory_space=pltpu.VMEM)],
+        out_specs=pl.BlockSpec(memory_space=pltpu.VMEM),
+        scratch_shapes=[
+            pltpu.SemaphoreType.DMA((n,)),
+            pltpu.SemaphoreType.DMA((n,)),
+            pltpu.SemaphoreType.DMA(()),
+        ],
+        compiler_params=pltpu.CompilerParams(collective_id=cid, has_side_effects=True),
+    )(x)
 
 
 def merged_2(array, axis, combine):
@@ -90,7 +141,7 @@
     looked = jnp.take(token_embedding_table, jnp.clip(local_ids, 0, vocab_rows - 1), axis=0).astype(
         jnp.float32
     )
-    looked = jnp.where(present[:, None], looked, 0.0)
+    looked = jnp.where(present[:, None], looked, 0.0).astype(jnp.bfloat16)
     everywhere = lax.psum(looked, ("seq", "req"))
     embedded = lax.dynamic_slice_in_dim(everywhere, req_index * group_rows, group_rows, 0)
     joined = jnp.concatenate([hidden, embedded.astype(jnp.bfloat16)], axis=1)
@@ -160,17 +211,40 @@
     def own_slice(member):
         return lax.dynamic_slice_in_dim(member, first_head, own_heads, 2)
 
-    fresh_part = (own_slice(fresh_max), own_slice(fresh_sum), own_slice(fresh_out))
-    merged = merged_2((local_max, local_sum, local_out), "seq", softmax_join)
-    combined = softmax_join(tuple((own_slice(member) for member in merged)), fresh_part)
+    pad_cols = 256 - HD - 2
+    packed = jnp.concatenate(
+        [
+            local_out,
+            local_max[..., None],
+            local_sum[..., None],
+            jnp.zeros(local_out.shape[:-1] + (pad_cols,), jnp.float32),
+        ],
+        axis=-1,
+    )
+    packed = packed.reshape(requests * steps_each, seq_devices, own_heads, 256)
+    packed = jnp.transpose(packed, (1, 0, 2, 3)).reshape(seq_devices, group_rows * own_heads, 256)
+    arrived = exchange(packed, "seq", 0).reshape(seq_devices, requests, steps_each, own_heads, 256)
+    part_o = arrived[..., :HD]
+    part_m = arrived[..., HD]
+    part_l = arrived[..., HD + 1]
+    f_max, f_sum, f_out = own_slice(fresh_max), own_slice(fresh_sum), own_slice(fresh_out)
+    overall = jnp.maximum(jnp.max(part_m, axis=0), f_max)
+    part_factor = jnp.exp(part_m - overall[None])
+    fresh_factor = jnp.exp(f_max - overall)
+    denominator = jnp.sum(part_l * part_factor, axis=0) + f_sum * fresh_factor
+    numerator = jnp.sum(part_o * part_factor[..., None], axis=0) + f_out * fresh_factor[..., None]
     attention = (
-        (combined[2] / combined[1][..., None])
+        (numerator / denominator[..., None])
         .astype(jnp.bfloat16)
         .reshape(group_rows, own_heads * HD)
     )
     projected_out = jnp.dot(attention, attention_output_weight, preferred_element_type=jnp.float32)
-    mixed_sum = lax.psum(projected_out, "seq")
-    after_attn = (joined.astype(jnp.float32) + mixed_sum).astype(jnp.bfloat16)
+    model_width = projected_out.shape[1]
+    row_share = group_rows // seq_devices
+    out_parts = exchange(projected_out.reshape(seq_devices, row_share, model_width), "seq", 1)
+    own_rows = lax.dynamic_slice_in_dim(joined, seq_index * row_share, row_share, 0)
+    after_rows = (own_rows.astype(jnp.float32) + jnp.sum(out_parts, axis=0)).astype(jnp.bfloat16)
+    after_attn = exchange(after_rows, "seq", 2, gather=True).reshape(group_rows, model_width)
     second_normed_state = rms_norm(after_attn, feedforward_norm_gain)
     residual_cols, second_spread_state = (
         lax.all_to_all(after_attn, "req", split_axis=1, concat_axis=0, tiled=True),
@@ -194,12 +268,9 @@
     inner_act = (jax.nn.silu(gate_preactivation) * up_projection_part).astype(jnp.bfloat16)
     out_rows = residual_cols.shape[0] // seq_devices
     block_rows = inner_act
-    down_sum = lax.psum_scatter(
-        jnp.dot(block_rows, down_weight, preferred_element_type=jnp.float32),
-        "seq",
-        scatter_dimension=0,
-        tiled=True,
-    )
+    down_full = jnp.dot(block_rows, down_weight, preferred_element_type=jnp.float32)
+    down_parts = exchange(down_full.reshape(seq_devices, out_rows, down_full.shape[1]), "seq", 3)
+    down_sum = jnp.sum(down_parts, axis=0)
     residual_rows = lax.dynamic_slice_in_dim(residual_cols, seq_index * out_rows, out_rows, 0)
     return (residual_rows.astype(jnp.float32) + down_sum).astype(jnp.bfloat16)
 

time: 532 us -> 423 us (0.80)
  blocking collectives: 162 us -> 59.1 us
  Pallas kernels: 0 us -> 41.3 us
  waiting for transfers between devices: 209 us -> 180 us
  local copies, waits for them, and re-layouts: 66.7 us -> 56.2 us
  other arithmetic: 40.1 us -> 30.8 us
    psum x1 -> x0, blocking collectives: 75.4 us -> none  [body(): everywhere = lax.psum(looked, ('seq', 'req'))]
    unnamed x6 -> x3, waiting for transfers between devices: 71.8 us -> 0.05 us
    psum x1, waiting for transfers between devices: 87.6 us -> 146 us  [body(): everywhere = lax.psum(looked, ('seq', 'req'))]
    pallas_call x0 -> x4, Pallas kernels: none -> 41.3 us  [exchange(): pl.pallas_call(functools.partial(_exchange_kernel, axis, n, gather), out_...]
    all_gather x2 -> x0, blocking collectives: 34.2 us -> none  [merged_2(): everything = jax.tree.map(lambda part: lax.all_gather(part, axis), array)]
    add x31 -> x1, other arithmetic: 15.4 us -> 0.7 us  [body(): denominator = jnp.sum(part_l * part_factor, axis=0) + f_sum * fresh_factor]
    dynamic_slice x15 -> x1, local copies, waits for them, and re-layouts: 14.7 us -> 0.91 us  [body(): lax.dynamic_slice_in_dim(everywhere, req_index * group_rows, group_rows, 0)]
    all_gather x1 -> x0, waiting for transfers between devices: 10.1 us -> none  [merged_2(): everything = jax.tree.map(lambda part: lax.all_gather(part, axis), array)]
  transfers between devices with their start and end apart: 7 -> 5, of which waited for: 5 -> 3; matrix products, arithmetic and copies ran while one was open for 10% -> 11% of each run, Pallas kernels for 0% -> 3%
where the time goes in v1:
time: 423 us; the launch traced here: 418 us
  waiting for transfers between devices  180 us (43%)
  blocking collectives  59.1 us (14%)
  local copies, waits for them, and re-layouts  56.2 us (13%)
  Pallas kernels  41.3 us (10%)
  other arithmetic  30.8 us (7%)
  matrix products  28.3 us (7%)
  between operations  13.4 us (3%)
  starting transfers between devices  9.3 us (2%)
    psum x1, waiting for transfers between devices, body(): everywhere = lax.psum(looked, ('seq', 'req'))  146 us
    pallas_call x4, Pallas kernels, exchange(): pl.pallas_call(functools.partial(_exchange_kernel, axis, n, gather), out_...  41.3 us
    psum x1, waiting for transfers between devices, body(): lax.psum((jnp.dot(second_spread_state, gate_weight, preferred_element_typ...  28.2 us
    psum x1, blocking collectives, body(): lax.psum((jnp.dot(second_spread_state, gate_weight, preferred_element_typ...  23.4 us
    all_to_all x1, blocking collectives, body(): lax.all_to_all(second_normed_state, 'req', split_axis=1, concat_axis=0, t...  18.5 us
    all_gather x1, blocking collectives, body(): lax.all_gather(qkv_part.astype(jnp.bfloat16), 'seq', axis=1, tiled=True)  17.2 us
    reshape x1, local copies, waits for them, and re-layouts, body(): cache_v = cached_value_pages.reshape(slots * page_len, HEADS, HD)  13.1 us
    reshape x1, local copies, waits for them, and re-layouts, body(): cache_k = rotated_key_cache.reshape(slots * page_len, HEADS, HD)  13.1 us
  transfers between devices with their start and end apart: 5, of which 3 were waited for; matrix products, arithmetic and copies ran while one was open for 11% of the time, Pallas kernels for 3%

profile of v1, /device:TPU:1, one launch (start us, length us, event | category | flops | bytes accessed | tf_op | source)
XLA Modules:
  0.0 418.0 jit_solution(4329988674732986204)
XLA Ops:
  6.5 0.8 compare_and_fusion.1
  7.4 4.9 %gather_fusion = bf16[128,3584]{1,0:T(8,128)(2,1)} fusion(bf16[250,3584]{1,0:T(8,128)(2,1)} %param.19, s32[1024]{0:T(1024)S(1)} %pad_clamp_fusion), kind=kCustom, calls=%fused_computation | custom fusion | bytes 1835520 | tf_op jit(solution)/shard_map/jit(_take)/gather | solution.py:141
  12.3 2.5 select_convert_fusion
  18.6 146.4 %all-reduce.4.cloned.1.call-done = bf16[128,3584]{1,0:T(8,128)(2,1)} async-done(((bf16[128,3584]{1,0:T(8,128)(2,1)}), bf16[128,3584]{1,0:T(8,128)(2,1)}) %all-reduce.4.cloned.1.call-update) | async-done | bytes 917520 | tf_op jit(solution)/shard_map/psum | solution.py:145
  165.1 0.9 constant_dynamic-slice_fusion.2
  166.0 0.7 concatenate.30
  166.9 1.1 multiply_convert_fusion.1
  167.9 0.7 copy.116
  168.6 4.4 %all-to-all-start = ((bf16[16,8,896]{2,0,1:T(8,128)(2,1)}), bf16[16,8,896]{2,0,1:T(8,128)(2,1)S(1)}, u32[]{:S(2)}, u32[]{:S(2)}) async-start(bf16[16,8,896]{2,0,1:T(8,128)(2,1)} %copy.116), calls=%async_computation | async-start | bytes 458752 | tf_op jit(solution)/shard_map/all_to_all | solution.py:149
  173.0 1.3 add_convert_fusion.4
  174.3 4.9 %all-to-all-done = bf16[16,8,896]{2,0,1:T(8,128)(2,1)S(1)} async-done(((bf16[16,8,896]{2,0,1:T(8,128)(2,1)}), bf16[16,8,896]{2,0,1:T(8,128)(2,1)S(1)}, u32[]{:S(2)}, u32[]{:S(2)}) %all-to-all-start) | async-done | bytes 229408 | tf_op jit(solution)/shard_map/all_to_all | solution.py:149
  179.2 2.6 fusion.56
  182.3 0.8 copy.115
  183.1 13.1 %reshape.253 = bf16[768,16,224]{2,1,0:T(8,128)(2,1)} reshape(bf16[6,1,128,3584]{3,2,1,0:T(8,128)(2,1)} %param.22) | data formatting | bytes 11010048 | tf_op jit(solution)/shard_map/reshape | solution.py:167
  196.3 13.1 %reshape.254 = bf16[768,16,224]{2,1,0:T(8,128)(2,1)} reshape(bf16[6,1,128,3584]{3,2,1,0:T(8,128)(2,1)} %param.23) | data formatting | bytes 11010048 | tf_op jit(solution)/shard_map/reshape | solution.py:168
  210.8 0.7 multiply_cosine_fusion
  212.3 0.8 convert_bitcast_fusion
  213.1 17.2 %all-gather = bf16[16,672,16]{1,2,0:T(8,128)(2,1)S(1)} all-gather(bf16[1,672,16]{1,2,0:T(8,128)(2,1)S(1)} %convert_bitcast_fusion), channel_id=1, replica_groups=mesh['seq'=16,'req'=8] {'seq'}, dimensions={0}, use_global_device_ids=true | all-gather | bytes 365568 | tf_op jit(solution)/shard_map/all_gather | solution.py:157
  230.3 0.9 copy.117
  231.1 1.5 reshape.275
  232.7 0.9 fusion.52
  233.5 1.1 reshape.263
  234.7 0.8 fusion.54
  235.5 1.1 reshape.262
  236.7 1.8 subtract_convert_fusion
  238.5 7.6 %select_reduce_fusion = (f32[4,4,16]{1,0,2:T(4,128)S(1)}, f32[4,4,16,768]{3,1,0,2:T(4,128)}) fusion(pred[4,768]{1,0:T(4,128)(4,1)} %fusion.45, bf16[768,16,224,1]{2,1,0,3:T(8,128)(2,1)} %bitcast.121, bf16[4,4,16,112]{3,1,0,2:T(4,128)(2,1)S(1)} %get-tuple-element.27, bf16[4,4,16,112]{3,1,0,2:T(4,128)(2,1)S(1)} %get-tuple-element.28), kind=kOutput, calls=%fused_computation.15 | convolution fusion | flops 88899328 | bytes 6410240 | tf_op jit(solution)/shard_map/rthd,khd->rthk/dot_general | solution.py:183
  246.2 2.3 fusion.15
  248.5 7.6 %fusion.12 = f32[4,4,16,224]{3,1,0,2:T(4,128)} fusion(bf16[768,16,224,1]{2,1,0,3:T(8,128)(2,1)} %bitcast.120, f32[4,4,16,768]{3,1,0,2:T(4,128)} %get-tuple-element.33, f32[4,4,16]{1,0,2:T(4,128)S(1)} %get-tuple-element.32, pred[4,768]{1,0:T(4,128)(4,1)S(1)} %copy-done.17), kind=kOutput, calls=%fused_computation.13 | convolution fusion | flops 88670208 | bytes 6524928 | tf_op jit(solution)/shard_map/rthk,khd->rthd/dot_general | solution.py:190
  256.1 1.0 concatenate.33
  257.1 0.9 copy.123
  258.0 0.8 copy.125
  258.8 0.8 copy.124
  259.6 1.8 maximum_bitcast_fusion.x_ref
  261.4 9.2 %shard_map.163 = f32[16,16,256]{2,1,0:T(8,128)} custom-call(f32[16,16,256]{2,1,0:T(8,128)} %maximum_bitcast_fusion.x_ref), custom_call_target="tpu_custom_call" | custom-call | tf_op jit(solution)/shard_map/pallas_call | solution.py:54
  270.6 1.0 reshape.256
  271.7 1.5 fusion.53
  273.2 1.2 pad_maximum_fusion.1
  274.3 0.9 fusion.30
  275.2 1.1 copy.131
  276.7 1.1 copy.153
  277.8 1.1 copy.156
  278.8 0.7 max.7
  279.6 0.7 fusion.48
  281.0 1.1 reshape.257
  282.1 0.7 multiply_add_fusion
  283.7 1.1 reshape.259.x_ref
  284.7 10.3 %shard_map.164 = f32[16,1,7168]{2,1,0:T(1,128)} custom-call(f32[16,1,7168]{2,1,0:T(1,128)} %reshape.259.x_ref), custom_call_target="tpu_custom_call" | custom-call | tf_op jit(solution)/shard_map/pallas_call | solution.py:54
  295.0 1.3 reduce_sum.95
  297.0 10.0 %shard_map.165 = bf16[16,1,7168]{2,1,0:T(2,128)(2,1)} custom-call(bf16[1,7168]{1,0:T(2,128)(2,1)} %add_convert_fusion.3.x_ref), custom_call_target="tpu_custom_call" | custom-call | tf_op jit(solution)/shard_map/pallas_call | solution.py:54
  307.0 1.6 multiply_reduce_fusion
  308.7 2.3 reduce.6
  311.7 18.5 %all_to_all.51 = bf16[16,8,896]{2,0,1:T(8,128)(2,1)S(1)} all-to-all(bf16[16,8,896]{2,0,1:T(8,128)(2,1)S(1)} %copy.142), channel_id=1, replica_groups=mesh['seq'=16,'req'=8] {'req'}, dimensions={1} | all-to-all | bytes 458752 | tf_op jit(solution)/shard_map/all_to_all | solution.py:251
  330.2 1.3 fusion.58
  331.5 1.2 fusion.60
  332.7 1.7 copy.195
  334.4 4.9 %all-to-all-start.1 = ((bf16[16,8,896]{2,0,1:T(8,128)(2,1)}), bf16[16,8,896]{2,0,1:T(8,128)(2,1)}, u32[]{:S(2)}, u32[]{:S(2)}) async-start(bf16[16,8,896]{2,0,1:T(8,128)(2,1)} %bitcast.129), calls=%async_computation.2 | async-start | bytes 458752 | tf_op jit(solution)/shard_map/all_to_all | solution.py:250
  339.3 1.2 fusion.59
  340.4 23.4 %psum.30 = bf16[128,128]{1,0:T(8,128)(2,1)S(1)} all-reduce(f32[128,128]{1,0:T(8,128)S(1)} %fusion.59), channel_id=1, replica_groups=mesh['seq'=16,'req'=8] {'req'}, use_global_device_ids=true, to_apply=%region_15.16 | all-reduce | flops 16384 | bytes 98304 | tf_op jit(solution)/shard_map/psum | solution.py:253
  363.8 28.2 %all-reduce.6.cloned.1.call-done = (f32[128,896]{1,0:T(8,128)}, f32[128,896]{1,0:T(8,128)}) async-done(((f32[128,896]{1,0:T(8,128)}, f32[128,896]{1,0:T(8,128)}), (f32[128,896]{1,0:T(8,128)}, f32[128,896]{1,0:T(8,128)})) %all-reduce.6.cloned.1.call-update) | async-done | bytes 917520 | tf_op jit(solution)/shard_map/psum | solution.py:253
  392.0 2.1 convolution_add_fusion.1
  394.1 3.2 convolution_bitcast_fusion.x_ref
  397.3 11.8 %shard_map.166 = f32[16,8,896]{2,1,0:T(8,128)} custom-call(f32[16,8,896]{2,1,0:T(8,128)} %convolution_bitcast_fusion.x_ref), custom_call_target="tpu_custom_call" | custom-call | tf_op jit(solution)/shard_map/pallas_call | solution.py:54
  409.1 1.1 reduce_sum.98
  410.2 1.3 add_convert_fusion.2
  (98 shorter events, 10.2 us)
Async XLA Ops:
  6.5 276.6 %copy-start = (bf16[224,7168]{1,0:T(8,128)(2,1)S(1)}, bf16[224,7168]{1,0:T(8,128)(2,1)}, u32[]{:S(2)}) copy-start(bf16[224,7168]{1,0:T(8,128)(2,1)} %param.26) | copy-start | bytes 9633796
  6.5 158.5 %all-reduce.4.cloned.1.call-start = ((), (), s32[]{:S(2)}) async-start(), calls=%async_computation.4 | async-start | bytes 1835008 | tf_op jit(solution)/shard_map/psum | solution.py:145
  12.2 2.6 copy-start.20
  12.2 2.7 copy-start.19
  12.3 4.3 %copy-start.6 = (bf16[16,3584]{1,0:T(8,128)(2,1)S(1)}, bf16[16,3584]{1,0:T(8,128)(2,1)}, u32[]{:S(2)}) copy-start(bf16[16,3584]{1,0:T(8,128)(2,1)} %param.18) | copy-start | bytes 344068
  12.3 4.4 %copy-start.15 = (bf16[7168]{0:T(1024)(128)(2,1)S(1)}, bf16[7168]{0:T(1024)(128)(2,1)}, u32[]{:S(2)}) copy-start(bf16[7168]{0:T(1024)(128)(2,1)} %param.20) | copy-start | bytes 43012
  166.0 15.8 %copy-start.2 = (bf16[16,3584]{1,0:T(8,128)(2,1)}, bf16[16,3584]{1,0:T(8,128)(2,1)S(1)}, u32[]{:S(2)}) copy-start(bf16[16,3584]{1,0:T(8,128)(2,1)S(1)} %constant_dynamic-slice_fusion.2) | copy-start | bytes 344068
  168.6 10.6 %all-to-all-start = ((bf16[16,8,896]{2,0,1:T(8,128)(2,1)}), bf16[16,8,896]{2,0,1:T(8,128)(2,1)S(1)}, u32[]{:S(2)}, u32[]{:S(2)}) async-start(bf16[16,8,896]{2,0,1:T(8,128)(2,1)} %copy.116), calls=%async_computation | async-start | bytes 458752 | tf_op jit(solution)/shard_map/all_to_all | solution.py:149
  173.0 39.3 %reduce-scatter.2.cloned.1.call-start = ((), (), s32[]{:S(2)}) async-start(), calls=%async_computation.5 | async-start | bytes 442368 | tf_op jit(solution)/shard_map/reduce_scatter | solution.py:151
  181.8 210.2 %all-reduce.6.cloned.1.call-start = ((), (), s32[]{:S(2)}) async-start(), calls=%async_computation.6 | async-start | bytes 1835008 | tf_op jit(solution)/shard_map/psum | solution.py:253
  196.3 13.2 %copy-start.16 = (bf16[7168]{0:T(1024)(128)(2,1)S(1)}, bf16[7168]{0:T(1024)(128)(2,1)}, u32[]{:S(2)}) copy-start(bf16[7168]{0:T(1024)(128)(2,1)} %param.27) | copy-start | bytes 43012
  196.3 14.6 %copy-start.18 = (f32[4,4]{1,0:T(4,128)S(1)}, f32[4,4]{1,0:T(4,128)}, u32[]{:S(2)}) copy-start(f32[4,4]{1,0:T(4,128)} %add_convert_fusion.4) | copy-start | bytes 196
  196.3 14.6 %copy-start.23 = (f32[112]{0:T(128)S(1)}, f32[112]{0:T(128)}, u32[]{:S(2)}) copy-start(f32[112]{0:T(128)} %multiply_power_fusion) | copy-start | bytes 1348
  196.3 15.3 %copy-start.13 = (s32[768]{0:T(1024)S(1)}, s32[768]{0:T(1024)}, u32[]{:S(2)}) copy-start(s32[768]{0:T(1024)} %iota_bitcast_fusion) | copy-start | bytes 9220
  196.3 15.3 %copy-start.14 = (pred[1,4,6,128]{3,2,1,0:T(8,128)(4,1)S(1)}, pred[1,4,6,128]{3,2,1,0:T(8,128)(4,1)}, u32[]{:S(2)}) copy-start(pred[1,4,6,128]{3,2,1,0:T(8,128)(4,1)} %broadcast_bitcast_fusion.1) | copy-start | bytes 9220
  196.3 15.3 %copy-start.21 = (s32[4]{0:T(128)S(1)}, s32[4]{0:T(128)}, u32[]{:S(2)}) copy-start(s32[4]{0:T(128)} %param.24) | copy-start | bytes 52
  233.5 3.1 copy-start.11
  233.5 3.1 copy-start.12
  238.5 7.6 %copy-start.8 = (bf16[4,4,16,112]{3,1,0,2:T(4,128)(2,1)}, bf16[4,4,16,112]{3,1,0,2:T(4,128)(2,1)S(1)}, u32[]{:S(2)}) copy-start(bf16[4,4,16,112]{3,1,0,2:T(4,128)(2,1)S(1)} %get-tuple-element.27) | copy-start | bytes 172036
  238.5 7.6 %copy-start.9 = (bf16[4,4,16,112]{3,1,0,2:T(4,128)(2,1)}, bf16[4,4,16,112]{3,1,0,2:T(4,128)(2,1)S(1)}, u32[]{:S(2)}) copy-start(bf16[4,4,16,112]{3,1,0,2:T(4,128)(2,1)S(1)} %get-tuple-element.28) | copy-start | bytes 172036
  238.5 7.7 %copy-start.17 = (pred[4,768]{1,0:T(4,128)(4,1)S(1)}, pred[4,768]{1,0:T(4,128)(4,1)}, u32[]{:S(2)}) copy-start(pred[4,768]{1,0:T(4,128)(4,1)} %fusion.45) | copy-start | bytes 9220
  259.6 16.7 %copy-start.22 = (pred[4,4]{1,0:T(4,128)(4,1)S(1)}, pred[4,4]{1,0:T(4,128)(4,1)}, u32[]{:S(2)}) copy-start(pred[4,4]{1,0:T(4,128)(4,1)} %iota_compare_fusion) | copy-start | bytes 52
  283.6 12.7 %copy-start.3 = (bf16[16,3584]{1,0:T(8,128)(2,1)S(1)}, bf16[16,3584]{1,0:T(8,128)(2,1)}, u32[]{:S(2)}) copy-start(bf16[16,3584]{1,0:T(8,128)(2,1)} %copy-done.2) | copy-start | bytes 344068
  283.7 12.7 %copy-start.7 = (bf16[16,3584]{1,0:T(8,128)(2,1)S(1)}, bf16[16,3584]{1,0:T(8,128)(2,1)}, u32[]{:S(2)}) copy-start(bf16[16,3584]{1,0:T(8,128)(2,1)} %param.18) | copy-start | bytes 344068
  284.7 26.3 %copy-start.10 = (f32[8,896]{1,0:T(8,128)S(1)}, f32[8,896]{1,0:T(8,128)}, u32[]{:S(2)}) copy-start(f32[8,896]{1,0:T(8,128)} %reshape.264) | copy-start | bytes 86020
  310.9 0.7 copy-start.1
  311.0 19.2 %copy-start.4 = (bf16[896,896]{1,0:T(8,128)(2,1)S(1)}, bf16[896,896]{1,0:T(8,128)(2,1)}, u32[]{:S(2)}) copy-start(bf16[896,896]{1,0:T(8,128)(2,1)} %param.28) | copy-start | bytes 4816900
  311.0 20.4 %copy-start.5 = (bf16[896,896]{1,0:T(8,128)(2,1)S(1)}, bf16[896,896]{1,0:T(8,128)(2,1)}, u32[]{:S(2)}) copy-start(bf16[896,896]{1,0:T(8,128)(2,1)} %param.29) | copy-start | bytes 4816900
  334.4 75.8 %all-to-all-start.1 = ((bf16[16,8,896]{2,0,1:T(8,128)(2,1)}), bf16[16,8,896]{2,0,1:T(8,128)(2,1)}, u32[]{:S(2)}, u32[]{:S(2)}) async-start(bf16[16,8,896]{2,0,1:T(8,128)(2,1)} %bitcast.129), calls=%async_computation.2 | async-start | bytes 458752 | tf_op jit(solution)/shard_map/all_to_all | solution.py:250
Sparse Core Ops, SparseCore 0:
  14.9 150.0 all-reduce.3
  181.9 25.3 reduce-scatter.1
  332.9 59.1 all-reduce.5

commit v2 on v1

--- a/solution.py
+++ b/solution.py
@@ -141,20 +141,19 @@
     looked = jnp.take(token_embedding_table, jnp.clip(local_ids, 0, vocab_rows - 1), axis=0).astype(
         jnp.float32
     )
-    looked = jnp.where(present[:, None], looked, 0.0).astype(jnp.bfloat16)
+    looked = jnp.where(present[:, None], looked, 0.0)
     everywhere = lax.psum(looked, ("seq", "req"))
     embedded = lax.dynamic_slice_in_dim(everywhere, req_index * group_rows, group_rows, 0)
     joined = jnp.concatenate([hidden, embedded.astype(jnp.bfloat16)], axis=1)
     normed = rms_norm(joined, attention_norm_gain)
-    spread = lax.all_to_all(normed, "req", split_axis=1, concat_axis=0, tiled=True)
-    block_rows = spread
-    qkv_part = lax.psum_scatter(
-        jnp.dot(block_rows, query_key_value_weight, preferred_element_type=jnp.float32),
-        "req",
-        scatter_dimension=0,
-        tiled=True,
-    )
-    projected = lax.all_gather(qkv_part.astype(jnp.bfloat16), "seq", axis=1, tiled=True)
+    width_share = normed.shape[1] // req_devices
+    to_owners = jnp.transpose(normed.reshape(group_rows, req_devices, width_share), (1, 0, 2))
+    block_rows = exchange(to_owners, "req", 4).reshape(req_devices * group_rows, width_share)
+    qkv_full = jnp.dot(block_rows, query_key_value_weight, preferred_element_type=jnp.float32)
+    qkv_parts = exchange(qkv_full.reshape(req_devices, group_rows, qkv_full.shape[1]), "req", 5)
+    qkv_part = jnp.sum(qkv_parts, axis=0).astype(jnp.bfloat16)
+    qkv_all = exchange(qkv_part, "seq", 6, gather=True)
+    projected = jnp.transpose(qkv_all, (1, 0, 2)).reshape(group_rows, seq_devices * qkv_part.shape[1])
     head_cols = HEADS * HD
     queries = projected[:, :head_cols].reshape(requests, steps_each, HEADS, HD)
     new_keys = projected[:, head_cols : 2 * head_cols].reshape(requests, steps_each, HEADS, HD)
@@ -246,18 +245,24 @@
     after_rows = (own_rows.astype(jnp.float32) + jnp.sum(out_parts, axis=0)).astype(jnp.bfloat16)
     after_attn = exchange(after_rows, "seq", 2, gather=True).reshape(group_rows, model_width)
     second_normed_state = rms_norm(after_attn, feedforward_norm_gain)
-    residual_cols, second_spread_state = (
-        lax.all_to_all(after_attn, "req", split_axis=1, concat_axis=0, tiled=True),
-        lax.all_to_all(second_normed_state, "req", split_axis=1, concat_axis=0, tiled=True),
-    )
-    gate_total, up_total, low_sum = lax.psum(
-        (
+    both = jnp.stack([after_attn, second_normed_state]).reshape(2, group_rows, req_devices, width_share)
+    both_parts = exchange(jnp.transpose(both, (2, 0, 1, 3)), "req", 7)
+    residual_cols = both_parts[:, 0].reshape(req_devices * group_rows, width_share)
+    second_spread_state = both_parts[:, 1].reshape(req_devices * group_rows, width_share)
+    units = gate_weight.shape[1]
+    mlp_full = jnp.concatenate(
+        [
             jnp.dot(second_spread_state, gate_weight, preferred_element_type=jnp.float32),
             jnp.dot(second_spread_state, up_weight, preferred_element_type=jnp.float32),
             jnp.dot(second_spread_state, adapter_down_map, preferred_element_type=jnp.float32),
-        ),
-        "req",
-    )
+        ],
+        axis=1,
+    )
+    mlp_parts = exchange(mlp_full.reshape(req_devices, group_rows, mlp_full.shape[1]), "req", 8)
+    mlp_sum = jnp.sum(mlp_parts, axis=0)
+    gate_total = mlp_sum[:, :units]
+    up_total = mlp_sum[:, units : 2 * units]
+    low_sum = mlp_sum[:, 2 * units :]
     adapter_hidden = low_sum.astype(jnp.bfloat16)
     gate_preactivation = gate_total + jnp.dot(
         adapter_hidden, adapter_gate_map, preferred_element_type=jnp.float32
@@ -265,7 +270,8 @@
     up_projection_part = up_total + jnp.dot(
         adapter_hidden, adapter_up_map, preferred_element_type=jnp.float32
     )
-    inner_act = (jax.nn.silu(gate_preactivation) * up_projection_part).astype(jnp.bfloat16)
+    group_act = (jax.nn.silu(gate_preactivation) * up_projection_part).astype(jnp.bfloat16)
+    inner_act = exchange(group_act, "req", 9, gather=True).reshape(req_devices * group_rows, units)
     out_rows = residual_cols.shape[0] // seq_devices
     block_rows = inner_act
     down_full = jnp.dot(block_rows, down_weight, preferred_element_type=jnp.float32)

time: 423 us -> 301 us (0.71)
  waiting for transfers between devices: 180 us -> 0 us
  Pallas kernels: 41.3 us -> 113 us
  blocking collectives: 59.1 us -> 75.6 us
  between operations: 13.4 us -> 0.35 us
  starting transfers between devices: 9.3 us -> 0 us
    psum x2 -> x0, waiting for transfers between devices: 175 us -> none  [the longest x1 146 us: body(): everywhere = lax.psum(looked, ('seq', 'req'))]
    pallas_call x4 -> x10, Pallas kernels: 41.3 us -> 113 us  [exchange(): pl.pallas_call(functools.partial(_exchange_kernel, axis, n, gather), out_...]
    psum x1, blocking collectives: 23.4 us -> 75.6 us  [body(): everywhere = lax.psum(looked, ('seq', 'req'))]
    all_to_all x1 -> x0, blocking collectives: 18.5 us -> none  [body(): lax.all_to_all(second_normed_state, 'req', split_axis=1, concat_axis=0, t...]
    all_gather x1 -> x0, blocking collectives: 17.2 us -> none  [body(): lax.all_gather(qkv_part.astype(jnp.bfloat16), 'seq', axis=1, tiled=True)]
    all_to_all x2 -> x0, starting transfers between devices: 9.25 us -> none  [the longest x1 4.89 us: body(): lax.all_to_all(after_attn, 'req', split_axis=1, concat_axis=0, tiled=True)]
    all_to_all x2 -> x0, waiting for transfers between devices: 4.89 us -> none  [the longest x1 4.89 us: body(): lax.all_to_all(normed, 'req', split_axis=1, concat_axis=0, tiled=True)]
  transfers between devices with their start and end apart: 5 -> 0, of which waited for: 3 -> 0; matrix products, arithmetic and copies ran while one was open for 11% -> 0% of each run, Pallas kernels for 3% -> 0%
where the time goes in v2:
time: 301 us; the launch traced here: 299 us
  Pallas kernels  113 us (38%)
  blocking collectives  75.6 us (25%)
  local copies, waits for them, and re-layouts  52.6 us (17%)
  matrix products  28.6 us (10%)
  other arithmetic  28.2 us (9%)
    pallas_call x10, Pallas kernels, exchange(): pl.pallas_call(functools.partial(_exchange_kernel, axis, n, gather), out_...  113 us
    psum x1, blocking collectives, body(): everywhere = lax.psum(looked, ('seq', 'req'))  75.6 us
    reshape x1, local copies, waits for them, and re-layouts, body(): cache_k = rotated_key_cache.reshape(slots * page_len, HEADS, HD)  13.1 us
    reshape x1, local copies, waits for them, and re-layouts, body(): cache_v = cached_value_pages.reshape(slots * page_len, HEADS, HD)  13.1 us
    dot_general x1, matrix products, body(): jnp.einsum('rthk,khd->rthd', weights.astype(jnp.bfloat16), cache_v, prefe...  7.61 us
    dot_general x1, matrix products, body(): jnp.einsum('rthd,khd->rthk', queries, cache_k, preferred_element_type=jnp...  7.5 us

profile of v2, /device:TPU:1, one launch (start us, length us, event | category | flops | bytes accessed | tf_op | source)
XLA Modules:
  0.0 298.6 jit_solution(10362320281373019499)
XLA Ops:
  0.0 0.8 compare_and_fusion.1
  0.8 4.8 %gather_fusion = bf16[128,3584]{1,0:T(8,128)(2,1)} fusion(bf16[250,3584]{1,0:T(8,128)(2,1)} %param.19, s32[1024]{0:T(1024)S(1)} %pad_clamp_fusion), kind=kCustom, calls=%fused_computation | custom fusion | bytes 1835520 | tf_op jit(solution)/shard_map/jit(_take)/gather | solution.py:141
  5.7 2.8 convert_select_fusion
  8.4 75.6 %all-reduce.1 = bf16[128,3584]{1,0:T(8,128)(2,1)} all-reduce(f32[128,3584]{1,0:T(8,128)} %convert_select_fusion), channel_id=1, replica_groups=mesh['seq'=16,'req'=8] {'seq','req'}, use_global_device_ids=true, to_apply=%region_0.1 | all-reduce | flops 458752 | bytes 2752512 | tf_op jit(solution)/shard_map/psum | solution.py:145
  84.1 0.9 dynamic-slice_convert_fusion
  85.0 0.6 copy-done.1
  85.8 0.8 reshape.297
  86.6 0.8 fusion.26.x_ref
  87.4 8.7 %shard_map.163 = bf16[8,16,896]{2,1,0:T(8,128)(2,1)} custom-call(bf16[8,16,896]{2,1,0:T(8,128)(2,1)} %fusion.26.x_ref), custom_call_target="tpu_custom_call" | custom-call | tf_op jit(solution)/shard_map/pallas_call | solution.py:54
  96.1 2.7 fusion.12.x_ref
  98.8 10.3 %shard_map.164 = f32[8,16,672]{2,1,0:T(8,128)} custom-call(f32[8,16,672]{2,1,0:T(8,128)} %fusion.12.x_ref), custom_call_target="tpu_custom_call" | custom-call | tf_op jit(solution)/shard_map/pallas_call | solution.py:54
  109.1 1.6 reduce_sum.107.x_ref
  110.7 11.2 %shard_map.165 = bf16[16,16,672]{2,1,0:T(8,128)(2,1)} custom-call(bf16[16,672]{1,0:T(8,128)(2,1)} %reduce_sum.107.x_ref), custom_call_target="tpu_custom_call" | custom-call | tf_op jit(solution)/shard_map/pallas_call | solution.py:54
  122.0 1.9 copy.106
  123.8 1.5 reshape.288
  125.4 0.8 fusion.48
  126.2 1.1 reshape.299
  127.3 0.7 fusion.50
  128.1 1.1 reshape.298
  129.5 1.8 subtract_convert_fusion
  131.9 0.3 fusion.45
  132.4 13.1 %reshape.289 = bf16[768,16,224]{2,1,0:T(8,128)(2,1)} reshape(bf16[6,1,128,3584]{3,2,1,0:T(8,128)(2,1)} %param.22) | data formatting | bytes 11010048 | tf_op jit(solution)/shard_map/reshape | solution.py:166
  145.6 7.5 %select_reduce_fusion = (f32[4,4,16]{1,0,2:T(4,128)S(1)}, f32[4,4,16,768]{3,1,0,2:T(4,128)}) fusion(pred[4,768]{1,0:T(4,128)(4,1)S(1)} %fusion.41, bf16[768,16,224,1]{2,1,0,3:T(8,128)(2,1)} %bitcast.116, bf16[4,4,16,112]{3,1,0,2:T(4,128)(2,1)S(1)} %get-tuple-element.27, bf16[4,4,16,112]{3,1,0,2:T(4,128)(2,1)S(1)} %get-tuple-element.28), kind=kOutput, calls=%fused_computation.19 | convolution fusion | flops 88899328 | bytes 6410240 | tf_op jit(solution)/shard_map/rthd,khd->rthk/dot_general | solution.py:182
  153.1 13.1 %reshape.290 = bf16[768,16,224]{2,1,0:T(8,128)(2,1)} reshape(bf16[6,1,128,3584]{3,2,1,0:T(8,128)(2,1)} %param.23) | data formatting | bytes 11010048 | tf_op jit(solution)/shard_map/reshape | solution.py:167
  166.2 7.6 %fusion.14 = f32[4,4,16,224]{3,1,0,2:T(4,128)} fusion(bf16[768,16,224,1]{2,1,0,3:T(8,128)(2,1)} %bitcast.117, f32[4,4,16,768]{3,1,0,2:T(4,128)} %get-tuple-element.33, f32[4,4,16]{1,0,2:T(4,128)S(1)} %get-tuple-element.32, pred[4,768]{1,0:T(4,128)(4,1)S(1)} %fusion.41), kind=kOutput, calls=%fused_computation.12 | convolution fusion | flops 88670208 | bytes 6524928 | tf_op jit(solution)/shard_map/rthk,khd->rthd/dot_general | solution.py:189
  173.8 1.0 concatenate.37
  174.8 1.7 fusion.19
  176.6 0.8 copy.114
  177.5 0.8 copy.113
  178.4 1.8 maximum_bitcast_fusion.1.x_ref
  180.2 9.5 %shard_map.166 = f32[16,16,256]{2,1,0:T(8,128)} custom-call(f32[16,16,256]{2,1,0:T(8,128)} %maximum_bitcast_fusion.1.x_ref), custom_call_target="tpu_custom_call" | custom-call | tf_op jit(solution)/shard_map/pallas_call | solution.py:54
  189.7 1.0 reshape.292
  190.7 0.9 fusion.49
  191.7 1.9 fusion.29
  193.6 1.1 copy.120
  194.9 1.1 copy.144
  196.0 1.1 copy.147
  197.1 0.7 fusion.44
  198.1 0.7 multiply_add_fusion
  199.4 1.1 reshape.293
  200.8 0.5 fusion.52
  201.3 1.1 reshape.295.x_ref
  202.4 10.2 %shard_map.167 = f32[16,1,7168]{2,1,0:T(1,128)} custom-call(f32[16,1,7168]{2,1,0:T(1,128)} %reshape.295.x_ref), custom_call_target="tpu_custom_call" | custom-call | tf_op jit(solution)/shard_map/pallas_call | solution.py:54
  212.6 1.3 reduce_sum.114
  214.0 0.7 add_convert_fusion.3.x_ref
  214.6 10.4 %shard_map.168 = bf16[16,1,7168]{2,1,0:T(2,128)(2,1)} custom-call(bf16[1,7168]{1,0:T(2,128)(2,1)} %add_convert_fusion.3.x_ref), custom_call_target="tpu_custom_call" | custom-call | tf_op jit(solution)/shard_map/pallas_call | solution.py:54
  225.0 3.0 reduce.6
  228.0 1.0 copy.155
  229.0 1.6 multiply_reduce_fusion
  230.8 0.8 maximum_bitcast_fusion.x_ref
  231.6 15.2 %shard_map.169 = bf16[8,2,16,896]{3,2,1,0:T(8,128)(2,1)} custom-call(bf16[8,2,16,896]{3,2,1,0:T(8,128)(2,1)} %maximum_bitcast_fusion.x_ref), custom_call_target="tpu_custom_call" | custom-call | tf_op jit(solution)/shard_map/pallas_call | solution.py:54
  246.9 1.2 fusion.47
  248.1 1.9 fusion.53
  250.0 0.4 fusion.54
  250.7 1.0 pad_maximum_fusion
  251.8 16.8 %shard_map.170 = f32[8,16,1920]{2,1,0:T(8,128)} custom-call(f32[8,16,1920]{2,1,0:T(8,128)} %bitcast.118), custom_call_target="tpu_custom_call" | custom-call | tf_op jit(solution)/shard_map/pallas_call | solution.py:54
  268.6 1.9 reduce_sum.117
  270.5 1.1 convolution_add_fusion.1
  271.6 1.7 fusion.18.x_ref
  273.3 8.0 %shard_map.171 = bf16[8,16,896]{2,1,0:T(8,128)(2,1)} custom-call(bf16[16,896]{1,0:T(8,128)(2,1)} %fusion.18.x_ref), custom_call_target="tpu_custom_call" | custom-call | tf_op jit(solution)/shard_map/pallas_call | solution.py:54
  281.3 2.8 fusion.4.x_ref
  284.1 12.8 %shard_map.172 = f32[16,8,896]{2,1,0:T(8,128)} custom-call(f32[16,8,896]{2,1,0:T(8,128)} %fusion.4.x_ref), custom_call_target="tpu_custom_call" | custom-call | tf_op jit(solution)/shard_map/pallas_call | solution.py:54
  296.9 1.1 reduce_sum.118
  297.9 0.6 add_convert_fusion.2
  (68 shorter events, 3.5 us)
Async XLA Ops:
  0.0 200.8 %copy-start = (bf16[224,7168]{1,0:T(8,128)(2,1)S(1)}, bf16[224,7168]{1,0:T(8,128)(2,1)}, u32[]{:S(2)}) copy-start(bf16[224,7168]{1,0:T(8,128)(2,1)} %param.26) | copy-start | bytes 9633796
  8.4 76.5 %copy-start.4 = (bf16[16,3584]{1,0:T(8,128)(2,1)S(1)}, bf16[16,3584]{1,0:T(8,128)(2,1)}, u32[]{:S(2)}) copy-start(bf16[16,3584]{1,0:T(8,128)(2,1)} %param.18) | copy-start | bytes 344068
  85.0 0.6 copy-start.1
  126.2 3.1 %copy-start.12 = (s32[4]{0:T(128)S(1)}, s32[4]{0:T(128)}, u32[]{:S(2)}) copy-start(s32[4]{0:T(128)} %param.24) | copy-start | bytes 52
  126.2 5.3 %copy-start.11 = (s32[4,48]{1,0:T(4,128)S(1)}, s32[4,48]{1,0:T(4,128)}, u32[]{:S(2)}) copy-start(s32[4,48]{1,0:T(4,128)} %param.25) | copy-start | bytes 2308
  131.4 14.2 %copy-start.8 = (bf16[4,4,16,112]{3,1,0,2:T(4,128)(2,1)}, bf16[4,4,16,112]{3,1,0,2:T(4,128)(2,1)S(1)}, u32[]{:S(2)}) copy-start(bf16[4,4,16,112]{3,1,0,2:T(4,128)(2,1)S(1)} %get-tuple-element.27) | copy-start | bytes 172036
  131.4 14.2 %copy-start.9 = (bf16[4,4,16,112]{3,1,0,2:T(4,128)(2,1)}, bf16[4,4,16,112]{3,1,0,2:T(4,128)(2,1)S(1)}, u32[]{:S(2)}) copy-start(bf16[4,4,16,112]{3,1,0,2:T(4,128)(2,1)S(1)} %get-tuple-element.28) | copy-start | bytes 172036
  177.5 14.1 %copy-start.7 = (bf16[4,4,16,112]{3,1,0,2:T(4,128)(2,1)S(1)}, bf16[4,4,16,112]{3,1,0,2:T(4,128)(2,1)}, u32[]{:S(2)}) copy-start(bf16[4,4,16,112]{3,1,0,2:T(4,128)(2,1)} %get-tuple-element.14) | copy-start | bytes 172036
  201.3 12.6 %copy-start.2 = (bf16[16,3584]{1,0:T(8,128)(2,1)S(1)}, bf16[16,3584]{1,0:T(8,128)(2,1)}, u32[]{:S(2)}) copy-start(bf16[16,3584]{1,0:T(8,128)(2,1)} %copy-done.1) | copy-start | bytes 344068
  201.3 12.6 %copy-start.5 = (bf16[16,3584]{1,0:T(8,128)(2,1)S(1)}, bf16[16,3584]{1,0:T(8,128)(2,1)}, u32[]{:S(2)}) copy-start(bf16[16,3584]{1,0:T(8,128)(2,1)} %param.18) | copy-start | bytes 344068
  202.4 28.2 %copy-start.10 = (bf16[7168]{0:T(1024)(128)(2,1)S(1)}, bf16[7168]{0:T(1024)(128)(2,1)}, u32[]{:S(2)}) copy-start(bf16[7168]{0:T(1024)(128)(2,1)} %param.27) | copy-start | bytes 43012
  246.9 3.2 %copy-start.3 = (bf16[896,896]{1,0:T(8,128)(2,1)S(1)}, bf16[896,896]{1,0:T(8,128)(2,1)}, u32[]{:S(2)}) copy-start(bf16[896,896]{1,0:T(8,128)(2,1)} %param.29) | copy-start | bytes 4816900
  248.1 2.4 copy-start.6

commit v3 on v2

--- a/solution.py
+++ b/solution.py
@@ -141,9 +141,11 @@
     looked = jnp.take(token_embedding_table, jnp.clip(local_ids, 0, vocab_rows - 1), axis=0).astype(
         jnp.float32
     )
-    looked = jnp.where(present[:, None], looked, 0.0)
-    everywhere = lax.psum(looked, ("seq", "req"))
-    embedded = lax.dynamic_slice_in_dim(everywhere, req_index * group_rows, group_rows, 0)
+    looked = jnp.where(present[:, None], looked, 0.0).astype(jnp.bfloat16)
+    by_group = exchange(looked.reshape(req_devices, group_rows, looked.shape[1]), "req", 10)
+    column_part = jnp.sum(by_group.astype(jnp.float32), axis=0).astype(jnp.bfloat16)
+    from_columns = exchange(column_part, "seq", 11, gather=True)
+    embedded = jnp.sum(from_columns.astype(jnp.float32), axis=0)
     joined = jnp.concatenate([hidden, embedded.astype(jnp.bfloat16)], axis=1)
     normed = rms_norm(joined, attention_norm_gain)
     width_share = normed.shape[1] // req_devices
@@ -163,8 +165,8 @@
     new_keys = rotate(new_keys.astype(jnp.float32), positions).astype(jnp.bfloat16)
     slots = rotated_key_cache.shape[0]
     page_len = rotated_key_cache.shape[2]
-    cache_k = rotated_key_cache.reshape(slots * page_len, HEADS, HD)
-    cache_v = cached_value_pages.reshape(slots * page_len, HEADS, HD)
+    cache_k = rotated_key_cache.reshape(slots * page_len, head_cols)
+    cache_v = cached_value_pages.reshape(slots * page_len, head_cols)
     slot_ids = seq_index * slots + jnp.arange(slots, dtype=jnp.int32)
     page_ids = jnp.arange(request_page_slots.shape[1], dtype=jnp.int32)
     is_live = page_ids[None, :] < ((lengths + page_len - 1) // page_len)[:, None]
@@ -178,16 +180,30 @@
         requests, slots * page_len
     )
     score_scale = 1.0 / math.sqrt(HD)
+    head_mask = (jnp.arange(head_cols, dtype=jnp.int32)[None, :] // HD) == jnp.arange(
+        HEADS, dtype=jnp.int32
+    )[:, None]
+    query_rows = queries.reshape(group_rows, head_cols)
+    spread_queries = jnp.where(head_mask[None], query_rows[:, None, :], jnp.zeros((), jnp.bfloat16))
     scores = (
-        jnp.einsum("rthd,khd->rthk", queries, cache_k, preferred_element_type=jnp.float32)
+        jnp.dot(
+            spread_queries.reshape(group_rows * HEADS, head_cols),
+            cache_k.T,
+            preferred_element_type=jnp.float32,
+        )
         * score_scale
-    )
+    ).reshape(requests, steps_each, HEADS, slots * page_len)
     mask_b = is_valid[:, None, None, :]
     local_max = jnp.max(jnp.where(mask_b, scores, NEGATIVE), axis=-1)
     weights = jnp.where(mask_b, jnp.exp(scores - local_max[..., None]), 0.0)
     local_sum = jnp.sum(weights, axis=-1)
-    local_out = jnp.einsum(
-        "rthk,khd->rthd", weights.astype(jnp.bfloat16), cache_v, preferred_element_type=jnp.float32
+    spread_out = jnp.dot(
+        weights.astype(jnp.bfloat16).reshape(group_rows * HEADS, slots * page_len),
+        cache_v,
+        preferred_element_type=jnp.float32,
+    ).reshape(group_rows, HEADS, head_cols)
+    local_out = jnp.sum(jnp.where(head_mask[None], spread_out, 0.0), axis=1).reshape(
+        requests, steps_each, HEADS, HD
     )
     fresh_scores = (
         jnp.einsum("rthd,rshd->rths", queries, new_keys, preferred_element_type=jnp.float32)

time: 301 us -> 256 us (0.85)
  blocking collectives: 75.6 us -> 0 us
  Pallas kernels: 113 us -> 167 us
  local copies, waits for them, and re-layouts: 52.6 us -> 28.5 us
  other arithmetic: 28.2 us -> 37.2 us
  matrix products: 28.6 us -> 21 us
    psum x1 -> x0, blocking collectives: 75.6 us -> none  [body(): everywhere = lax.psum(looked, ('seq', 'req'))]
    pallas_call x10 -> x12, Pallas kernels: 113 us -> 167 us  [exchange(): pl.pallas_call(functools.partial(_exchange_kernel, axis, n, gather), out_...]
    reshape x2 -> x0, local copies, waits for them, and re-layouts: 26.3 us -> none  [the longest x1 13.1 us: body(): cache_k = rotated_key_cache.reshape(slots * page_len, HEADS, HD)]
    dot_general x2, matrix products: 15.1 us -> 6.04 us  [the longest x1 4.39 us: body(): jnp.dot(spread_queries.reshape(group_rows * HEADS, head_cols), cache_k.T,...]
where the time goes in v3:
time: 256 us; the launch traced here: 254 us
  Pallas kernels  167 us (65%)
  other arithmetic  37.2 us (15%)
  local copies, waits for them, and re-layouts  28.5 us (11%)
  matrix products  21 us (8%)
    pallas_call x12, Pallas kernels, exchange(): pl.pallas_call(functools.partial(_exchange_kernel, axis, n, gather), out_...  167 us

profile of v3, /device:TPU:1, one launch (start us, length us, event | category | flops | bytes accessed | tf_op | source)
XLA Modules:
  0.0 253.9 jit_solution(4319849050702989179)
XLA Ops:
  0.5 0.9 and_select_fusion
  2.2 0.9 fusion.34
  4.8 0.9 select_reduce_fusion
  6.0 0.7 multiply_cosine_fusion
  6.8 1.3 fusion.30
  8.1 0.8 reshape.388
  8.9 1.4 reshape.391
  10.9 4.7 %gather_fusion = bf16[128,3584]{1,0:T(8,128)(2,1)} fusion(bf16[250,3584]{1,0:T(8,128)(2,1)} %param.19, s32[1024]{0:T(1024)S(1)} %pad_clamp_fusion), kind=kCustom, calls=%fused_computation | custom fusion | bytes 1835520 | tf_op jit(solution)/shard_map/jit(_take)/gather | solution.py:141
  15.7 2.5 select_convert_fusion.x_ref
  18.1 18.4 %shard_map.163 = bf16[8,16,3584]{2,1,0:T(8,128)(2,1)} custom-call(bf16[8,16,3584]{2,1,0:T(8,128)(2,1)} %select_convert_fusion.x_ref), custom_call_target="tpu_custom_call" | custom-call | tf_op jit(solution)/shard_map/pallas_call | solution.py:54
  36.5 2.0 reduce_sum.138.x_ref
  38.5 35.7 %shard_map.164 = bf16[16,16,3584]{2,1,0:T(8,128)(2,1)} custom-call(bf16[16,3584]{1,0:T(8,128)(2,1)} %reduce_sum.138.x_ref), custom_call_target="tpu_custom_call" | custom-call | tf_op jit(solution)/shard_map/pallas_call | solution.py:54
  74.2 1.8 reduce_sum.139
  76.2 0.8 fusion.11.x_ref
  77.0 8.6 %shard_map.165 = bf16[8,16,896]{2,1,0:T(8,128)(2,1)} custom-call(bf16[8,16,896]{2,1,0:T(8,128)(2,1)} %fusion.11.x_ref), custom_call_target="tpu_custom_call" | custom-call | tf_op jit(solution)/shard_map/pallas_call | solution.py:54
  85.6 2.7 %fusion.3.x_ref = f32[8,16,672]{2,1,0:T(8,128)} fusion(bf16[8,16,896]{2,1,0:T(8,128)(2,1)} %shard_map.165, bf16[896,672]{0,1:T(8,128)(2,1)} %param.21), kind=kOutput, calls=%fused_computation.8 | convolution fusion | flops 154140672 | bytes 1777664 | tf_op jit(solution)/shard_map/dot_general | solution.py:154
  88.3 10.1 %shard_map.166 = f32[8,16,672]{2,1,0:T(8,128)} custom-call(f32[8,16,672]{2,1,0:T(8,128)} %fusion.3.x_ref), custom_call_target="tpu_custom_call" | custom-call | tf_op jit(solution)/shard_map/pallas_call | solution.py:54
  98.4 1.6 reduce_sum.142.x_ref
  100.0 10.8 %shard_map.167 = bf16[16,16,672]{2,1,0:T(8,128)(2,1)} custom-call(bf16[16,672]{1,0:T(8,128)(2,1)} %reduce_sum.142.x_ref), custom_call_target="tpu_custom_call" | custom-call | tf_op jit(solution)/shard_map/pallas_call | solution.py:54
  110.8 1.9 copy.91
  112.7 1.5 reshape.379
  114.2 0.8 fusion.37
  115.0 1.8 reshape.384
  116.8 1.1 reshape.390
  118.0 1.5 subtract_convert_fusion
  119.5 1.1 reshape.389
  121.0 1.8 fusion.12
  122.8 1.1 copy.101
  124.5 1.1 convert_element_type.120
  127.6 0.9 fusion.16
  128.5 1.2 broadcast_select_fusion
  129.7 4.4 %fusion.7 = (f32[256]{0:T(256)S(1)}, f32[256,768]{1,0:T(8,128)S(1)}) fusion(pred[4,768]{1,0:T(4,128)(4,1)S(1)} %copy-done.11, bf16[256,3584]{1,0:T(8,128)(2,1)S(1)} %bitcast.125, bf16[768,3584]{1,0:T(8,128)(2,1)} %bitcast.126), kind=kOutput, calls=%fused_computation.17 | convolution fusion | flops 1409875712 | bytes 8130560 | tf_op jit(solution)/shard_map/dot_general | solution.py:189
  134.5 1.7 fusion.2
  136.3 0.9 concatenate.36
  137.2 1.1 copy.95
  138.3 0.8 copy.97
  139.1 0.8 copy.96
  139.9 1.8 maximum_bitcast_fusion.1.x_ref
  141.7 9.7 %shard_map.168 = f32[16,16,256]{2,1,0:T(8,128)} custom-call(f32[16,16,256]{2,1,0:T(8,128)} %maximum_bitcast_fusion.1.x_ref), custom_call_target="tpu_custom_call" | custom-call | tf_op jit(solution)/shard_map/pallas_call | solution.py:54
  151.4 1.0 reshape.383
  152.5 0.9 fusion.38
  153.4 1.1 copy.122
  154.5 1.1 copy.119
  156.1 0.8 fusion.28
  157.4 1.1 reshape.386.x_ref
  158.5 10.8 %shard_map.169 = f32[16,1,7168]{2,1,0:T(1,128)} custom-call(f32[16,1,7168]{2,1,0:T(1,128)} %reshape.386.x_ref), custom_call_target="tpu_custom_call" | custom-call | tf_op jit(solution)/shard_map/pallas_call | solution.py:54
  169.3 1.3 reduce_sum.150
  171.3 10.1 %shard_map.170 = bf16[16,1,7168]{2,1,0:T(2,128)(2,1)} custom-call(bf16[1,7168]{1,0:T(2,128)(2,1)} %add_convert_fusion.2.x_ref), custom_call_target="tpu_custom_call" | custom-call | tf_op jit(solution)/shard_map/pallas_call | solution.py:54
  181.4 1.6 multiply_reduce_fusion
  183.0 2.3 reduce.10
  185.5 0.8 maximum_bitcast_fusion.x_ref
  186.4 15.0 %shard_map.171 = bf16[8,2,16,896]{3,2,1,0:T(8,128)(2,1)} custom-call(bf16[8,2,16,896]{3,2,1,0:T(8,128)(2,1)} %maximum_bitcast_fusion.x_ref), custom_call_target="tpu_custom_call" | custom-call | tf_op jit(solution)/shard_map/pallas_call | solution.py:54
  201.3 1.2 fusion.36
  202.6 1.2 fusion.44
  203.7 1.9 fusion.43
  206.1 1.1 pad_maximum_fusion
  207.1 16.8 %shard_map.172 = f32[8,16,1920]{2,1,0:T(8,128)} custom-call(f32[8,16,1920]{2,1,0:T(8,128)} %bitcast.127), custom_call_target="tpu_custom_call" | custom-call | tf_op jit(solution)/shard_map/pallas_call | solution.py:54
  223.9 1.9 reduce_sum.153
  225.8 1.1 convolution_add_fusion.1
  226.9 1.7 fusion.6.x_ref
  228.6 8.0 %shard_map.173 = bf16[8,16,896]{2,1,0:T(8,128)(2,1)} custom-call(bf16[16,896]{1,0:T(8,128)(2,1)} %fusion.6.x_ref), custom_call_target="tpu_custom_call" | custom-call | tf_op jit(solution)/shard_map/pallas_call | solution.py:54
  236.6 2.8 %fusion.x_ref = f32[16,8,896]{2,1,0:T(8,128)} fusion(bf16[16,8,896]{2,1,0:T(8,128)(2,1)} %bitcast.137, bf16[896,896]{1,0:T(8,128)(2,1)} %param.33), kind=kOutput, calls=%fused_computation.4 | convolution fusion | flops 205520896 | bytes 2293760 | tf_op jit(solution)/shard_map/dot_general | solution.py:293
  239.4 12.8 %shard_map.174 = f32[16,8,896]{2,1,0:T(8,128)} custom-call(f32[16,8,896]{2,1,0:T(8,128)} %fusion.x_ref), custom_call_target="tpu_custom_call" | custom-call | tf_op jit(solution)/shard_map/pallas_call | solution.py:54
  252.2 1.1 reduce_sum.154
  (83 shorter events, 10.7 us)
Async XLA Ops:
  0.0 156.9 %copy-start = (bf16[224,7168]{1,0:T(8,128)(2,1)S(1)}, bf16[224,7168]{1,0:T(8,128)(2,1)}, u32[]{:S(2)}) copy-start(bf16[224,7168]{1,0:T(8,128)(2,1)} %param.26) | copy-start | bytes 9633796
  38.5 37.5 %copy-start.4 = (bf16[16,3584]{1,0:T(8,128)(2,1)S(1)}, bf16[16,3584]{1,0:T(8,128)(2,1)}, u32[]{:S(2)}) copy-start(bf16[16,3584]{1,0:T(8,128)(2,1)} %param.18) | copy-start | bytes 344068
  76.0 22.4 %copy-start.1 = (bf16[16,3584]{1,0:T(8,128)(2,1)}, bf16[16,3584]{1,0:T(8,128)(2,1)S(1)}, u32[]{:S(2)}) copy-start(bf16[16,3584]{1,0:T(8,128)(2,1)S(1)} %reduce_sum.139) | copy-start | bytes 344068
  115.0 5.7 %copy-start.9 = (f32[4,4,112]{2,1,0:T(4,128)S(1)}, f32[4,4,112]{2,1,0:T(4,128)}, u32[]{:S(2)}) copy-start(f32[4,4,112]{2,1,0:T(4,128)} %get-tuple-element.29) | copy-start | bytes 21508
  115.0 5.7 %copy-start.10 = (f32[4,4,112]{2,1,0:T(4,128)S(1)}, f32[4,4,112]{2,1,0:T(4,128)}, u32[]{:S(2)}) copy-start(f32[4,4,112]{2,1,0:T(4,128)} %get-tuple-element.30) | copy-start | bytes 21508
  120.7 6.9 %copy-start.6 = (bf16[4,4,16,224]{3,2,1,0:T(8,128)(2,1)S(1)}, bf16[4,4,16,224]{3,2,1,0:T(8,128)(2,1)}, u32[]{:S(2)}) copy-start(bf16[4,4,16,224]{3,2,1,0:T(8,128)(2,1)} %reshape.384) | copy-start | bytes 344068
  122.7 6.9 %copy-start.11 = (pred[4,768]{1,0:T(4,128)(4,1)S(1)}, pred[4,768]{1,0:T(4,128)(4,1)}, u32[]{:S(2)}) copy-start(pred[4,768]{1,0:T(4,128)(4,1)} %fusion.30) | copy-start | bytes 9220
  128.5 5.9 %slice-start = ((s8[5505024]{0:T(1024)(128)(4,1)}), s8[4194304]{0:T(1024)(128)(4,1)S(1)}, s32[]{:S(2)}) async-start(s8[5505024]{0:T(1024)(128)(4,1)} %bitcast.148), calls=%async_computation | async-start | bytes 8388608
  129.7 4.7 %copy-start.7 = (pred[16,3584]{1,0:T(8,128)(4,1)S(1)}, pred[16,3584]{1,0:T(8,128)(4,1)}, u32[]{:S(2)}) copy-start(pred[16,3584]{1,0:T(8,128)(4,1)} %iota_compare_fusion) | copy-start | bytes 172036
  129.7 4.7 %slice-start.1 = ((s8[5505024]{0:T(1024)(128)(4,1)}), s8[1310720]{0:T(1024)(128)(4,1)S(1)}, s32[]{:S(2)}) async-start(s8[5505024]{0:T(1024)(128)(4,1)} %bitcast.148), calls=%async_computation.1 | async-start | bytes 2621440
  134.5 5.5 %copy-start.12 = (f32[256]{0:T(256)S(1)}, f32[256]{0:T(256)}, u32[]{:S(2)}) copy-start(f32[256]{0:T(256)} %pad.10.clone) | copy-start | bytes 3076
  157.4 13.2 %copy-start.2 = (bf16[16,3584]{1,0:T(8,128)(2,1)S(1)}, bf16[16,3584]{1,0:T(8,128)(2,1)}, u32[]{:S(2)}) copy-start(bf16[16,3584]{1,0:T(8,128)(2,1)} %copy-done.1) | copy-start | bytes 344068
  157.4 13.2 %copy-start.5 = (bf16[16,3584]{1,0:T(8,128)(2,1)S(1)}, bf16[16,3584]{1,0:T(8,128)(2,1)}, u32[]{:S(2)}) copy-start(bf16[16,3584]{1,0:T(8,128)(2,1)} %param.18) | copy-start | bytes 344068
  158.5 26.8 %copy-start.8 = (f32[8,896]{1,0:T(8,128)S(1)}, f32[8,896]{1,0:T(8,128)}, u32[]{:S(2)}) copy-start(f32[8,896]{1,0:T(8,128)} %reshape.391) | copy-start | bytes 86020
  201.3 4.3 %copy-start.3 = (bf16[896,896]{1,0:T(8,128)(2,1)S(1)}, bf16[896,896]{1,0:T(8,128)(2,1)}, u32[]{:S(2)}) copy-start(bf16[896,896]{1,0:T(8,128)(2,1)} %param.28) | copy-start | bytes 4816900

commit v4 on v3

--- a/solution.py
+++ b/solution.py
@@ -144,10 +144,13 @@
     looked = jnp.where(present[:, None], looked, 0.0).astype(jnp.bfloat16)
     by_group = exchange(looked.reshape(req_devices, group_rows, looked.shape[1]), "req", 10)
     column_part = jnp.sum(by_group.astype(jnp.float32), axis=0).astype(jnp.bfloat16)
-    from_columns = exchange(column_part, "seq", 11, gather=True)
-    embedded = jnp.sum(from_columns.astype(jnp.float32), axis=0)
-    joined = jnp.concatenate([hidden, embedded.astype(jnp.bfloat16)], axis=1)
-    normed = rms_norm(joined, attention_norm_gain)
+    row_share = group_rows // seq_devices
+    row_parts = exchange(column_part.reshape(seq_devices, row_share, column_part.shape[1]), "seq", 11)
+    embedded_rows = jnp.sum(row_parts.astype(jnp.float32), axis=0).astype(jnp.bfloat16)
+    own_hidden = lax.dynamic_slice_in_dim(hidden, seq_index * row_share, row_share, 0)
+    own_rows = jnp.concatenate([own_hidden, embedded_rows], axis=1)
+    normed_rows = rms_norm(own_rows, attention_norm_gain)
+    normed = exchange(normed_rows, "seq", 12, gather=True).reshape(group_rows, own_rows.shape[1])
     width_share = normed.shape[1] // req_devices
     to_owners = jnp.transpose(normed.reshape(group_rows, req_devices, width_share), (1, 0, 2))
     block_rows = exchange(to_owners, "req", 4).reshape(req_devices * group_rows, width_share)
@@ -255,9 +258,7 @@
     )
     projected_out = jnp.dot(attention, attention_output_weight, preferred_element_type=jnp.float32)
     model_width = projected_out.shape[1]
-    row_share = group_rows // seq_devices
     out_parts = exchange(projected_out.reshape(seq_devices, row_share, model_width), "seq", 1)
-    own_rows = lax.dynamic_slice_in_dim(joined, seq_index * row_share, row_share, 0)
     after_rows = (own_rows.astype(jnp.float32) + jnp.sum(out_parts, axis=0)).astype(jnp.bfloat16)
     after_attn = exchange(after_rows, "seq", 2, gather=True).reshape(group_rows, model_width)
     second_normed_state = rms_norm(after_attn, feedforward_norm_gain)

time: 256 us -> 242 us (0.945)
  Pallas kernels: 167 us -> 158 us
  other arithmetic: 37.2 us -> 31.2 us
    pallas_call x12 -> x13, Pallas kernels: 167 us -> 158 us  [exchange(): pl.pallas_call(functools.partial(_exchange_kernel, axis, n, gather), out_...]
    pallas_call x1 -> x2, other arithmetic: 2.28 us -> 5.26 us  [exchange(): pl.pallas_call(functools.partial(_exchange_kernel, axis, n, gather), out_...]
    dot_general x1, matrix products: 1.65 us -> 4.22 us  [body(): jnp.dot(weights.astype(jnp.bfloat16).reshape(group_rows * HEADS, slots *...]
where the time goes in v4:
time: 242 us; the launch traced here: 240 us
  Pallas kernels  158 us (65%)
  other arithmetic  31.2 us (13%)
  local copies, waits for them, and re-layouts  28.3 us (12%)
  matrix products  21.8 us (9%)
    pallas_call x13, Pallas kernels, exchange(): pl.pallas_call(functools.partial(_exchange_kernel, axis, n, gather), out_...  158 us
    pallas_call x2, other arithmetic, exchange(): pl.pallas_call(functools.partial(_exchange_kernel, axis, n, gather), out_...  5.26 us
    gather x1, local copies, waits for them, and re-layouts, body(): jnp.take(token_embedding_table, jnp.clip(local_ids, 0, vocab_rows - 1), a...  4.89 us

profile of v4, /device:TPU:1, one launch (start us, length us, event | category | flops | bytes accessed | tf_op | source)
XLA Modules:
  0.0 240.2 jit_solution(13614792768214033540)
XLA Ops:
  0.0 0.8 compare_and_fusion.1
  0.8 4.9 %gather_fusion = bf16[128,3584]{1,0:T(8,128)(2,1)} fusion(bf16[250,3584]{1,0:T(8,128)(2,1)} %param.19, s32[1024]{0:T(1024)S(1)} %pad_clamp_fusion), kind=kCustom, calls=%fused_computation | custom fusion | bytes 1835520 | tf_op jit(solution)/shard_map/jit(_take)/gather | solution.py:141
  5.9 2.5 %select_convert_fusion.x_ref = bf16[8,16,3584]{2,1,0:T(8,128)(2,1)} fusion(bf16[8,16,3584]{2,1,0:T(8,128)(2,1)} %bitcast.131, pred[8,16]{1,0:T(8,128)(4,1)S(1)} %broadcast_in_dim.153, pred[8,16]{1,0:T(8,128)(4,1)S(1)} %broadcast_in_dim.151), kind=kLoop, calls=%fused_computation.2 | loop fusion | flops 1835008 | bytes 1835264 | tf_op jit(solution)/shard_map/convert_element_type | solution.py:144
  8.3 18.4 %shard_map.163 = bf16[8,16,3584]{2,1,0:T(8,128)(2,1)} custom-call(bf16[8,16,3584]{2,1,0:T(8,128)(2,1)} %select_convert_fusion.x_ref), custom_call_target="tpu_custom_call" | custom-call | tf_op jit(solution)/shard_map/pallas_call | solution.py:54
  26.8 1.3 reduce_sum.138
  28.1 0.9 copy.86.x_ref
  29.0 12.2 %shard_map.164 = bf16[16,1,3584]{2,1,0:T(2,128)(2,1)} custom-call(bf16[16,1,3584]{2,1,0:T(2,128)(2,1)} %copy.86.x_ref), custom_call_target="tpu_custom_call" | custom-call | tf_op jit(solution)/shard_map/pallas_call | solution.py:54
  41.2 1.2 reduce_sum.139
  42.3 0.9 fusion.34
  43.8 0.7 multiply_reduce_fusion.1
  45.3 0.6 convert_element_type.127.x_ref
  46.0 12.8 %shard_map.165 = bf16[16,1,7168]{2,1,0:T(2,128)(2,1)} custom-call(bf16[1,7168]{1,0:T(2,128)(2,1)} %convert_element_type.127.x_ref), custom_call_target="tpu_custom_call" | custom-call | tf_op jit(solution)/shard_map/pallas_call | solution.py:54
  58.7 2.3 reduce.13
  61.0 0.7 copy.145
  61.7 8.9 %shard_map.166 = bf16[8,16,896]{2,1,0:T(8,128)(2,1)} custom-call(bf16[8,16,896]{2,1,0:T(8,128)(2,1)} %bitcast.136), custom_call_target="tpu_custom_call" | custom-call | tf_op jit(solution)/shard_map/pallas_call | solution.py:54
  70.6 2.7 %fusion.3.x_ref = f32[8,16,672]{2,1,0:T(8,128)} fusion(bf16[8,16,896]{2,1,0:T(8,128)(2,1)} %shard_map.166, bf16[896,672]{0,1:T(8,128)(2,1)} %param.21), kind=kOutput, calls=%fused_computation.8 | convolution fusion | flops 154140672 | bytes 1777664 | tf_op jit(solution)/shard_map/dot_general | solution.py:157
  73.3 10.3 %shard_map.167 = f32[8,16,672]{2,1,0:T(8,128)} custom-call(f32[8,16,672]{2,1,0:T(8,128)} %fusion.3.x_ref), custom_call_target="tpu_custom_call" | custom-call | tf_op jit(solution)/shard_map/pallas_call | solution.py:54
  83.6 1.6 reduce_sum.142.x_ref
  85.2 12.3 %shard_map.168 = bf16[16,16,672]{2,1,0:T(8,128)(2,1)} custom-call(bf16[16,672]{1,0:T(8,128)(2,1)} %reduce_sum.142.x_ref), custom_call_target="tpu_custom_call" | custom-call | tf_op jit(solution)/shard_map/pallas_call | solution.py:54
  97.5 1.9 copy.90
  99.4 1.5 reshape.434
  100.9 0.8 fusion.36
  101.7 1.1 reshape.443
  102.9 0.7 add_convert_fusion.3
  103.9 0.8 maximum_convert_fusion
  104.7 1.1 reshape.444
  106.1 1.2 fusion.11
  107.9 0.9 copy.93
  109.1 1.4 broadcast_select_fusion
  111.6 4.8 %fusion.7 = (f32[256]{0:T(256)S(1)}, f32[256,768]{1,0:T(8,128)S(1)}) fusion(pred[4,768]{1,0:T(4,128)(4,1)S(1)} %fusion.28, bf16[256,3584]{1,0:T(8,128)(2,1)} %bitcast.125, bf16[768,3584]{1,0:T(8,128)(2,1)} %bitcast.126), kind=kOutput, calls=%fused_computation.17 | convolution fusion | flops 1409875712 | bytes 8130560 | tf_op jit(solution)/shard_map/dot_general | solution.py:192
  116.7 4.2 %fusion.2 = f32[16,3584]{1,0:T(8,128)S(1)} fusion(bf16[16,16,768]{2,1,0:T(8,128)(2,1)S(1)} %bitcast.140, bf16[768,3584,1]{1,0,2:T(8,128)(2,1)} %bitcast.149, pred[16,3584]{1,0:T(8,128)(4,1)S(1)} %iota_compare_fusion), kind=kOutput, calls=%fused_computation.6 | convolution fusion | flops 1411063808 | bytes 6184960 | tf_op jit(solution)/shard_map/dot_general | solution.py:203
  120.9 0.9 concatenate.47
  121.8 1.1 copy.94
  123.0 0.8 copy.96
  123.9 0.8 copy.95
  124.8 1.8 maximum_bitcast_fusion.1.x_ref
  126.6 9.5 %shard_map.169 = f32[16,16,256]{2,1,0:T(8,128)} custom-call(f32[16,16,256]{2,1,0:T(8,128)} %maximum_bitcast_fusion.1.x_ref), custom_call_target="tpu_custom_call" | custom-call | tf_op jit(solution)/shard_map/pallas_call | solution.py:54
  136.2 1.0 reshape.438
  137.2 0.9 fusion.37
  138.1 1.1 copy.118
  139.2 1.1 copy.121
  141.1 1.1 reshape.439
  143.0 1.1 reshape.441.x_ref
  144.1 10.7 %shard_map.170 = f32[16,1,7168]{2,1,0:T(1,128)} custom-call(f32[16,1,7168]{2,1,0:T(1,128)} %reshape.441.x_ref), custom_call_target="tpu_custom_call" | custom-call | tf_op jit(solution)/shard_map/pallas_call | solution.py:54
  154.8 1.3 reduce_sum.150
  156.2 0.6 add_convert_fusion.2.x_ref
  156.8 10.1 %shard_map.171 = bf16[16,1,7168]{2,1,0:T(2,128)(2,1)} custom-call(bf16[1,7168]{1,0:T(2,128)(2,1)} %add_convert_fusion.2.x_ref), custom_call_target="tpu_custom_call" | custom-call | tf_op jit(solution)/shard_map/pallas_call | solution.py:54
  166.9 3.0 %reduce.14 = bf16[16,7168]{1,0:T(8,128)(2,1)} reduce(bf16[16,1,7168]{2,1,0:T(2,128)(2,1)} %shard_map.171, bf16[]{:T(256)} %constant.106), dimensions={1}, to_apply=%pallas_call.47.reduce_sub_computation | reduce | bytes 458754 | tf_op jit(solution)/shard_map/pallas_call | solution.py:54
  169.9 1.0 copy.128
  170.9 1.6 multiply_reduce_fusion
  172.7 0.8 maximum_bitcast_fusion.x_ref
  173.5 15.0 %shard_map.172 = bf16[8,2,16,896]{3,2,1,0:T(8,128)(2,1)} custom-call(bf16[8,2,16,896]{3,2,1,0:T(8,128)(2,1)} %maximum_bitcast_fusion.x_ref), custom_call_target="tpu_custom_call" | custom-call | tf_op jit(solution)/shard_map/pallas_call | solution.py:54
  188.5 1.2 fusion.35
  189.7 1.9 fusion.41
  192.3 1.0 pad_maximum_fusion
  193.4 16.8 %shard_map.173 = f32[8,16,1920]{2,1,0:T(8,128)} custom-call(f32[8,16,1920]{2,1,0:T(8,128)} %bitcast.127), custom_call_target="tpu_custom_call" | custom-call | tf_op jit(solution)/shard_map/pallas_call | solution.py:54
  210.2 1.9 reduce_sum.153
  212.1 1.1 convolution_add_fusion.1
  213.2 1.7 fusion.6.x_ref
  214.9 8.0 %shard_map.174 = bf16[8,16,896]{2,1,0:T(8,128)(2,1)} custom-call(bf16[16,896]{1,0:T(8,128)(2,1)} %fusion.6.x_ref), custom_call_target="tpu_custom_call" | custom-call | tf_op jit(solution)/shard_map/pallas_call | solution.py:54
  222.9 2.8 %fusion.x_ref = f32[16,8,896]{2,1,0:T(8,128)} fusion(bf16[16,8,896]{2,1,0:T(8,128)(2,1)} %bitcast.135, bf16[896,896]{1,0:T(8,128)(2,1)} %param.33), kind=kOutput, calls=%fused_computation.4 | convolution fusion | flops 205520896 | bytes 2293760 | tf_op jit(solution)/shard_map/dot_general | solution.py:294
  225.7 12.8 %shard_map.175 = f32[16,8,896]{2,1,0:T(8,128)} custom-call(f32[16,8,896]{2,1,0:T(8,128)} %fusion.x_ref), custom_call_target="tpu_custom_call" | custom-call | tf_op jit(solution)/shard_map/pallas_call | solution.py:54
  238.5 1.1 reduce_sum.154
  239.6 0.6 add_convert_fusion.1
  (77 shorter events, 6.3 us)
Async XLA Ops:
  0.0 142.5 %copy-start = (bf16[224,7168]{1,0:T(8,128)(2,1)S(1)}, bf16[224,7168]{1,0:T(8,128)(2,1)}, u32[]{:S(2)}) copy-start(bf16[224,7168]{1,0:T(8,128)(2,1)} %param.26) | copy-start | bytes 9633796
  8.3 37.0 %copy-start.7 = (bf16[7168]{0:T(1024)(128)(2,1)S(1)}, bf16[7168]{0:T(1024)(128)(2,1)}, u32[]{:S(2)}) copy-start(bf16[7168]{0:T(1024)(128)(2,1)} %param.20) | copy-start | bytes 43012
  42.3 3.6 %copy-start.3 = (bf16[1,3584]{1,0:T(2,128)(2,1)}, bf16[1,3584]{1,0:T(2,128)(2,1)S(1)}, u32[]{:S(2)}) copy-start(bf16[1,3584]{1,0:T(2,128)(2,1)S(1)} %concatenate.42) | copy-start | bytes 21508
  43.2 0.6 copy-start.5
  106.1 4.4 %copy-start.10 = (s32[4]{0:T(128)S(1)}, s32[4]{0:T(128)}, u32[]{:S(2)}) copy-start(s32[4]{0:T(128)} %param.24) | copy-start | bytes 52
  106.1 4.5 %copy-start.9 = (s32[4,48]{1,0:T(4,128)S(1)}, s32[4,48]{1,0:T(4,128)}, u32[]{:S(2)}) copy-start(s32[4,48]{1,0:T(4,128)} %param.25) | copy-start | bytes 2308
  143.0 13.1 %copy-start.4 = (bf16[1,3584]{1,0:T(2,128)(2,1)S(1)}, bf16[1,3584]{1,0:T(2,128)(2,1)}, u32[]{:S(2)}) copy-start(bf16[1,3584]{1,0:T(2,128)(2,1)} %copy-done.3) | copy-start | bytes 21508
  143.0 13.1 %copy-start.6 = (bf16[1,3584]{1,0:T(2,128)(2,1)S(1)}, bf16[1,3584]{1,0:T(2,128)(2,1)}, u32[]{:S(2)}) copy-start(bf16[1,3584]{1,0:T(2,128)(2,1)} %copy-done.5) | copy-start | bytes 21508
  144.1 28.4 %copy-start.8 = (bf16[7168]{0:T(1024)(128)(2,1)S(1)}, bf16[7168]{0:T(1024)(128)(2,1)}, u32[]{:S(2)}) copy-start(bf16[7168]{0:T(1024)(128)(2,1)} %param.27) | copy-start | bytes 43012
  188.5 3.2 %copy-start.1 = (bf16[896,896]{1,0:T(8,128)(2,1)S(1)}, bf16[896,896]{1,0:T(8,128)(2,1)}, u32[]{:S(2)}) copy-start(bf16[896,896]{1,0:T(8,128)(2,1)} %param.29) | copy-start | bytes 4816900
  189.7 2.4 copy-start.2

commit v5 on v4

--- a/solution.py
+++ b/solution.py
@@ -63,6 +63,86 @@
         ],
         compiler_params=pltpu.CompilerParams(collective_id=cid, has_side_effects=True),
     )(x)
+
+
+def _greet(axes_sizes):
+    barrier = pltpu.get_barrier_semaphore()
+    total = 0
+    for axis, n in axes_sizes:
+        me = lax.axis_index(axis)
+        for k in range(1, n):
+            peer = lax.rem(me + k, n)
+            pl.semaphore_signal(barrier, 1, device_id={axis: peer}, device_id_type=MESH_ID)
+        total += n - 1
+    pl.semaphore_wait(barrier, total)
+
+
+def _start_round(axis, n, gather, source, target, send_sem, recv_sem, local_sem):
+    me = lax.axis_index(axis)
+    copies = []
+    for k in range(1, n):
+        peer = lax.rem(me + k, n)
+        copy = pltpu.make_async_remote_copy(
+            src_ref=source if gather else source.at[peer],
+            dst_ref=target.at[me],
+            send_sem=send_sem.at[k],
+            recv_sem=recv_sem.at[k],
+            device_id={axis: peer},
+            device_id_type=MESH_ID,
+        )
+        copy.start()
+        copies.append(copy)
+    local = pltpu.make_async_copy(source if gather else source.at[me], target.at[me], local_sem)
+    local.start()
+    copies.append(local)
+    return copies
+
+
+def _two_round_kernel(first, second, mid, n_extra, x_ref, *refs):
+    extra = refs[:n_extra]
+    y_ref, landed, staged, send_a, recv_a, send_b, recv_b, local_sems = refs[n_extra:]
+    axis_a, n_a, gather_a = first
+    axis_b, n_b, gather_b = second
+    greeted = [(axis_a, n_a)] if axis_a == axis_b else [(axis_a, n_a), (axis_b, n_b)]
+    _greet(greeted)
+    for copy in _start_round(axis_a, n_a, gather_a, x_ref, landed, send_a, recv_a, local_sems.at[0]):
+        copy.wait()
+    staged[...] = mid(landed, *extra)
+    for copy in _start_round(axis_b, n_b, gather_b, staged, y_ref, send_b, recv_b, local_sems.at[1]):
+        copy.wait()
+
+
+def two_rounds(x, first, second, mid, staged_shape, staged_dtype, cid, extra=()):
+    axis_a, gather_a = first
+    axis_b, gather_b = second
+    n_a, n_b = lax.axis_size(axis_a), lax.axis_size(axis_b)
+    landed_shape = (n_a,) + x.shape if gather_a else x.shape
+    out_shape = (n_b,) + staged_shape if gather_b else staged_shape
+    return pl.pallas_call(
+        functools.partial(
+            _two_round_kernel, (axis_a, n_a, gather_a), (axis_b, n_b, gather_b), mid, len(extra)
+        ),
+        out_shape=jax.ShapeDtypeStruct(out_shape, staged_dtype),
+        in_specs=[pl.BlockSpec(memory_space=pltpu.VMEM)] * (1 + len(extra)),
+        out_specs=pl.BlockSpec(memory_space=pltpu.VMEM),
+        scratch_shapes=[
+            pltpu.VMEM(landed_shape, x.dtype),
+            pltpu.VMEM(staged_shape, staged_dtype),
+            pltpu.SemaphoreType.DMA((n_a,)),
+            pltpu.SemaphoreType.DMA((n_a,)),
+            pltpu.SemaphoreType.DMA((n_b,)),
+            pltpu.SemaphoreType.DMA((n_b,)),
+            pltpu.SemaphoreType.DMA((2,)),
+        ],
+        compiler_params=pltpu.CompilerParams(collective_id=cid, has_side_effects=True),
+    )(x, *extra)
+
+
+def _block_sum(landed):
+    total = landed[0].astype(jnp.float32)
+    for k in range(1, landed.shape[0]):
+        total = total + landed[k].astype(jnp.float32)
+    return total
 
 
 def merged_2(array, axis, combine):
@@ -142,10 +222,17 @@
         jnp.float32
     )
     looked = jnp.where(present[:, None], looked, 0.0).astype(jnp.bfloat16)
-    by_group = exchange(looked.reshape(req_devices, group_rows, looked.shape[1]), "req", 10)
-    column_part = jnp.sum(by_group.astype(jnp.float32), axis=0).astype(jnp.bfloat16)
     row_share = group_rows // seq_devices
-    row_parts = exchange(column_part.reshape(seq_devices, row_share, column_part.shape[1]), "seq", 11)
+    by_group = looked.reshape(req_devices, seq_devices, row_share, looked.shape[1])
+    row_parts = two_rounds(
+        by_group,
+        ("req", False),
+        ("seq", False),
+        lambda landed: _block_sum(landed).astype(jnp.bfloat16),
+        by_group.shape[1:],
+        jnp.bfloat16,
+        10,
+    )
     embedded_rows = jnp.sum(row_parts.astype(jnp.float32), axis=0).astype(jnp.bfloat16)
     own_hidden = lax.dynamic_slice_in_dim(hidden, seq_index * row_share, row_share, 0)
     own_rows = jnp.concatenate([own_hidden, embedded_rows], axis=1)
@@ -155,10 +242,16 @@
     to_owners = jnp.transpose(normed.reshape(group_rows, req_devices, width_share), (1, 0, 2))
     block_rows = exchange(to_owners, "req", 4).reshape(req_devices * group_rows, width_share)
     qkv_full = jnp.dot(block_rows, query_key_value_weight, preferred_element_type=jnp.float32)
-    qkv_parts = exchange(qkv_full.reshape(req_devices, group_rows, qkv_full.shape[1]), "req", 5)
-    qkv_part = jnp.sum(qkv_parts, axis=0).astype(jnp.bfloat16)
-    qkv_all = exchange(qkv_part, "seq", 6, gather=True)
-    projected = jnp.transpose(qkv_all, (1, 0, 2)).reshape(group_rows, seq_devices * qkv_part.shape[1])
+    qkv_all = two_rounds(
+        qkv_full.reshape(req_devices, group_rows, qkv_full.shape[1]),
+        ("req", False),
+        ("seq", True),
+        lambda landed: _block_sum(landed).astype(jnp.bfloat16),
+        (group_rows, qkv_full.shape[1]),
+        jnp.bfloat16,
+        5,
+    )
+    projected = jnp.transpose(qkv_all, (1, 0, 2)).reshape(group_rows, seq_devices * qkv_all.shape[2])
     head_cols = HEADS * HD
     queries = projected[:, :head_cols].reshape(requests, steps_each, HEADS, HD)
     new_keys = projected[:, head_cols : 2 * head_cols].reshape(requests, steps_each, HEADS, HD)
@@ -258,9 +351,16 @@
     )
     projected_out = jnp.dot(attention, attention_output_weight, preferred_element_type=jnp.float32)
     model_width = projected_out.shape[1]
-    out_parts = exchange(projected_out.reshape(seq_devices, row_share, model_width), "seq", 1)
-    after_rows = (own_rows.astype(jnp.float32) + jnp.sum(out_parts, axis=0)).astype(jnp.bfloat16)
-    after_attn = exchange(after_rows, "seq", 2, gather=True).reshape(group_rows, model_width)
+    after_attn = two_rounds(
+        projected_out.reshape(seq_devices, row_share, model_width),
+        ("seq", False),
+        ("seq", True),
+        lambda landed, own: (own[...].astype(jnp.float32) + _block_sum(landed)).astype(jnp.bfloat16),
+        (row_share, model_width),
+        jnp.bfloat16,
+        1,
+        extra=(own_rows,),
+    ).reshape(group_rows, model_width)
     second_normed_state = rms_norm(after_attn, feedforward_norm_gain)
     both = jnp.stack([after_attn, second_normed_state]).reshape(2, group_rows, req_devices, width_share)
     both_parts = exchange(jnp.transpose(both, (2, 0, 1, 3)), "req", 7)
@@ -275,20 +375,25 @@
         ],
         axis=1,
     )
-    mlp_parts = exchange(mlp_full.reshape(req_devices, group_rows, mlp_full.shape[1]), "req", 8)
-    mlp_sum = jnp.sum(mlp_parts, axis=0)
-    gate_total = mlp_sum[:, :units]
-    up_total = mlp_sum[:, units : 2 * units]
-    low_sum = mlp_sum[:, 2 * units :]
-    adapter_hidden = low_sum.astype(jnp.bfloat16)
-    gate_preactivation = gate_total + jnp.dot(
-        adapter_hidden, adapter_gate_map, preferred_element_type=jnp.float32
-    )
-    up_projection_part = up_total + jnp.dot(
-        adapter_hidden, adapter_up_map, preferred_element_type=jnp.float32
-    )
-    group_act = (jax.nn.silu(gate_preactivation) * up_projection_part).astype(jnp.bfloat16)
-    inner_act = exchange(group_act, "req", 9, gather=True).reshape(req_devices * group_rows, units)
+    def activate(landed, gate_map, up_map):
+        total = _block_sum(landed)
+        low = total[:, 2 * units :].astype(jnp.bfloat16)
+        gate_pre = total[:, :units] + jnp.dot(low, gate_map[...], preferred_element_type=jnp.float32)
+        up_part = total[:, units : 2 * units] + jnp.dot(
+            low, up_map[...], preferred_element_type=jnp.float32
+        )
+        return (gate_pre / (1.0 + jnp.exp(-gate_pre)) * up_part).astype(jnp.bfloat16)
+
+    inner_act = two_rounds(
+        mlp_full.reshape(req_devices, group_rows, mlp_full.shape[1]),
+        ("req", False),
+        ("req", True),
+        activate,
+        (group_rows, units),
+        jnp.bfloat16,
+        8,
+        extra=(adapter_gate_map, adapter_up_map),
+    ).reshape(req_devices * group_rows, units)
     out_rows = residual_cols.shape[0] // seq_devices
     block_rows = inner_act
     down_full = jnp.dot(block_rows, down_weight, preferred_element_type=jnp.float32)

time: 242 us -> 228 us (0.942)
  Pallas kernels: 158 us -> 153 us
  other arithmetic: 31.2 us -> 28 us
  matrix products: 21.8 us -> 18.9 us
    pallas_call x13 -> x5, Pallas kernels: 158 us -> 57.5 us  [exchange(): pl.pallas_call(functools.partial(_exchange_kernel, axis, n, gather), out_...]
    pallas_call x0 -> x4, Pallas kernels: none -> 95.8 us  [two_rounds(): pl.pallas_call(functools.partial(_two_round_kernel, (axis_a, n_a, gather_...]
    reduce_sum x4 -> x0, other arithmetic: 6.17 us -> none  [the longest x1 1.92 us: body(): mlp_sum = jnp.sum(mlp_parts, axis=0)]
    convert_element_type x1, other arithmetic: 2.46 us -> 5.62 us  [body(): looked = jnp.where(present[:, None], looked, 0.0).astype(jnp.bfloat16)]
    pallas_call x0 -> x1, other arithmetic: none -> 2.98 us  [two_rounds(): pl.pallas_call(functools.partial(_two_round_kernel, (axis_a, n_a, gather_...]
    pallas_call x2 -> x1, other arithmetic: 5.26 us -> 2.29 us  [exchange(): pl.pallas_call(functools.partial(_exchange_kernel, axis, n, gather), out_...]
    dot_general x2 -> x0, matrix products: 2.8 us -> none  [the longest x1 1.72 us: body(): jnp.dot(adapter_hidden, adapter_up_map, preferred_element_type=jnp.float32)]
where the time goes in v5:
time: 228 us; the launch traced here: 227 us
  Pallas kernels  153 us (67%)
  other arithmetic  28 us (12%)
  local copies, waits for them, and re-layouts  25.9 us (11%)
  matrix products  18.9 us (8%)
    pallas_call x4, Pallas kernels, two_rounds(): pl.pallas_call(functools.partial(_two_round_kernel, (axis_a, n_a, gather_...  95.8 us
    pallas_call x5, Pallas kernels, exchange(): pl.pallas_call(functools.partial(_exchange_kernel, axis, n, gather), out_...  57.5 us
    convert_element_type x1, other arithmetic, body(): looked = jnp.where(present[:, None], looked, 0.0).astype(jnp.bfloat16)  5.62 us
    gather x1, local copies, waits for them, and re-layouts, body(): jnp.take(token_embedding_table, jnp.clip(local_ids, 0, vocab_rows - 1), a...  4.85 us
    dot_general x1, matrix products, body(): jnp.dot(spread_queries.reshape(group_rows * HEADS, head_cols), cache_k.T,...  4.83 us

profile of v5, /device:TPU:1, one launch (start us, length us, event | category | flops | bytes accessed | tf_op | source)
XLA Modules:
  0.0 227.2 jit_solution(7023394173917568299)
XLA Ops:
  0.0 0.8 compare_and_fusion.1
  0.8 4.8 %gather_fusion = bf16[128,3584]{1,0:T(8,128)(2,1)} fusion(bf16[250,3584]{1,0:T(8,128)(2,1)} %param.19, s32[1024]{0:T(1024)S(1)} %pad_clamp_fusion), kind=kCustom, calls=%fused_computation | custom fusion | bytes 1835520 | tf_op jit(solution)/shard_map/jit(_take)/gather | solution.py:221
  5.8 5.6 %fusion.x_ref = bf16[8,16,1,3584]{3,2,1,0:T(2,128)(2,1)} fusion(pred[8,16]{1,0:T(8,128)(4,1)S(1)} %broadcast_in_dim.156, pred[8,16]{1,0:T(8,128)(4,1)S(1)} %broadcast_in_dim.158, bf16[8,16,1,3584]{3,1,0,2:T(8,128)(2,1)} %bitcast.127), kind=kLoop, calls=%fused_computation.4 | loop fusion | flops 1835008 | bytes 1835264 | tf_op jit(solution)/shard_map/convert_element_type | solution.py:224
  11.5 37.1 %shard_map.163 = bf16[16,1,3584]{2,1,0:T(2,128)(2,1)} custom-call(bf16[8,16,1,3584]{3,2,1,0:T(2,128)(2,1)} %fusion.x_ref), custom_call_target="tpu_custom_call" | custom-call | tf_op jit(solution)/shard_map/pallas_call | solution.py:121
  48.5 1.2 reduce_sum.98
  49.7 0.9 fusion.34
  50.6 1.2 multiply_reduce_fusion.1
  52.6 0.6 convert_element_type.122.x_ref
  53.2 12.0 %shard_map.164 = bf16[16,1,7168]{2,1,0:T(2,128)(2,1)} custom-call(bf16[1,7168]{1,0:T(2,128)(2,1)} %convert_element_type.122.x_ref), custom_call_target="tpu_custom_call" | custom-call | tf_op jit(solution)/shard_map/pallas_call | solution.py:54
  65.1 2.3 %reduce.11 = bf16[16,7168]{1,0:T(8,128)(2,1)S(1)} reduce(bf16[16,1,7168]{2,1,0:T(2,128)(2,1)} %shard_map.164, bf16[]{:T(256)} %constant.102), dimensions={1}, to_apply=%pallas_call.28.reduce_sub_computation | reduce | bytes 458754 | tf_op jit(solution)/shard_map/pallas_call | solution.py:54
  67.4 0.7 copy.146
  68.1 8.9 %shard_map.165 = bf16[8,16,896]{2,1,0:T(8,128)(2,1)} custom-call(bf16[8,16,896]{2,1,0:T(8,128)(2,1)} %bitcast.132), custom_call_target="tpu_custom_call" | custom-call | tf_op jit(solution)/shard_map/pallas_call | solution.py:54
  77.0 2.7 %fusion.5.x_ref = f32[8,16,672]{2,1,0:T(8,128)} fusion(bf16[8,16,896]{2,1,0:T(8,128)(2,1)} %shard_map.165, bf16[896,672]{0,1:T(8,128)(2,1)} %param.21), kind=kOutput, calls=%fused_computation.11 | convolution fusion | flops 154140672 | bytes 1777664 | tf_op jit(solution)/shard_map/dot_general | solution.py:244
  79.7 20.2 %shard_map.166 = bf16[16,16,672]{2,1,0:T(8,128)(2,1)} custom-call(f32[8,16,672]{2,1,0:T(8,128)} %fusion.5.x_ref), custom_call_target="tpu_custom_call" | custom-call | tf_op jit(solution)/shard_map/pallas_call | solution.py:121
  99.9 1.9 copy.90
  101.7 1.5 reshape.426
  103.3 0.8 fusion.36
  104.1 1.1 reshape.436
  105.3 0.7 add_convert_fusion.2
  106.2 0.8 subtract_convert_fusion
  107.0 1.1 reshape.435
  108.3 0.1 maximum_convert_fusion
  108.5 1.1 fusion.11
  109.6 0.2 copy.100
  110.2 0.2 convert_element_type.127
  110.5 1.4 broadcast_select_fusion.2
  112.0 0.2 select_reduce_fusion
  112.5 0.3 fusion.32
  113.0 4.8 %fusion.7 = (f32[256]{0:T(256)S(1)}, f32[256,768]{1,0:T(8,128)S(1)}) fusion(pred[4,768]{1,0:T(4,128)(4,1)S(1)} %fusion.28, bf16[256,3584]{1,0:T(8,128)(2,1)} %bitcast.121, bf16[768,3584]{1,0:T(8,128)(2,1)} %bitcast.122), kind=kOutput, calls=%fused_computation.16 | convolution fusion | flops 1409875712 | bytes 8130560 | tf_op jit(solution)/shard_map/dot_general | solution.py:285
  117.8 0.3 fusion.9
  118.1 4.2 %fusion.4 = f32[16,3584]{1,0:T(8,128)S(1)} fusion(bf16[16,16,768]{2,1,0:T(8,128)(2,1)S(1)} %bitcast.135, bf16[768,3584,1]{1,0,2:T(8,128)(2,1)} %bitcast.143, pred[16,3584]{1,0:T(8,128)(4,1)S(1)} %iota_compare_fusion), kind=kOutput, calls=%fused_computation.9 | convolution fusion | flops 1411063808 | bytes 6184960 | tf_op jit(solution)/shard_map/dot_general | solution.py:296
  122.3 0.9 concatenate.43
  123.2 1.1 copy.94
  124.4 0.8 copy.96
  125.3 0.8 copy.95
  126.2 1.8 maximum_bitcast_fusion.1.x_ref
  128.0 9.6 %shard_map.167 = f32[16,16,256]{2,1,0:T(8,128)} custom-call(f32[16,16,256]{2,1,0:T(8,128)} %maximum_bitcast_fusion.1.x_ref), custom_call_target="tpu_custom_call" | custom-call | tf_op jit(solution)/shard_map/pallas_call | solution.py:54
  137.6 1.0 reshape.430
  138.7 0.9 fusion.37
  139.6 1.1 copy.118
  140.6 1.1 copy.121
  141.7 0.2 fusion.31
  142.2 0.1 fusion.10
  142.4 0.2 copy.106
  142.5 1.1 reshape.431
  143.7 0.2 fusion.15
  144.0 0.5 fusion.40
  144.5 1.1 reshape.433.x_ref
  145.6 18.0 %shard_map.168 = bf16[16,1,7168]{2,1,0:T(2,128)(2,1)} custom-call(f32[16,1,7168]{2,1,0:T(1,128)} %reshape.433.x_ref, bf16[1,7168]{1,0:T(2,128)(2,1)} %get-tuple-element.8.refs_0_), custom_call_target="tpu_custom_call" | custom-call | tf_op jit(solution)/shard_map/pallas_call | solution.py:121
  163.6 3.0 %reduce.12 = bf16[16,7168]{1,0:T(8,128)(2,1)} reduce(bf16[16,1,7168]{2,1,0:T(2,128)(2,1)} %shard_map.168, bf16[]{:T(256)} %constant.102), dimensions={1}, to_apply=%pallas_call.32.reduce_sub_computation | reduce | bytes 458754 | tf_op jit(solution)/shard_map/pallas_call | solution.py:121
  166.6 1.0 copy.128
  167.5 1.6 multiply_reduce_fusion
  169.4 0.8 maximum_bitcast_fusion.x_ref
  170.2 14.0 %shard_map.169 = bf16[8,2,16,896]{3,2,1,0:T(8,128)(2,1)} custom-call(bf16[8,2,16,896]{3,2,1,0:T(8,128)(2,1)} %maximum_bitcast_fusion.x_ref), custom_call_target="tpu_custom_call" | custom-call | tf_op jit(solution)/shard_map/pallas_call | solution.py:54
  184.2 1.2 fusion.35
  185.4 1.9 fusion.41
  187.3 0.4 fusion.42
  187.8 0.2 fusion.43
  188.0 1.0 pad_maximum_fusion
  189.0 20.6 %shard_map.170 = bf16[8,16,896]{2,1,0:T(8,128)(2,1)} custom-call(f32[8,16,1920]{2,1,0:T(8,128)} %bitcast.123, bf16[128,896]{1,0:T(8,128)(2,1)} %refs_0_.1, bf16[128,896]{1,0:T(8,128)(2,1)} %refs_1_.1), custom_call_target="tpu_custom_call" | custom-call | tf_op jit(solution)/shard_map/pallas_call | solution.py:121
  209.6 2.8 %fusion.2.x_ref = f32[16,8,896]{2,1,0:T(8,128)} fusion(bf16[16,8,896]{2,1,0:T(8,128)(2,1)} %bitcast.131, bf16[896,896]{1,0:T(8,128)(2,1)} %param.33), kind=kOutput, calls=%fused_computation.7 | convolution fusion | flops 205520896 | bytes 2293760 | tf_op jit(solution)/shard_map/dot_general | solution.py:399
  212.4 13.1 %shard_map.171 = f32[16,8,896]{2,1,0:T(8,128)} custom-call(f32[16,8,896]{2,1,0:T(8,128)} %fusion.2.x_ref), custom_call_target="tpu_custom_call" | custom-call | tf_op jit(solution)/shard_map/pallas_call | solution.py:54
  225.5 1.1 reduce_sum.108
  226.6 0.6 add_convert_fusion.1
  (57 shorter events, 2.6 us)
Async XLA Ops:
  0.0 144.0 %copy-start = (bf16[224,7168]{1,0:T(8,128)(2,1)S(1)}, bf16[224,7168]{1,0:T(8,128)(2,1)}, u32[]{:S(2)}) copy-start(bf16[224,7168]{1,0:T(8,128)(2,1)} %param.26) | copy-start | bytes 9633796
  11.5 41.1 %copy-start.3 = (bf16[7168]{0:T(1024)(128)(2,1)S(1)}, bf16[7168]{0:T(1024)(128)(2,1)}, u32[]{:S(2)}) copy-start(bf16[7168]{0:T(1024)(128)(2,1)} %param.20) | copy-start | bytes 43012
  108.4 3.5 %copy-start.6 = (s32[4]{0:T(128)S(1)}, s32[4]{0:T(128)}, u32[]{:S(2)}) copy-start(s32[4]{0:T(128)} %param.24) | copy-start | bytes 52
  108.4 3.6 %copy-start.5 = (s32[4,48]{1,0:T(4,128)S(1)}, s32[4,48]{1,0:T(4,128)}, u32[]{:S(2)}) copy-start(s32[4,48]{1,0:T(4,128)} %param.25) | copy-start | bytes 2308
  144.5 24.6 %copy-start.4 = (bf16[7168]{0:T(1024)(128)(2,1)S(1)}, bf16[7168]{0:T(1024)(128)(2,1)}, u32[]{:S(2)}) copy-start(bf16[7168]{0:T(1024)(128)(2,1)} %param.27) | copy-start | bytes 43012
  184.2 3.2 %copy-start.1 = (bf16[896,896]{1,0:T(8,128)(2,1)S(1)}, bf16[896,896]{1,0:T(8,128)(2,1)}, u32[]{:S(2)}) copy-start(bf16[896,896]{1,0:T(8,128)(2,1)} %param.29) | copy-start | bytes 4816900
  185.4 2.4 %copy-start.2 = (bf16[896,128]{1,0:T(8,128)(2,1)S(1)}, bf16[896,128]{1,0:T(8,128)(2,1)}, u32[]{:S(2)}) copy-start(bf16[896,128]{1,0:T(8,128)(2,1)} %param.30) | copy-start | bytes 688132

commit v6 on v5

--- a/solution.py
+++ b/solution.py
@@ -223,7 +223,8 @@
     )
     looked = jnp.where(present[:, None], looked, 0.0).astype(jnp.bfloat16)
     row_share = group_rows // seq_devices
-    by_group = looked.reshape(req_devices, seq_devices, row_share, looked.shape[1])
+    lanes = 128
+    by_group = looked.reshape(req_devices, seq_devices, row_share * looked.shape[1] // lanes, lanes)
     row_parts = two_rounds(
         by_group,
         ("req", False),
@@ -233,11 +234,17 @@
         jnp.bfloat16,
         10,
     )
-    embedded_rows = jnp.sum(row_parts.astype(jnp.float32), axis=0).astype(jnp.bfloat16)
+    embedded_rows = (
+        jnp.sum(row_parts.astype(jnp.float32), axis=0)
+        .astype(jnp.bfloat16)
+        .reshape(row_share, looked.shape[1])
+    )
     own_hidden = lax.dynamic_slice_in_dim(hidden, seq_index * row_share, row_share, 0)
     own_rows = jnp.concatenate([own_hidden, embedded_rows], axis=1)
     normed_rows = rms_norm(own_rows, attention_norm_gain)
-    normed = exchange(normed_rows, "seq", 12, gather=True).reshape(group_rows, own_rows.shape[1])
+    normed = exchange(normed_rows.reshape(-1, lanes), "seq", 12, gather=True).reshape(
+        group_rows, own_rows.shape[1]
+    )
     width_share = normed.shape[1] // req_devices
     to_owners = jnp.transpose(normed.reshape(group_rows, req_devices, width_share), (1, 0, 2))
     block_rows = exchange(to_owners, "req", 4).reshape(req_devices * group_rows, width_share)
@@ -352,14 +359,14 @@
     projected_out = jnp.dot(attention, attention_output_weight, preferred_element_type=jnp.float32)
     model_width = projected_out.shape[1]
     after_attn = two_rounds(
-        projected_out.reshape(seq_devices, row_share, model_width),
+        projected_out.reshape(seq_devices, row_share * model_width // lanes, lanes),
         ("seq", False),
         ("seq", True),
         lambda landed, own: (own[...].astype(jnp.float32) + _block_sum(landed)).astype(jnp.bfloat16),
-        (row_share, model_width),
+        (row_share * model_width // lanes, lanes),
         jnp.bfloat16,
         1,
-        extra=(own_rows,),
+        extra=(own_rows.reshape(-1, lanes),),
     ).reshape(group_rows, model_width)
     second_normed_state = rms_norm(after_attn, feedforward_norm_gain)
     both = jnp.stack([after_attn, second_normed_state]).reshape(2, group_rows, req_devices, width_share)

time: 228 us -> 209 us (0.917)
  Pallas kernels: 153 us -> 139 us
  other arithmetic: 28 us -> 19.6 us
  local copies, waits for them, and re-layouts: 25.9 us -> 28.9 us
    pallas_call x4, Pallas kernels: 95.8 us -> 84.2 us  [two_rounds(): pl.pallas_call(functools.partial(_two_round_kernel, (axis_a, n_a, gather_...]
    pallas_call x2 -> x0, other arithmetic: 5.26 us -> none  [the longest x1 2.98 us: two_rounds(): pl.pallas_call(functools.partial(_two_round_kernel, (axis_a, n_a, gather_...]
    convert_element_type x1, other arithmetic: 5.62 us -> 2.36 us  [body(): looked = jnp.where(present[:, None], looked, 0.0).astype(jnp.bfloat16)]
    pallas_call x5, Pallas kernels: 57.5 us -> 54.8 us  [exchange(): pl.pallas_call(functools.partial(_exchange_kernel, axis, n, gather), out_...]
    gather x1 -> x2, local copies, waits for them, and re-layouts: 4.85 us -> 7.26 us  [body(): jnp.take(token_embedding_table, jnp.clip(local_ids, 0, vocab_rows - 1), a...]
where the time goes in v6:
time: 209 us; the launch traced here: 207 us
  Pallas kernels  139 us (67%)
  local copies, waits for them, and re-layouts  28.9 us (14%)
  other arithmetic  19.6 us (9%)
  matrix products  18.9 us (9%)
    pallas_call x4, Pallas kernels, two_rounds(): pl.pallas_call(functools.partial(_two_round_kernel, (axis_a, n_a, gather_...  84.2 us
    pallas_call x5, Pallas kernels, exchange(): pl.pallas_call(functools.partial(_exchange_kernel, axis, n, gather), out_...  54.8 us
    gather x2, local copies, waits for them, and re-layouts, body(): jnp.take(token_embedding_table, jnp.clip(local_ids, 0, vocab_rows - 1), a...  7.26 us
    dot_general x1, matrix products, body(): jnp.dot(spread_queries.reshape(group_rows * HEADS, head_cols), cache_k.T,...  4.83 us
    dot_general x1, matrix products, body(): jnp.dot(weights.astype(jnp.bfloat16).reshape(group_rows * HEADS, slots *...  4.22 us

profile of v6, /device:TPU:1, one launch (start us, length us, event | category | flops | bytes accessed | tf_op | source)
XLA Modules:
  0.0 207.5 jit_solution(14153097856616326301)
XLA Ops:
  0.0 0.8 compare_and_fusion.1
  0.8 4.9 %gather_fusion = bf16[128,3584]{1,0:T(8,128)(2,1)} fusion(bf16[250,3584]{1,0:T(8,128)(2,1)} %param.19, s32[1024]{0:T(1024)S(1)} %pad_clamp_fusion), kind=kCustom, calls=%fused_computation | custom fusion | bytes 1835520 | tf_op jit(solution)/shard_map/jit(_take)/gather | solution.py:221
  5.7 2.4 %gather.7 = bf16[8,16,28,128]{3,2,1,0:T(8,128)(2,1)} reshape(bf16[128,3584]{1,0:T(8,128)(2,1)} %gather_fusion) | data formatting | bytes 1835008 | tf_op jit(solution)/shard_map/jit(_take)/gather | solution.py:221
  8.3 2.4 %select_convert_fusion.x_ref = bf16[8,16,28,128]{3,2,1,0:T(8,128)(2,1)} fusion(bf16[8,16,28,128]{3,2,1,0:T(8,128)(2,1)} %gather.7, pred[8,16]{1,0:T(8,128)(4,1)S(1)} %broadcast_in_dim.158, pred[8,16]{1,0:T(8,128)(4,1)S(1)} %broadcast_in_dim.156), kind=kLoop, calls=%fused_computation.5 | loop fusion | flops 1835008 | bytes 1835264 | tf_op jit(solution)/shard_map/convert_element_type | solution.py:224
  10.6 27.8 %shard_map.163 = bf16[16,28,128]{2,1,0:T(8,128)(2,1)} custom-call(bf16[8,16,28,128]{3,2,1,0:T(8,128)(2,1)} %select_convert_fusion.x_ref), custom_call_target="tpu_custom_call" | custom-call | tf_op jit(solution)/shard_map/pallas_call | solution.py:121
  38.4 0.9 reduce_sum.98
  39.4 0.9 fusion.37
  40.2 0.7 fusion.36
  40.9 0.7 multiply_reduce_fusion.1
  42.4 0.6 fusion.28.x_ref
  43.0 9.6 %shard_map.164 = bf16[16,56,128]{2,1,0:T(8,128)(2,1)} custom-call(bf16[56,128]{1,0:T(8,128)(2,1)} %fusion.28.x_ref), custom_call_target="tpu_custom_call" | custom-call | tf_op jit(solution)/shard_map/pallas_call | solution.py:54
  52.7 1.2 reshape_reshape.3
  53.9 0.7 copy.156
  54.6 9.1 %shard_map.165 = bf16[8,16,896]{2,1,0:T(8,128)(2,1)} custom-call(bf16[8,16,896]{2,1,0:T(8,128)(2,1)} %bitcast.137), custom_call_target="tpu_custom_call" | custom-call | tf_op jit(solution)/shard_map/pallas_call | solution.py:54
  63.7 2.7 %fusion.6.x_ref = f32[8,16,672]{2,1,0:T(8,128)} fusion(bf16[8,16,896]{2,1,0:T(8,128)(2,1)} %shard_map.165, bf16[896,672]{0,1:T(8,128)(2,1)} %param.21), kind=kOutput, calls=%fused_computation.11 | convolution fusion | flops 154140672 | bytes 1777664 | tf_op jit(solution)/shard_map/dot_general | solution.py:251
  66.4 18.9 %shard_map.166 = bf16[16,16,672]{2,1,0:T(8,128)(2,1)} custom-call(f32[8,16,672]{2,1,0:T(8,128)} %fusion.6.x_ref), custom_call_target="tpu_custom_call" | custom-call | tf_op jit(solution)/shard_map/pallas_call | solution.py:121
  85.3 1.9 copy.94
  87.2 1.5 reshape.410
  88.7 0.8 fusion.39
  89.5 1.1 reshape.420
  90.7 0.7 add_convert_fusion.2
  91.6 0.8 subtract_convert_fusion
  92.4 1.1 reshape.419
  93.9 1.1 fusion.12
  95.0 0.2 copy.104
  95.7 0.2 convert_element_type.113
  95.9 1.4 broadcast_select_fusion
  97.5 0.2 select_reduce_fusion
  97.9 0.3 fusion.34
  98.4 4.8 %fusion.8 = (f32[256]{0:T(256)S(1)}, f32[256,768]{1,0:T(8,128)S(1)}) fusion(pred[4,768]{1,0:T(4,128)(4,1)S(1)} %fusion.30, bf16[256,3584]{1,0:T(8,128)(2,1)} %bitcast.129, bf16[768,3584]{1,0:T(8,128)(2,1)} %bitcast.130), kind=kOutput, calls=%fused_computation.16 | convolution fusion | flops 1409875712 | bytes 8130560 | tf_op jit(solution)/shard_map/dot_general | solution.py:292
  103.3 0.3 fusion.10
  103.6 4.2 %fusion.5 = f32[16,3584]{1,0:T(8,128)S(1)} fusion(bf16[16,16,768]{2,1,0:T(8,128)(2,1)S(1)} %bitcast.138, bf16[768,3584,1]{1,0,2:T(8,128)(2,1)} %bitcast.150, pred[16,3584]{1,0:T(8,128)(4,1)S(1)} %iota_compare_fusion), kind=kOutput, calls=%fused_computation.9 | convolution fusion | flops 1411063808 | bytes 6184960 | tf_op jit(solution)/shard_map/dot_general | solution.py:303
  107.8 0.9 concatenate.46
  108.7 1.1 copy.98
  109.8 0.8 copy.100
  110.8 0.8 copy.99
  111.7 1.8 maximum_bitcast_fusion.1.x_ref
  113.5 9.8 %shard_map.167 = f32[16,16,256]{2,1,0:T(8,128)} custom-call(f32[16,16,256]{2,1,0:T(8,128)} %maximum_bitcast_fusion.1.x_ref), custom_call_target="tpu_custom_call" | custom-call | tf_op jit(solution)/shard_map/pallas_call | solution.py:54
  123.3 1.0 reshape.414
  124.3 0.9 fusion.40
  125.2 1.1 copy.124
  126.3 1.1 copy.127
  127.4 0.2 fusion.33
  127.9 0.1 fusion.11
  128.0 0.2 copy.110
  128.2 1.1 reshape.415
  129.3 0.2 fusion.16
  129.6 0.5 fusion
  130.2 0.9 copy.115.x_ref
  131.1 16.7 %shard_map.168 = bf16[16,56,128]{2,1,0:T(8,128)(2,1)} custom-call(f32[16,56,128]{2,1,0:T(8,128)} %copy.115.x_ref, bf16[56,128]{1,0:T(8,128)(2,1)} %bitcast.143), custom_call_target="tpu_custom_call" | custom-call | tf_op jit(solution)/shard_map/pallas_call | solution.py:121
  147.8 1.2 stack.6
  149.0 1.1 multiply_reduce_fusion
  150.4 0.8 maximum_bitcast_fusion.x_ref
  151.2 14.4 %shard_map.169 = bf16[8,2,16,896]{3,2,1,0:T(8,128)(2,1)} custom-call(bf16[8,2,16,896]{3,2,1,0:T(8,128)(2,1)} %maximum_bitcast_fusion.x_ref), custom_call_target="tpu_custom_call" | custom-call | tf_op jit(solution)/shard_map/pallas_call | solution.py:54
  165.6 1.2 fusion.38
  166.8 1.9 fusion.43
  168.8 0.4 fusion.44
  169.2 0.2 fusion.45
  169.4 1.0 pad_maximum_fusion
  170.5 20.7 %shard_map.170 = bf16[8,16,896]{2,1,0:T(8,128)(2,1)} custom-call(f32[8,16,1920]{2,1,0:T(8,128)} %bitcast.131, bf16[128,896]{1,0:T(8,128)(2,1)} %refs_0_.1, bf16[128,896]{1,0:T(8,128)(2,1)} %refs_1_.1), custom_call_target="tpu_custom_call" | custom-call | tf_op jit(solution)/shard_map/pallas_call | solution.py:121
  191.2 2.8 %fusion.3.x_ref = f32[16,8,896]{2,1,0:T(8,128)} fusion(bf16[16,8,896]{2,1,0:T(8,128)(2,1)} %bitcast.136, bf16[896,896]{1,0:T(8,128)(2,1)} %param.33), kind=kOutput, calls=%fused_computation.7 | convolution fusion | flops 205520896 | bytes 2293760 | tf_op jit(solution)/shard_map/dot_general | solution.py:406
  194.0 11.8 %shard_map.171 = f32[16,8,896]{2,1,0:T(8,128)} custom-call(f32[16,8,896]{2,1,0:T(8,128)} %fusion.3.x_ref), custom_call_target="tpu_custom_call" | custom-call | tf_op jit(solution)/shard_map/pallas_call | solution.py:54
  205.8 1.1 reduce_sum.108
  206.9 0.6 add_convert_fusion.1
  (57 shorter events, 2.7 us)
Async XLA Ops:
  0.0 129.6 %copy-start = (bf16[224,7168]{1,0:T(8,128)(2,1)S(1)}, bf16[224,7168]{1,0:T(8,128)(2,1)}, u32[]{:S(2)}) copy-start(bf16[224,7168]{1,0:T(8,128)(2,1)} %param.26) | copy-start | bytes 9633796
  8.1 34.3 %copy-start.3 = (bf16[7168]{0:T(1024)(128)(2,1)S(1)}, bf16[7168]{0:T(1024)(128)(2,1)}, u32[]{:S(2)}) copy-start(bf16[7168]{0:T(1024)(128)(2,1)} %param.20) | copy-start | bytes 43012
  93.9 3.5 %copy-start.6 = (s32[4]{0:T(128)S(1)}, s32[4]{0:T(128)}, u32[]{:S(2)}) copy-start(s32[4]{0:T(128)} %param.24) | copy-start | bytes 52
  93.9 3.6 %copy-start.5 = (s32[4,48]{1,0:T(4,128)S(1)}, s32[4,48]{1,0:T(4,128)}, u32[]{:S(2)}) copy-start(s32[4,48]{1,0:T(4,128)} %param.25) | copy-start | bytes 2308
  130.2 20.0 %copy-start.4 = (bf16[7168]{0:T(1024)(128)(2,1)S(1)}, bf16[7168]{0:T(1024)(128)(2,1)}, u32[]{:S(2)}) copy-start(bf16[7168]{0:T(1024)(128)(2,1)} %param.27) | copy-start | bytes 43012
  165.6 3.2 %copy-start.1 = (bf16[896,896]{1,0:T(8,128)(2,1)S(1)}, bf16[896,896]{1,0:T(8,128)(2,1)}, u32[]{:S(2)}) copy-start(bf16[896,896]{1,0:T(8,128)(2,1)} %param.29) | copy-start | bytes 4816900
  166.8 2.4 %copy-start.2 = (bf16[896,128]{1,0:T(8,128)(2,1)S(1)}, bf16[896,128]{1,0:T(8,128)(2,1)}, u32[]{:S(2)}) copy-start(bf16[896,128]{1,0:T(8,128)(2,1)} %param.30) | copy-start | bytes 688132

commit v7 on v6

--- a/solution.py
+++ b/solution.py
@@ -143,6 +143,87 @@
     for k in range(1, landed.shape[0]):
         total = total + landed[k].astype(jnp.float32)
     return total
+
+
+def _mlp_kernel(
+    x_ref, gate_ref, up_ref, down_map_ref, gate_map_ref, up_map_ref, down_ref,
+    out_ref, spread_ref, landed1, staged1, staged2, landed2, staged3, landed3,
+    send0, recv0, send1, recv1, send2, recv2, send3, recv3, local_sems,
+):
+    n_req = spread_ref.shape[0]
+    n_seq = landed3.shape[0]
+    rows = n_req * spread_ref.shape[2]
+    units = gate_ref.shape[1]
+    _greet([("req", n_req), ("seq", n_seq)])
+    for copy in _start_round("req", n_req, False, x_ref, spread_ref, send0, recv0, local_sems.at[0]):
+        copy.wait()
+    normed_all = spread_ref[:, 1].reshape(rows, spread_ref.shape[3])
+    staged1[:, :, :units] = jnp.dot(
+        normed_all, gate_ref[...], preferred_element_type=jnp.float32
+    ).reshape(staged1.shape[0], staged1.shape[1], units)
+    staged1[:, :, units : 2 * units] = jnp.dot(
+        normed_all, up_ref[...], preferred_element_type=jnp.float32
+    ).reshape(staged1.shape[0], staged1.shape[1], units)
+    staged1[:, :, 2 * units :] = jnp.dot(
+        normed_all, down_map_ref[...], preferred_element_type=jnp.float32
+    ).reshape(staged1.shape[0], staged1.shape[1], staged1.shape[2] - 2 * units)
+    for copy in _start_round("req", n_req, False, staged1, landed1, send1, recv1, local_sems.at[1]):
+        copy.wait()
+    total = _block_sum(landed1)
+    low = total[:, 2 * units :].astype(jnp.bfloat16)
+    gate_pre = total[:, :units] + jnp.dot(low, gate_map_ref[...], preferred_element_type=jnp.float32)
+    up_part = total[:, units : 2 * units] + jnp.dot(
+        low, up_map_ref[...], preferred_element_type=jnp.float32
+    )
+    staged2[...] = (gate_pre / (1.0 + jnp.exp(-gate_pre)) * up_part).astype(jnp.bfloat16)
+    for copy in _start_round("req", n_req, True, staged2, landed2, send2, recv2, local_sems.at[2]):
+        copy.wait()
+    inner = landed2[...].reshape(rows, units)
+    staged3[...] = jnp.dot(inner, down_ref[...], preferred_element_type=jnp.float32).reshape(
+        staged3.shape
+    )
+    for copy in _start_round("seq", n_seq, False, staged3, landed3, send3, recv3, local_sems.at[3]):
+        copy.wait()
+    out_ref[...] = _block_sum(landed3)
+
+
+def fused_mlp(both, gate_weight, up_weight, down_map, gate_map, up_map, down_weight, cid):
+    n_req, n_seq = lax.axis_size("req"), lax.axis_size("seq")
+    group_rows = both.shape[2]
+    rows = n_req * group_rows
+    units = gate_weight.shape[1]
+    wide = 2 * units + down_map.shape[1]
+    out_rows = rows // n_seq
+    vmem = pltpu.VMEM
+    return pl.pallas_call(
+        _mlp_kernel,
+        out_shape=(
+            jax.ShapeDtypeStruct((out_rows, down_weight.shape[1]), jnp.float32),
+            jax.ShapeDtypeStruct(both.shape, both.dtype),
+        ),
+        in_specs=[pl.BlockSpec(memory_space=vmem)] * 7,
+        out_specs=(pl.BlockSpec(memory_space=vmem), pl.BlockSpec(memory_space=vmem)),
+        scratch_shapes=[
+            vmem((n_req, group_rows, wide), jnp.float32),
+            vmem((n_req, group_rows, wide), jnp.float32),
+            vmem((group_rows, units), jnp.bfloat16),
+            vmem((n_req, group_rows, units), jnp.bfloat16),
+            vmem((n_seq, out_rows, down_weight.shape[1]), jnp.float32),
+            vmem((n_seq, out_rows, down_weight.shape[1]), jnp.float32),
+            pltpu.SemaphoreType.DMA((n_req,)),
+            pltpu.SemaphoreType.DMA((n_req,)),
+            pltpu.SemaphoreType.DMA((n_req,)),
+            pltpu.SemaphoreType.DMA((n_req,)),
+            pltpu.SemaphoreType.DMA((n_req,)),
+            pltpu.SemaphoreType.DMA((n_req,)),
+            pltpu.SemaphoreType.DMA((n_seq,)),
+            pltpu.SemaphoreType.DMA((n_seq,)),
+            pltpu.SemaphoreType.DMA((4,)),
+        ],
+        compiler_params=pltpu.CompilerParams(
+            collective_id=cid, has_side_effects=True, vmem_limit_bytes=48 * 1024 * 1024
+        ),
+    )(both, gate_weight, up_weight, down_map, gate_map, up_map, down_weight)
 
 
 def merged_2(array, axis, combine):
@@ -370,42 +451,12 @@
     ).reshape(group_rows, model_width)
     second_normed_state = rms_norm(after_attn, feedforward_norm_gain)
     both = jnp.stack([after_attn, second_normed_state]).reshape(2, group_rows, req_devices, width_share)
-    both_parts = exchange(jnp.transpose(both, (2, 0, 1, 3)), "req", 7)
+    both = jnp.transpose(both, (2, 0, 1, 3))
+    down_sum, both_parts = fused_mlp(
+        both, gate_weight, up_weight, adapter_down_map, adapter_gate_map, adapter_up_map, down_weight, 7
+    )
     residual_cols = both_parts[:, 0].reshape(req_devices * group_rows, width_share)
-    second_spread_state = both_parts[:, 1].reshape(req_devices * group_rows, width_share)
-    units = gate_weight.shape[1]
-    mlp_full = jnp.concatenate(
-        [
-            jnp.dot(second_spread_state, gate_weight, preferred_element_type=jnp.float32),
-            jnp.dot(second_spread_state, up_weight, preferred_element_type=jnp.float32),
-            jnp.dot(second_spread_state, adapter_down_map, preferred_element_type=jnp.float32),
-        ],
-        axis=1,
-    )
-    def activate(landed, gate_map, up_map):
-        total = _block_sum(landed)
-        low = total[:, 2 * units :].astype(jnp.bfloat16)
-        gate_pre = total[:, :units] + jnp.dot(low, gate_map[...], preferred_element_type=jnp.float32)
-        up_part = total[:, units : 2 * units] + jnp.dot(
-            low, up_map[...], preferred_element_type=jnp.float32
-        )
-        return (gate_pre / (1.0 + jnp.exp(-gate_pre)) * up_part).astype(jnp.bfloat16)
-
-    inner_act = two_rounds(
-        mlp_full.reshape(req_devices, group_rows, mlp_full.shape[1]),
-        ("req", False),
-        ("req", True),
-        activate,
-        (group_rows, units),
-        jnp.bfloat16,
-        8,
-        extra=(adapter_gate_map, adapter_up_map),
-    ).reshape(req_devices * group_rows, units)
     out_rows = residual_cols.shape[0] // seq_devices
-    block_rows = inner_act
-    down_full = jnp.dot(block_rows, down_weight, preferred_element_type=jnp.float32)
-    down_parts = exchange(down_full.reshape(seq_devices, out_rows, down_full.shape[1]), "seq", 3)
-    down_sum = jnp.sum(down_parts, axis=0)
     residual_rows = lax.dynamic_slice_in_dim(residual_cols, seq_index * out_rows, out_rows, 0)
     return (residual_rows.astype(jnp.float32) + down_sum).astype(jnp.bfloat16)
 

time: 209 us -> 198 us (0.947)
  Pallas kernels: 139 us -> 132 us
  matrix products: 18.9 us -> 13.6 us
  local copies, waits for them, and re-layouts: 28.9 us -> 32.6 us
    pallas_call x0 -> x1, Pallas kernels: none -> 40.2 us  [fused_mlp(): pl.pallas_call(_mlp_kernel, out_shape=(jax.ShapeDtypeStruct((out_rows, do...]
    pallas_call x5 -> x3, Pallas kernels: 54.8 us -> 28.6 us  [exchange(): pl.pallas_call(functools.partial(_exchange_kernel, axis, n, gather), out_...]
    pallas_call x4 -> x3, Pallas kernels: 84.2 us -> 63.5 us  [two_rounds(): pl.pallas_call(functools.partial(_two_round_kernel, (axis_a, n_a, gather_...]
    dot_general x4 -> x0, matrix products: 5.35 us -> none  [the longest x1 2.78 us: body(): jnp.dot(block_rows, down_weight, preferred_element_type=jnp.float32)]
    unnamed x21 -> x27, local copies, waits for them, and re-layouts: 2.57 us -> 5.86 us
where the time goes in v7:
time: 198 us; the launch traced here: 197 us
  Pallas kernels  132 us (67%)
  local copies, waits for them, and re-layouts  32.6 us (16%)
  other arithmetic  17.8 us (9%)
  matrix products  13.6 us (7%)
    pallas_call x3, Pallas kernels, two_rounds(): pl.pallas_call(functools.partial(_two_round_kernel, (axis_a, n_a, gather_...  63.5 us
    pallas_call x1, Pallas kernels, fused_mlp(): pl.pallas_call(_mlp_kernel, out_shape=(jax.ShapeDtypeStruct((out_rows, do...  40.2 us
    pallas_call x3, Pallas kernels, exchange(): pl.pallas_call(functools.partial(_exchange_kernel, axis, n, gather), out_...  28.6 us
    gather x2, local copies, waits for them, and re-layouts, body(): jnp.take(token_embedding_table, jnp.clip(local_ids, 0, vocab_rows - 1), a...  7.26 us
    unnamed x27, local copies, waits for them, and re-layouts  5.86 us
    dot_general x1, matrix products, body(): jnp.dot(spread_queries.reshape(group_rows * HEADS, head_cols), cache_k.T,...  4.83 us
    dot_general x1, matrix products, body(): jnp.dot(weights.astype(jnp.bfloat16).reshape(group_rows * HEADS, slots *...  4.22 us

profile of v7, /device:TPU:1, one launch (start us, length us, event | category | flops | bytes accessed | tf_op | source)
XLA Modules:
  0.0 197.4 jit_solution(3913704999359932659)
XLA Ops:
  0.0 0.8 compare_and_fusion.1
  0.8 4.9 %gather_fusion = bf16[128,3584]{1,0:T(8,128)(2,1)} fusion(bf16[250,3584]{1,0:T(8,128)(2,1)} %param.19, s32[1024]{0:T(1024)S(1)} %pad_clamp_fusion), kind=kCustom, calls=%fused_computation | custom fusion | bytes 1835520 | tf_op jit(solution)/shard_map/jit(_take)/gather | solution.py:302
  5.7 2.4 %gather.7 = bf16[8,16,28,128]{3,2,1,0:T(8,128)(2,1)} reshape(bf16[128,3584]{1,0:T(8,128)(2,1)} %gather_fusion) | data formatting | bytes 1835008 | tf_op jit(solution)/shard_map/jit(_take)/gather | solution.py:302
  8.3 2.4 %select_convert_fusion.x_ref = bf16[8,16,28,128]{3,2,1,0:T(8,128)(2,1)} fusion(bf16[8,16,28,128]{3,2,1,0:T(8,128)(2,1)} %gather.7, pred[8,16]{1,0:T(8,128)(4,1)S(1)} %broadcast_in_dim.158, pred[8,16]{1,0:T(8,128)(4,1)S(1)} %broadcast_in_dim.156), kind=kLoop, calls=%fused_computation.5 | loop fusion | flops 1835008 | bytes 1835264 | tf_op jit(solution)/shard_map/convert_element_type | solution.py:305
  10.6 27.8 %shard_map.163 = bf16[16,28,128]{2,1,0:T(8,128)(2,1)} custom-call(bf16[8,16,28,128]{3,2,1,0:T(8,128)(2,1)} %select_convert_fusion.x_ref), custom_call_target="tpu_custom_call" | custom-call | tf_op jit(solution)/shard_map/pallas_call | solution.py:121
  38.4 0.9 reduce_sum.89
  39.4 0.9 fusion.35
  40.2 0.7 fusion.34
  40.9 0.7 multiply_reduce_fusion.1
  42.4 0.6 fusion.26.x_ref
  43.0 9.6 %shard_map.164 = bf16[16,56,128]{2,1,0:T(8,128)(2,1)} custom-call(bf16[56,128]{1,0:T(8,128)(2,1)} %fusion.26.x_ref), custom_call_target="tpu_custom_call" | custom-call | tf_op jit(solution)/shard_map/pallas_call | solution.py:54
  52.7 1.2 reshape_reshape.3
  53.9 0.7 copy.150
  54.6 9.1 %shard_map.165 = bf16[8,16,896]{2,1,0:T(8,128)(2,1)} custom-call(bf16[8,16,896]{2,1,0:T(8,128)(2,1)} %bitcast.119), custom_call_target="tpu_custom_call" | custom-call | tf_op jit(solution)/shard_map/pallas_call | solution.py:54
  63.7 2.7 %fusion.4.x_ref = f32[8,16,672]{2,1,0:T(8,128)} fusion(bf16[8,16,896]{2,1,0:T(8,128)(2,1)} %shard_map.165, bf16[896,672]{0,1:T(8,128)(2,1)} %param.21), kind=kOutput, calls=%fused_computation.9 | convolution fusion | flops 154140672 | bytes 1777664 | tf_op jit(solution)/shard_map/dot_general | solution.py:332
  66.4 18.9 %shard_map.166 = bf16[16,16,672]{2,1,0:T(8,128)(2,1)} custom-call(f32[8,16,672]{2,1,0:T(8,128)} %fusion.4.x_ref), custom_call_target="tpu_custom_call" | custom-call | tf_op jit(solution)/shard_map/pallas_call | solution.py:121
  85.3 1.9 copy.90
  87.2 1.5 reshape.403
  88.7 0.8 fusion.36
  89.5 1.1 reshape.412
  90.7 0.7 add_convert_fusion.2
  91.5 0.1 multiply_cosine_fusion
  91.6 0.8 subtract_convert_fusion
  92.4 1.1 reshape.411
  93.6 0.1 multiply_subtract_fusion
  93.7 0.1 maximum_convert_fusion
  93.9 1.1 fusion.10
  95.0 0.2 copy.100
  95.2 0.1 fusion.16
  95.5 0.1 copy.124
  95.7 0.2 convert_element_type.113
  95.9 1.4 broadcast_select_fusion
  97.5 0.2 select_reduce_fusion
  97.9 0.3 fusion.32
  98.4 4.8 %fusion.6 = (f32[256]{0:T(256)S(1)}, f32[256,768]{1,0:T(8,128)S(1)}) fusion(pred[4,768]{1,0:T(4,128)(4,1)S(1)} %fusion.28, bf16[256,3584]{1,0:T(8,128)(2,1)} %bitcast.116, bf16[768,3584]{1,0:T(8,128)(2,1)} %bitcast.117), kind=kOutput, calls=%fused_computation.13 | convolution fusion | flops 1409875712 | bytes 8130560 | tf_op jit(solution)/shard_map/dot_general | solution.py:373
  103.2 0.3 fusion.8
  103.6 4.2 %fusion.3 = f32[16,3584]{1,0:T(8,128)S(1)} fusion(bf16[16,16,768]{2,1,0:T(8,128)(2,1)S(1)} %bitcast.120, bf16[768,3584,1]{1,0,2:T(8,128)(2,1)} %bitcast.132, pred[16,3584]{1,0:T(8,128)(4,1)S(1)} %iota_compare_fusion), kind=kOutput, calls=%fused_computation.7 | convolution fusion | flops 1411063808 | bytes 6184960 | tf_op jit(solution)/shard_map/dot_general | solution.py:384
  107.8 0.9 concatenate.43
  108.7 1.1 copy.94
  109.8 0.8 copy.96
  110.8 0.8 copy.95
  111.7 1.8 maximum_bitcast_fusion.1.x_ref
  113.5 9.8 %shard_map.167 = f32[16,16,256]{2,1,0:T(8,128)} custom-call(f32[16,16,256]{2,1,0:T(8,128)} %maximum_bitcast_fusion.1.x_ref), custom_call_target="tpu_custom_call" | custom-call | tf_op jit(solution)/shard_map/pallas_call | solution.py:54
  123.3 1.0 reshape.407
  124.3 0.9 fusion.37
  125.2 1.1 copy.118
  126.3 1.1 copy.121
  127.4 0.2 fusion.31
  127.8 0.1 fusion.9
  128.0 0.2 copy.106
  128.2 1.1 reshape.408
  129.3 0.2 fusion.14
  129.6 0.5 fusion
  130.2 0.9 copy.111.x_ref
  131.1 16.8 %shard_map.168 = bf16[16,56,128]{2,1,0:T(8,128)(2,1)} custom-call(f32[16,56,128]{2,1,0:T(8,128)} %copy.111.x_ref, bf16[56,128]{1,0:T(8,128)(2,1)} %bitcast.125), custom_call_target="tpu_custom_call" | custom-call | tf_op jit(solution)/shard_map/pallas_call | solution.py:121
  147.9 1.9 stack.6
  149.7 1.1 multiply_reduce_fusion
  150.9 1.2 multiply_convert_fusion
  152.1 1.0 copy.113
  153.2 1.4 copy-done.2
  154.6 0.9 copy-done.4
  155.5 0.9 copy-done.5
  156.5 40.2 %shard_map.169 = (f32[8,896]{1,0:T(8,128)S(1)}, bf16[8,2,16,896]{3,2,1,0:T(8,128)(2,1)S(1)}) custom-call(bf16[8,2,16,896]{3,2,1,0:T(8,128)(2,1)S(1)} %maximum_bitcast_fusion.x_ref, bf16[896,896]{1,0:T(8,128)(2,1)S(1)} %copy-done.1, bf16[896,896]{1,0:T(8,128)(2,1)S(1)} %copy-done.2, bf16[896,128]{1,0:T(8,128)(2,1)S(1)} %copy-done.3, ...), custom_call_target="tpu_custom_call" | custom-call | tf_op jit(solution)/shard_map/pallas_call | solution.py:198
  196.8 0.6 add_convert_fusion.1
  (55 shorter events, 2.0 us)
Async XLA Ops:
  0.0 129.6 %copy-start = (bf16[224,7168]{1,0:T(8,128)(2,1)S(1)}, bf16[224,7168]{1,0:T(8,128)(2,1)}, u32[]{:S(2)}) copy-start(bf16[224,7168]{1,0:T(8,128)(2,1)} %param.26) | copy-start | bytes 9633796
  8.1 34.3 %copy-start.6 = (bf16[7168]{0:T(1024)(128)(2,1)S(1)}, bf16[7168]{0:T(1024)(128)(2,1)}, u32[]{:S(2)}) copy-start(bf16[7168]{0:T(1024)(128)(2,1)} %param.20) | copy-start | bytes 43012
  93.6 3.8 %copy-start.9 = (s32[4]{0:T(128)S(1)}, s32[4]{0:T(128)}, u32[]{:S(2)}) copy-start(s32[4]{0:T(128)} %param.24) | copy-start | bytes 52
  93.6 3.8 %copy-start.8 = (s32[4,48]{1,0:T(4,128)S(1)}, s32[4,48]{1,0:T(4,128)}, u32[]{:S(2)}) copy-start(s32[4,48]{1,0:T(4,128)} %param.25) | copy-start | bytes 2308
  129.6 21.3 %copy-start.7 = (bf16[7168]{0:T(1024)(128)(2,1)S(1)}, bf16[7168]{0:T(1024)(128)(2,1)}, u32[]{:S(2)}) copy-start(bf16[7168]{0:T(1024)(128)(2,1)} %param.27) | copy-start | bytes 43012
  130.2 23.0 %copy-start.3 = (bf16[896,128]{1,0:T(8,128)(2,1)S(1)}, bf16[896,128]{1,0:T(8,128)(2,1)}, u32[]{:S(2)}) copy-start(bf16[896,128]{1,0:T(8,128)(2,1)} %down_map_ref.1) | copy-start | bytes 688132
  150.9 2.2 %copy-start.1 = (bf16[896,896]{1,0:T(8,128)(2,1)S(1)}, bf16[896,896]{1,0:T(8,128)(2,1)}, u32[]{:S(2)}) copy-start(bf16[896,896]{1,0:T(8,128)(2,1)} %gate_ref.1) | copy-start | bytes 4816900
  153.2 1.4 copy-start.2
  154.6 0.9 copy-start.4
  155.5 0.9 copy-start.5

commit v8 on v7

--- a/solution.py
+++ b/solution.py
@@ -226,6 +226,64 @@
     )(both, gate_weight, up_weight, down_map, gate_map, up_map, down_weight)
 
 
+def _chain_kernel(spec, n_extra, x_ref, *refs):
+    extra = refs[:n_extra]
+    y_ref = refs[n_extra]
+    scratch = refs[n_extra + 1 :]
+    count = len(spec)
+    landed = list(scratch[: count - 1]) + [y_ref]
+    staged = scratch[count - 1 : 2 * count - 2]
+    sems = scratch[2 * count - 2 :]
+    axes = []
+    for axis, n, _, _ in spec:
+        if (axis, n) not in axes:
+            axes.append((axis, n))
+    _greet(axes)
+    source = x_ref
+    for k, (axis, n, gather, mid) in enumerate(spec):
+        copies = _start_round(
+            axis, n, gather, source, landed[k], sems[2 * k], sems[2 * k + 1], sems[-1].at[k]
+        )
+        for copy in copies:
+            copy.wait()
+        if mid is not None:
+            staged[k][...] = mid(landed[k], *extra)
+            source = staged[k]
+
+
+def chain(x, rounds, cid, extra=()):
+    spec, landed_shapes, staged_shapes = [], [], []
+    block = (x.shape, x.dtype)
+    for index, (axis, gather, mid, made) in enumerate(rounds):
+        n = lax.axis_size(axis)
+        shape, dtype = block
+        landed = ((n,) + shape if gather else shape, dtype)
+        spec.append((axis, n, gather, mid))
+        if index < len(rounds) - 1:
+            landed_shapes.append(landed)
+            staged_shapes.append(made)
+            block = made
+        else:
+            out = landed
+    sizes = [n for _, n, _, _ in spec]
+    semaphores = []
+    for n in sizes:
+        semaphores += [pltpu.SemaphoreType.DMA((n,)), pltpu.SemaphoreType.DMA((n,))]
+    return pl.pallas_call(
+        functools.partial(_chain_kernel, spec, len(extra)),
+        out_shape=jax.ShapeDtypeStruct(*out),
+        in_specs=[pl.BlockSpec(memory_space=pltpu.VMEM)] * (1 + len(extra)),
+        out_specs=pl.BlockSpec(memory_space=pltpu.VMEM),
+        scratch_shapes=[pltpu.VMEM(*item) for item in landed_shapes]
+        + [pltpu.VMEM(*item) for item in staged_shapes]
+        + semaphores
+        + [pltpu.SemaphoreType.DMA((len(spec),))],
+        compiler_params=pltpu.CompilerParams(
+            collective_id=cid, has_side_effects=True, vmem_limit_bytes=48 * 1024 * 1024
+        ),
+    )(x, *extra)
+
+
 def merged_2(array, axis, combine):
     everything = jax.tree.map(lambda part: lax.all_gather(part, axis), array)
     first = jax.tree.map(lambda part: part[0], everything)
@@ -328,16 +386,27 @@
     )
     width_share = normed.shape[1] // req_devices
     to_owners = jnp.transpose(normed.reshape(group_rows, req_devices, width_share), (1, 0, 2))
-    block_rows = exchange(to_owners, "req", 4).reshape(req_devices * group_rows, width_share)
-    qkv_full = jnp.dot(block_rows, query_key_value_weight, preferred_element_type=jnp.float32)
-    qkv_all = two_rounds(
-        qkv_full.reshape(req_devices, group_rows, qkv_full.shape[1]),
-        ("req", False),
-        ("seq", True),
-        lambda landed: _block_sum(landed).astype(jnp.bfloat16),
-        (group_rows, qkv_full.shape[1]),
-        jnp.bfloat16,
-        5,
+    qkv_cols = query_key_value_weight.shape[1]
+
+    def project(landed, weight):
+        flat = landed[...].reshape(req_devices * group_rows, width_share)
+        product = jnp.dot(flat, weight[...], preferred_element_type=jnp.float32)
+        return product.reshape(req_devices, group_rows, qkv_cols)
+
+    qkv_all = chain(
+        to_owners,
+        [
+            ("req", False, project, ((req_devices, group_rows, qkv_cols), jnp.float32)),
+            (
+                "req",
+                False,
+                lambda landed, weight: _block_sum(landed).astype(jnp.bfloat16),
+                ((group_rows, qkv_cols), jnp.bfloat16),
+            ),
+            ("seq", True, None, None),
+        ],
+        4,
+        extra=(query_key_value_weight,),
     )
     projected = jnp.transpose(qkv_all, (1, 0, 2)).reshape(group_rows, seq_devices * qkv_all.shape[2])
     head_cols = HEADS * HD

time: 198 us -> 196 us (0.990)
  local copies, waits for them, and re-layouts: 32.6 us -> 37.9 us
  Pallas kernels: 132 us -> 127 us
  matrix products: 13.6 us -> 10.9 us
    pallas_call x0 -> x1, Pallas kernels: none -> 23.1 us  [chain(): pl.pallas_call(functools.partial(_chain_kernel, spec, len(extra)), out_sh...]
    pallas_call x3 -> x2, Pallas kernels: 63.5 us -> 43.9 us  [two_rounds(): pl.pallas_call(functools.partial(_two_round_kernel, (axis_a, n_a, gather_...]
    pallas_call x3 -> x2, Pallas kernels: 28.6 us -> 19.3 us  [exchange(): pl.pallas_call(functools.partial(_exchange_kernel, axis, n, gather), out_...]
    unnamed x27 -> x30, local copies, waits for them, and re-layouts: 5.86 us -> 11.2 us
    dot_general x1 -> x0, matrix products: 2.66 us -> none  [body(): jnp.dot(block_rows, query_key_value_weight, preferred_element_type=jnp.fl...]
where the time goes in v8:
time: 196 us; the launch traced here: 195 us
  Pallas kernels  127 us (65%)
  local copies, waits for them, and re-layouts  37.9 us (19%)
  other arithmetic  17.7 us (9%)
  matrix products  10.9 us (6%)
    pallas_call x2, Pallas kernels, two_rounds(): pl.pallas_call(functools.partial(_two_round_kernel, (axis_a, n_a, gather_...  43.9 us
    pallas_call x1, Pallas kernels, fused_mlp(): pl.pallas_call(_mlp_kernel, out_shape=(jax.ShapeDtypeStruct((out_rows, do...  40.7 us
    pallas_call x1, Pallas kernels, chain(): pl.pallas_call(functools.partial(_chain_kernel, spec, len(extra)), out_sh...  23.1 us
    pallas_call x2, Pallas kernels, exchange(): pl.pallas_call(functools.partial(_exchange_kernel, axis, n, gather), out_...  19.3 us
    unnamed x30, local copies, waits for them, and re-layouts  11.2 us
    gather x2, local copies, waits for them, and re-layouts, body(): jnp.take(token_embedding_table, jnp.clip(local_ids, 0, vocab_rows - 1), a...  7.28 us
    dot_general x1, matrix products, body(): jnp.dot(spread_queries.reshape(group_rows * HEADS, head_cols), cache_k.T,...  4.84 us
    dot_general x1, matrix products, body(): jnp.dot(weights.astype(jnp.bfloat16).reshape(group_rows * HEADS, slots *...  4.22 us

profile of v8, /device:TPU:1, one launch (start us, length us, event | category | flops | bytes accessed | tf_op | source)
XLA Modules:
  0.0 194.7 jit_solution(2967375822595369828)
XLA Ops:
  0.0 0.8 compare_and_fusion.1
  0.8 4.9 %gather_fusion = bf16[128,3584]{1,0:T(8,128)(2,1)} fusion(bf16[250,3584]{1,0:T(8,128)(2,1)} %param.19, s32[1024]{0:T(1024)S(1)} %pad_clamp_fusion), kind=kCustom, calls=%fused_computation | custom fusion | bytes 1835520 | tf_op jit(solution)/shard_map/jit(_take)/gather | solution.py:360
  5.7 2.4 %gather.7 = bf16[8,16,28,128]{3,2,1,0:T(8,128)(2,1)} reshape(bf16[128,3584]{1,0:T(8,128)(2,1)} %gather_fusion) | data formatting | bytes 1835008 | tf_op jit(solution)/shard_map/jit(_take)/gather | solution.py:360
  8.3 2.4 %select_convert_fusion.x_ref = bf16[8,16,28,128]{3,2,1,0:T(8,128)(2,1)} fusion(bf16[8,16,28,128]{3,2,1,0:T(8,128)(2,1)} %gather.7, pred[8,16]{1,0:T(8,128)(4,1)S(1)} %broadcast_in_dim.158, pred[8,16]{1,0:T(8,128)(4,1)S(1)} %broadcast_in_dim.156), kind=kLoop, calls=%fused_computation.5 | loop fusion | flops 1835008 | bytes 1835264 | tf_op jit(solution)/shard_map/convert_element_type | solution.py:363
  10.6 27.8 %shard_map.163 = bf16[16,28,128]{2,1,0:T(8,128)(2,1)} custom-call(bf16[8,16,28,128]{3,2,1,0:T(8,128)(2,1)} %select_convert_fusion.x_ref), custom_call_target="tpu_custom_call" | custom-call | tf_op jit(solution)/shard_map/pallas_call | solution.py:121
  38.4 0.9 reduce_sum.89
  39.4 0.9 fusion.33
  40.3 0.7 fusion.32
  41.0 0.7 multiply_reduce_fusion.1
  42.4 0.6 fusion.24.x_ref
  43.1 9.6 %shard_map.164 = bf16[16,56,128]{2,1,0:T(8,128)(2,1)} custom-call(bf16[56,128]{1,0:T(8,128)(2,1)} %fusion.24.x_ref), custom_call_target="tpu_custom_call" | custom-call | tf_op jit(solution)/shard_map/pallas_call | solution.py:54
  52.7 1.9 reshape_reshape.3
  54.6 1.0 copy.155
  55.6 2.6 %copy.94.refs_0_ = bf16[896,672]{1,0:T(8,128)(2,1)} copy(bf16[896,672]{0,1:T(8,128)(2,1)} %param.21) | data formatting | bytes 2408448 | tf_op args[4]
  58.2 1.3 copy-done.1
  59.5 23.1 %shard_map.165 = bf16[16,16,672]{2,1,0:T(8,128)(2,1)S(1)} custom-call(bf16[8,16,896]{2,1,0:T(8,128)(2,1)S(1)} %bitcast.113, bf16[896,672]{1,0:T(8,128)(2,1)S(1)} %copy-done.1), custom_call_target="tpu_custom_call" | custom-call | tf_op jit(solution)/shard_map/pallas_call | solution.py:272
  82.6 0.9 copy.95
  83.5 1.5 reshape.399
  85.0 0.8 fusion.34
  85.8 1.1 reshape.408
  87.1 0.7 add_convert_fusion.2
  87.8 0.1 multiply_cosine_fusion
  88.0 0.8 subtract_convert_fusion
  88.7 1.1 reshape.407
  90.1 0.1 maximum_convert_fusion
  90.2 1.1 fusion.8
  91.4 0.2 copy.105
  91.6 0.1 fusion.14
  91.9 0.1 copy.129
  92.0 0.2 convert_element_type.113
  92.2 1.4 broadcast_select_fusion
  93.8 0.2 select_reduce_fusion
  94.2 0.3 fusion.30
  94.7 4.8 %fusion.4 = (f32[256]{0:T(256)S(1)}, f32[256,768]{1,0:T(8,128)S(1)}) fusion(pred[4,768]{1,0:T(4,128)(4,1)S(1)} %fusion.26, bf16[256,3584]{1,0:T(8,128)(2,1)} %bitcast.114, bf16[768,3584]{1,0:T(8,128)(2,1)} %bitcast.115), kind=kOutput, calls=%fused_computation.11 | convolution fusion | flops 1409875712 | bytes 8130560 | tf_op jit(solution)/shard_map/dot_general | solution.py:442
  99.6 0.3 fusion.6
  99.9 4.2 %fusion.3 = f32[16,3584]{1,0:T(8,128)S(1)} fusion(bf16[16,16,768]{2,1,0:T(8,128)(2,1)S(1)} %bitcast.116, bf16[768,3584,1]{1,0,2:T(8,128)(2,1)} %bitcast.128, pred[16,3584]{1,0:T(8,128)(4,1)S(1)} %iota_compare_fusion), kind=kOutput, calls=%fused_computation.7 | convolution fusion | flops 1411063808 | bytes 6184960 | tf_op jit(solution)/shard_map/dot_general | solution.py:453
  104.1 0.9 concatenate.43
  105.0 1.1 copy.99
  106.2 0.8 copy.101
  107.1 0.8 copy.100
  108.0 1.8 maximum_bitcast_fusion.1.x_ref
  109.8 9.7 %shard_map.166 = f32[16,16,256]{2,1,0:T(8,128)} custom-call(f32[16,16,256]{2,1,0:T(8,128)} %maximum_bitcast_fusion.1.x_ref), custom_call_target="tpu_custom_call" | custom-call | tf_op jit(solution)/shard_map/pallas_call | solution.py:54
  119.5 1.0 reshape.403
  120.5 0.9 fusion.35
  121.4 1.1 copy.123
  122.5 1.1 copy.126
  123.6 0.2 fusion.29
  124.1 0.1 fusion.7
  124.2 0.2 copy.111
  124.4 1.1 reshape.404
  125.5 0.2 fusion.12
  125.9 0.5 fusion
  126.4 0.9 copy.116.x_ref
  127.3 16.1 %shard_map.167 = bf16[16,56,128]{2,1,0:T(8,128)(2,1)} custom-call(f32[16,56,128]{2,1,0:T(8,128)} %copy.116.x_ref, bf16[56,128]{1,0:T(8,128)(2,1)} %bitcast.121), custom_call_target="tpu_custom_call" | custom-call | tf_op jit(solution)/shard_map/pallas_call | solution.py:121
  143.5 1.9 stack.6
  145.3 1.1 multiply_reduce_fusion
  146.5 1.1 multiply_convert_fusion
  147.6 1.0 copy.118
  148.6 1.4 copy-done.2
  150.1 1.4 copy-done.3
  151.5 0.9 copy-done.5
  152.4 0.9 copy-done.6
  153.4 40.7 %shard_map.168 = (f32[8,896]{1,0:T(8,128)S(1)}, bf16[8,2,16,896]{3,2,1,0:T(8,128)(2,1)S(1)}) custom-call(bf16[8,2,16,896]{3,2,1,0:T(8,128)(2,1)S(1)} %maximum_bitcast_fusion.x_ref, bf16[896,896]{1,0:T(8,128)(2,1)S(1)} %copy-done.2, bf16[896,896]{1,0:T(8,128)(2,1)S(1)} %copy-done.3, bf16[896,128]{1,0:T(8,128)(2,1)S(1)} %copy-done.4, ...), custom_call_target="tpu_custom_call" | custom-call | tf_op jit(solution)/shard_map/pallas_call | solution.py:198
  194.1 0.6 add_convert_fusion.1
  (56 shorter events, 2.1 us)
Async XLA Ops:
  0.0 125.8 %copy-start = (bf16[224,7168]{1,0:T(8,128)(2,1)S(1)}, bf16[224,7168]{1,0:T(8,128)(2,1)}, u32[]{:S(2)}) copy-start(bf16[224,7168]{1,0:T(8,128)(2,1)} %param.26) | copy-start | bytes 9633796
  5.7 36.7 %copy-start.7 = (bf16[7168]{0:T(1024)(128)(2,1)S(1)}, bf16[7168]{0:T(1024)(128)(2,1)}, u32[]{:S(2)}) copy-start(bf16[7168]{0:T(1024)(128)(2,1)} %param.20) | copy-start | bytes 43012
  58.2 1.3 copy-start.1
  87.0 6.7 %copy-start.10 = (s32[4]{0:T(128)S(1)}, s32[4]{0:T(128)}, u32[]{:S(2)}) copy-start(s32[4]{0:T(128)} %param.24) | copy-start | bytes 52
  87.0 6.8 %copy-start.9 = (s32[4,48]{1,0:T(4,128)S(1)}, s32[4,48]{1,0:T(4,128)}, u32[]{:S(2)}) copy-start(s32[4,48]{1,0:T(4,128)} %param.25) | copy-start | bytes 2308
  125.5 21.0 %copy-start.8 = (bf16[7168]{0:T(1024)(128)(2,1)S(1)}, bf16[7168]{0:T(1024)(128)(2,1)}, u32[]{:S(2)}) copy-start(bf16[7168]{0:T(1024)(128)(2,1)} %param.27) | copy-start | bytes 43012
  125.9 22.8 %copy-start.4 = (bf16[896,128]{1,0:T(8,128)(2,1)S(1)}, bf16[896,128]{1,0:T(8,128)(2,1)}, u32[]{:S(2)}) copy-start(bf16[896,128]{1,0:T(8,128)(2,1)} %down_map_ref.1) | copy-start | bytes 688132
  148.6 1.4 copy-start.2
  150.1 1.4 copy-start.3
  151.5 0.9 copy-start.5
  152.4 0.9 copy-start.6

commit v9 on v8

--- a/solution.py
+++ b/solution.py
@@ -282,6 +282,61 @@
             collective_id=cid, has_side_effects=True, vmem_limit_bytes=48 * 1024 * 1024
         ),
     )(x, *extra)
+
+
+def _embed_kernel(
+    x_a, x_b, out_a, out_b, landed_a, landed_b, staged_a, staged_b, arrived_a, arrived_b,
+    send_a, recv_a, send_b, recv_b, send_c, recv_c, send_d, recv_d, local_sems,
+):
+    n_req, n_seq = landed_a.shape[0], landed_b.shape[0]
+    _greet([("req", n_req), ("seq", n_seq)])
+    first = _start_round("req", n_req, False, x_a, landed_a, send_a, recv_a, local_sems.at[0])
+    first += _start_round("seq", n_seq, False, x_b, landed_b, send_b, recv_b, local_sems.at[1])
+    for copy in first:
+        copy.wait()
+    staged_a[...] = _block_sum(landed_a).astype(staged_a.dtype)
+    staged_b[...] = _block_sum(landed_b).astype(staged_b.dtype)
+    second = _start_round("seq", n_seq, False, staged_a, arrived_a, send_c, recv_c, local_sems.at[2])
+    second += _start_round("req", n_req, False, staged_b, arrived_b, send_d, recv_d, local_sems.at[3])
+    for copy in second:
+        copy.wait()
+    out_a[...] = _block_sum(arrived_a)
+    out_b[...] = _block_sum(arrived_b)
+
+
+def embed_rows(x_a, x_b, cid):
+    n_req, n_seq = x_a.shape[0], x_b.shape[0]
+    block_a, block_b = x_a.shape[2:], x_b.shape[2:]
+    vmem = pltpu.VMEM
+    return pl.pallas_call(
+        _embed_kernel,
+        out_shape=(
+            jax.ShapeDtypeStruct(block_a, jnp.float32),
+            jax.ShapeDtypeStruct(block_b, jnp.float32),
+        ),
+        in_specs=[pl.BlockSpec(memory_space=vmem)] * 2,
+        out_specs=(pl.BlockSpec(memory_space=vmem), pl.BlockSpec(memory_space=vmem)),
+        scratch_shapes=[
+            vmem(x_a.shape, x_a.dtype),
+            vmem(x_b.shape, x_b.dtype),
+            vmem(x_a.shape[1:], x_a.dtype),
+            vmem(x_b.shape[1:], x_b.dtype),
+            vmem((n_seq,) + block_a, x_a.dtype),
+            vmem((n_req,) + block_b, x_b.dtype),
+            pltpu.SemaphoreType.DMA((n_req,)),
+            pltpu.SemaphoreType.DMA((n_req,)),
+            pltpu.SemaphoreType.DMA((n_seq,)),
+            pltpu.SemaphoreType.DMA((n_seq,)),
+            pltpu.SemaphoreType.DMA((n_seq,)),
+            pltpu.SemaphoreType.DMA((n_seq,)),
+            pltpu.SemaphoreType.DMA((n_req,)),
+            pltpu.SemaphoreType.DMA((n_req,)),
+            pltpu.SemaphoreType.DMA((4,)),
+        ],
+        compiler_params=pltpu.CompilerParams(
+            collective_id=cid, has_side_effects=True, vmem_limit_bytes=48 * 1024 * 1024
+        ),
+    )(x_a, x_b)
 
 
 def merged_2(array, axis, combine):
@@ -363,21 +418,16 @@
     looked = jnp.where(present[:, None], looked, 0.0).astype(jnp.bfloat16)
     row_share = group_rows // seq_devices
     lanes = 128
-    by_group = looked.reshape(req_devices, seq_devices, row_share * looked.shape[1] // lanes, lanes)
-    row_parts = two_rounds(
-        by_group,
-        ("req", False),
-        ("seq", False),
-        lambda landed: _block_sum(landed).astype(jnp.bfloat16),
-        by_group.shape[1:],
-        jnp.bfloat16,
-        10,
-    )
-    embedded_rows = (
-        jnp.sum(row_parts.astype(jnp.float32), axis=0)
-        .astype(jnp.bfloat16)
-        .reshape(row_share, looked.shape[1])
-    )
+    half = looked.shape[1] // 2
+    per_row = looked.reshape(req_devices, seq_devices, row_share, looked.shape[1])
+    x_a = per_row[..., :half].reshape(req_devices, seq_devices, row_share * half // lanes, lanes)
+    x_b = jnp.transpose(per_row[..., half:], (1, 0, 2, 3)).reshape(
+        seq_devices, req_devices, row_share * half // lanes, lanes
+    )
+    sum_a, sum_b = embed_rows(x_a, x_b, 10)
+    embedded_rows = jnp.concatenate(
+        [sum_a.reshape(row_share, half), sum_b.reshape(row_share, half)], axis=1
+    ).astype(jnp.bfloat16)
     own_hidden = lax.dynamic_slice_in_dim(hidden, seq_index * row_share, row_share, 0)
     own_rows = jnp.concatenate([own_hidden, embedded_rows], axis=1)
     normed_rows = rms_norm(own_rows, attention_norm_gain)

time: 196 us -> 201 us (1.026)
  local copies, waits for them, and re-layouts: 37.9 us -> 44.2 us
  Pallas kernels: 127 us -> 121 us
  other arithmetic: 17.7 us -> 23.1 us
    pallas_call x2 -> x1, Pallas kernels: 43.9 us -> 16.7 us  [two_rounds(): pl.pallas_call(functools.partial(_two_round_kernel, (axis_a, n_a, gather_...]
    pallas_call x0 -> x1, Pallas kernels: none -> 21.3 us  [embed_rows(): pl.pallas_call(_embed_kernel, out_shape=(jax.ShapeDtypeStruct(block_a, jn...]
    reshape x0 -> x4, local copies, waits for them, and re-layouts: none -> 5 us  [the longest x2 3.26 us: body(): per_row[..., :half]]
    gather x2 -> x1, local copies, waits for them, and re-layouts: 7.28 us -> 4.69 us  [body(): jnp.take(token_embedding_table, jnp.clip(local_ids, 0, vocab_rows - 1), a...]
    dot_general x1, matrix products: 4.22 us -> 1.65 us  [body(): jnp.dot(weights.astype(jnp.bfloat16).reshape(group_rows * HEADS, slots *...]
    unnamed x30 -> x41, local copies, waits for them, and re-layouts: 11.2 us -> 12.3 us
where the time goes in v9:
time: 201 us; the launch traced here: 199 us
  Pallas kernels  121 us (60%)
  local copies, waits for them, and re-layouts  44.2 us (22%)
  other arithmetic  23.1 us (11%)
  matrix products  9.49 us (5%)
    pallas_call x1, Pallas kernels, fused_mlp(): pl.pallas_call(_mlp_kernel, out_shape=(jax.ShapeDtypeStruct((out_rows, do...  41 us
    pallas_call x1, Pallas kernels, chain(): pl.pallas_call(functools.partial(_chain_kernel, spec, len(extra)), out_sh...  23.9 us
    pallas_call x1, Pallas kernels, embed_rows(): pl.pallas_call(_embed_kernel, out_shape=(jax.ShapeDtypeStruct(block_a, jn...  21.3 us
    pallas_call x2, Pallas kernels, exchange(): pl.pallas_call(functools.partial(_exchange_kernel, axis, n, gather), out_...  18.6 us
    pallas_call x1, Pallas kernels, two_rounds(): pl.pallas_call(functools.partial(_two_round_kernel, (axis_a, n_a, gather_...  16.7 us
    unnamed x41, local copies, waits for them, and re-layouts  12.3 us
    gather x1, local copies, waits for them, and re-layouts, body(): jnp.take(token_embedding_table, jnp.clip(local_ids, 0, vocab_rows - 1), a...  4.69 us
    concatenate x7, local copies, waits for them, and re-layouts, body(): jnp.concatenate([local_out, local_max[..., None], local_sum[..., None], j...  4.44 us

profile of v9, /device:TPU:1, one launch (start us, length us, event | category | flops | bytes accessed | tf_op | source)
XLA Modules:
  0.0 199.4 jit_solution(13632785488082039215)
XLA Ops:
  0.5 0.9 and_select_fusion
  1.5 0.7 pad.10.clone
  2.2 0.9 fusion.32
  3.3 0.7 compare_and_fusion.1
  4.3 0.7 add_convert_fusion.2
  5.0 0.9 select_reduce_fusion
  6.2 0.7 multiply_cosine_fusion
  7.0 1.3 fusion.28
  8.3 0.9 fusion.34
  9.2 1.4 reshape.500
  10.5 0.6 iota_compare_fusion
  11.2 4.7 %gather_fusion = bf16[128,3584]{1,0:T(8,128)(2,1)} fusion(bf16[250,3584]{1,0:T(8,128)(2,1)} %param.19, s32[1024]{0:T(1024)S(1)} %pad_clamp_fusion), kind=kCustom, calls=%fused_computation | custom fusion | bytes 1835520 | tf_op jit(solution)/shard_map/jit(_take)/gather | solution.py:415
  15.9 1.9 select_convert_fusion
  17.8 0.8 slice_bitcast_fusion
  18.6 0.9 copy.116.x_b
  19.5 2.2 %reshape.512 = bf16[8,16,14,128]{3,2,0,1:T(8,128)(2,1)} reshape(bf16[8,16,1,1792]{3,0,1,2:T(8,128)(2,1)} %get-tuple-element.20) | data formatting | bytes 917504 | tf_op jit(solution)/shard_map/reshape | solution.py:423
  21.7 1.1 copy.143.x_a
  22.8 1.0 copy-done.2
  23.8 21.3 %shard_map.163 = (f32[14,128]{1,0:T(8,128)S(1)}, f32[14,128]{1,0:T(8,128)S(1)}) custom-call(bf16[8,16,14,128]{3,2,1,0:T(8,128)(2,1)S(1)} %copy.143.x_a, bf16[16,8,14,128]{3,2,1,0:T(8,128)(2,1)S(1)} %copy-done.2), custom_call_target="tpu_custom_call" | custom-call | tf_op jit(solution)/shard_map/pallas_call | solution.py:311
  45.2 0.7 maximum_reduce_fusion
  45.9 0.7 fusion.18
  47.2 0.6 fusion.26.x_ref
  47.9 9.3 %shard_map.164 = bf16[16,56,128]{2,1,0:T(8,128)(2,1)} custom-call(bf16[56,128]{1,0:T(8,128)(2,1)} %fusion.26.x_ref), custom_call_target="tpu_custom_call" | custom-call | tf_op jit(solution)/shard_map/pallas_call | solution.py:54
  57.1 1.9 reshape_reshape.3
  59.0 1.0 copy.185
  60.0 2.6 %copy.118.refs_0_ = bf16[896,672]{1,0:T(8,128)(2,1)} copy(bf16[896,672]{0,1:T(8,128)(2,1)} %param.21) | data formatting | bytes 2408448 | tf_op args[4]
  62.6 1.3 copy-done.1
  63.9 23.9 %shard_map.165 = bf16[16,16,672]{2,1,0:T(8,128)(2,1)S(1)} custom-call(bf16[8,16,896]{2,1,0:T(8,128)(2,1)S(1)} %bitcast.132, bf16[896,672]{1,0:T(8,128)(2,1)S(1)} %copy-done.1), custom_call_target="tpu_custom_call" | custom-call | tf_op jit(solution)/shard_map/pallas_call | solution.py:272
  87.8 0.9 copy.119
  88.7 1.5 reshape.490
  90.2 0.8 fusion.35
  91.0 1.8 reshape.495
  92.8 1.1 reshape.499
  94.0 1.4 subtract_convert_fusion
  95.4 1.1 reshape.498
  96.7 0.8 multiply_subtract_fusion
  97.6 1.1 fusion.8
  99.9 1.8 fusion.12
  101.8 1.2 broadcast_select_fusion
  103.0 4.4 %fusion.4 = (f32[256]{0:T(256)S(1)}, f32[256,768]{1,0:T(8,128)S(1)}) fusion(pred[4,768]{1,0:T(4,128)(4,1)S(1)} %copy-done.10, bf16[256,3584]{1,0:T(8,128)(2,1)S(1)} %bitcast.133, bf16[768,3584]{1,0:T(8,128)(2,1)} %bitcast.134), kind=kOutput, calls=%fused_computation.12 | convolution fusion | flops 1409875712 | bytes 8130560 | tf_op jit(solution)/shard_map/dot_general | solution.py:492
  107.7 1.7 fusion.3
  109.5 0.9 concatenate.75
  110.4 1.1 copy.123
  111.5 0.8 copy.125
  112.3 0.8 copy.124
  113.1 1.8 maximum_bitcast_fusion.1.x_ref
  114.9 9.3 %shard_map.166 = f32[16,16,256]{2,1,0:T(8,128)} custom-call(f32[16,16,256]{2,1,0:T(8,128)} %maximum_bitcast_fusion.1.x_ref), custom_call_target="tpu_custom_call" | custom-call | tf_op jit(solution)/shard_map/pallas_call | solution.py:54
  124.3 1.0 reshape.494
  125.3 0.9 fusion.36
  126.3 1.1 copy.151
  127.3 1.1 copy.148
  128.9 0.8 fusion.25
  130.3 0.9 copy.140.x_ref
  131.2 16.7 %shard_map.167 = bf16[16,56,128]{2,1,0:T(8,128)(2,1)} custom-call(f32[16,56,128]{2,1,0:T(8,128)} %copy.140.x_ref, bf16[56,128]{1,0:T(8,128)(2,1)} %bitcast.138), custom_call_target="tpu_custom_call" | custom-call | tf_op jit(solution)/shard_map/pallas_call | solution.py:121
  147.9 1.1 multiply_reduce_fusion
  149.1 1.9 stack.6
  150.9 1.1 multiply_convert_fusion
  152.0 1.0 copy.142
  153.0 1.4 copy-done.3
  154.4 1.4 copy-done.4
  155.9 0.9 copy-done.6
  156.8 0.9 copy-done.7
  157.7 41.0 %shard_map.168 = (f32[8,896]{1,0:T(8,128)S(1)}, bf16[8,2,16,896]{3,2,1,0:T(8,128)(2,1)S(1)}) custom-call(bf16[8,2,16,896]{3,2,1,0:T(8,128)(2,1)S(1)} %maximum_bitcast_fusion.x_ref, bf16[896,896]{1,0:T(8,128)(2,1)S(1)} %copy-done.3, bf16[896,896]{1,0:T(8,128)(2,1)S(1)} %copy-done.4, bf16[896,128]{1,0:T(8,128)(2,1)S(1)} %copy-done.5, ...), custom_call_target="tpu_custom_call" | custom-call | tf_op jit(solution)/shard_map/pallas_call | solution.py:198
  198.8 0.6 add_convert_fusion.1
  (76 shorter events, 4.5 us)
Async XLA Ops:
  0.0 129.8 %copy-start = (bf16[224,7168]{1,0:T(8,128)(2,1)S(1)}, bf16[224,7168]{1,0:T(8,128)(2,1)}, u32[]{:S(2)}) copy-start(bf16[224,7168]{1,0:T(8,128)(2,1)} %param.26) | copy-start | bytes 9633796
  17.7 29.5 %copy-start.11 = (bf16[7168]{0:T(1024)(128)(2,1)S(1)}, bf16[7168]{0:T(1024)(128)(2,1)}, u32[]{:S(2)}) copy-start(bf16[7168]{0:T(1024)(128)(2,1)} %param.20) | copy-start | bytes 43012
  22.8 1.0 copy-start.2
  62.6 1.3 copy-start.1
  91.0 8.1 %copy-start.13 = (pred[4,4]{1,0:T(4,128)(4,1)S(1)}, pred[4,4]{1,0:T(4,128)(4,1)}, u32[]{:S(2)}) copy-start(pred[4,4]{1,0:T(4,128)(4,1)} %iota_compare_fusion.1) | copy-start | bytes 52
  94.0 8.9 %copy-start.10 = (pred[4,768]{1,0:T(4,128)(4,1)S(1)}, pred[4,768]{1,0:T(4,128)(4,1)}, u32[]{:S(2)}) copy-start(pred[4,768]{1,0:T(4,128)(4,1)} %fusion.28) | copy-start | bytes 9220
  101.8 5.9 %slice-start = ((s8[5505024]{0:T(1024)(128)(4,1)}), s8[4194304]{0:T(1024)(128)(4,1)S(1)}, s32[]{:S(2)}) async-start(s8[5505024]{0:T(1024)(128)(4,1)} %bitcast.147), calls=%async_computation | async-start | bytes 8388608
  102.9 4.7 %copy-start.8 = (pred[16,3584]{1,0:T(8,128)(4,1)S(1)}, pred[16,3584]{1,0:T(8,128)(4,1)}, u32[]{:S(2)}) copy-start(pred[16,3584]{1,0:T(8,128)(4,1)} %iota_compare_fusion) | copy-start | bytes 172036
  102.9 4.7 %slice-start.1 = ((s8[5505024]{0:T(1024)(128)(4,1)}), s8[1310720]{0:T(1024)(128)(4,1)S(1)}, s32[]{:S(2)}) async-start(s8[5505024]{0:T(1024)(128)(4,1)} %bitcast.147), calls=%async_computation.1 | async-start | bytes 2621440
  107.7 5.5 %copy-start.12 = (f32[256]{0:T(256)S(1)}, f32[256]{0:T(256)}, u32[]{:S(2)}) copy-start(f32[256]{0:T(256)} %pad.10.clone) | copy-start | bytes 3076
  128.7 22.3 %copy-start.9 = (f32[8,896]{1,0:T(8,128)S(1)}, f32[8,896]{1,0:T(8,128)}, u32[]{:S(2)}) copy-start(f32[8,896]{1,0:T(8,128)} %reshape.500) | copy-start | bytes 86020
  129.8 23.2 %copy-start.5 = (bf16[896,128]{1,0:T(8,128)(2,1)S(1)}, bf16[896,128]{1,0:T(8,128)(2,1)}, u32[]{:S(2)}) copy-start(bf16[896,128]{1,0:T(8,128)(2,1)} %down_map_ref.1) | copy-start | bytes 688132
  153.0 1.4 copy-start.3
  154.4 1.4 copy-start.4
  155.9 0.9 copy-start.6
  156.8 0.9 copy-start.7

commit v10 on v8

--- a/solution.py
+++ b/solution.py
@@ -146,17 +146,29 @@
 
 
 def _mlp_kernel(
-    x_ref, gate_ref, up_ref, down_map_ref, gate_map_ref, up_map_ref, down_ref,
+    x_ref, gate_hbm, up_hbm, down_map_hbm, gate_map_hbm, up_map_hbm, down_hbm,
     out_ref, spread_ref, landed1, staged1, staged2, landed2, staged3, landed3,
     send0, recv0, send1, recv1, send2, recv2, send3, recv3, local_sems,
+    gate_ref, up_ref, down_map_ref, gate_map_ref, up_map_ref, down_ref, weight_sems,
 ):
     n_req = spread_ref.shape[0]
     n_seq = landed3.shape[0]
     rows = n_req * spread_ref.shape[2]
     units = gate_ref.shape[1]
+    loads = []
+    pairs = (
+        (gate_hbm, gate_ref), (up_hbm, up_ref), (down_map_hbm, down_map_ref),
+        (gate_map_hbm, gate_map_ref), (up_map_hbm, up_map_ref), (down_hbm, down_ref),
+    )
+    for index, (source, target) in enumerate(pairs):
+        load = pltpu.make_async_copy(source, target, weight_sems.at[index])
+        load.start()
+        loads.append(load)
     _greet([("req", n_req), ("seq", n_seq)])
     for copy in _start_round("req", n_req, False, x_ref, spread_ref, send0, recv0, local_sems.at[0]):
         copy.wait()
+    for load in loads[:3]:
+        load.wait()
     normed_all = spread_ref[:, 1].reshape(rows, spread_ref.shape[3])
     staged1[:, :, :units] = jnp.dot(
         normed_all, gate_ref[...], preferred_element_type=jnp.float32
@@ -169,6 +181,8 @@
     ).reshape(staged1.shape[0], staged1.shape[1], staged1.shape[2] - 2 * units)
     for copy in _start_round("req", n_req, False, staged1, landed1, send1, recv1, local_sems.at[1]):
         copy.wait()
+    for load in loads[3:5]:
+        load.wait()
     total = _block_sum(landed1)
     low = total[:, 2 * units :].astype(jnp.bfloat16)
     gate_pre = total[:, :units] + jnp.dot(low, gate_map_ref[...], preferred_element_type=jnp.float32)
@@ -178,6 +192,7 @@
     staged2[...] = (gate_pre / (1.0 + jnp.exp(-gate_pre)) * up_part).astype(jnp.bfloat16)
     for copy in _start_round("req", n_req, True, staged2, landed2, send2, recv2, local_sems.at[2]):
         copy.wait()
+    loads[5].wait()
     inner = landed2[...].reshape(rows, units)
     staged3[...] = jnp.dot(inner, down_ref[...], preferred_element_type=jnp.float32).reshape(
         staged3.shape
@@ -201,7 +216,7 @@
             jax.ShapeDtypeStruct((out_rows, down_weight.shape[1]), jnp.float32),
             jax.ShapeDtypeStruct(both.shape, both.dtype),
         ),
-        in_specs=[pl.BlockSpec(memory_space=vmem)] * 7,
+        in_specs=[pl.BlockSpec(memory_space=vmem)] + [pl.BlockSpec(memory_space=pl.ANY)] * 6,
         out_specs=(pl.BlockSpec(memory_space=vmem), pl.BlockSpec(memory_space=vmem)),
         scratch_shapes=[
             vmem((n_req, group_rows, wide), jnp.float32),
@@ -219,7 +234,12 @@
             pltpu.SemaphoreType.DMA((n_seq,)),
             pltpu.SemaphoreType.DMA((n_seq,)),
             pltpu.SemaphoreType.DMA((4,)),
-        ],
+        ]
+        + [
+            vmem(weight.shape, weight.dtype)
+            for weight in (gate_weight, up_weight, down_map, gate_map, up_map, down_weight)
+        ]
+        + [pltpu.SemaphoreType.DMA((6,))],
         compiler_params=pltpu.CompilerParams(
             collective_id=cid, has_side_effects=True, vmem_limit_bytes=48 * 1024 * 1024
         ),
@@ -227,13 +247,20 @@
 
 
 def _chain_kernel(spec, n_extra, x_ref, *refs):
-    extra = refs[:n_extra]
+    extra_hbm = refs[:n_extra]
     y_ref = refs[n_extra]
     scratch = refs[n_extra + 1 :]
     count = len(spec)
     landed = list(scratch[: count - 1]) + [y_ref]
     staged = scratch[count - 1 : 2 * count - 2]
-    sems = scratch[2 * count - 2 :]
+    extra = scratch[2 * count - 2 : 2 * count - 2 + n_extra]
+    extra_sems = scratch[2 * count - 2 + n_extra]
+    sems = scratch[2 * count - 1 + n_extra :]
+    loads = []
+    for index in range(n_extra):
+        load = pltpu.make_async_copy(extra_hbm[index], extra[index], extra_sems.at[index])
+        load.start()
+        loads.append(load)
     axes = []
     for axis, n, _, _ in spec:
         if (axis, n) not in axes:
@@ -246,6 +273,9 @@
         )
         for copy in copies:
             copy.wait()
+        if k == 0:
+            for load in loads:
+                load.wait()
         if mid is not None:
             staged[k][...] = mid(landed[k], *extra)
             source = staged[k]
@@ -272,10 +302,13 @@
     return pl.pallas_call(
         functools.partial(_chain_kernel, spec, len(extra)),
         out_shape=jax.ShapeDtypeStruct(*out),
-        in_specs=[pl.BlockSpec(memory_space=pltpu.VMEM)] * (1 + len(extra)),
+        in_specs=[pl.BlockSpec(memory_space=pltpu.VMEM)]
+        + [pl.BlockSpec(memory_space=pl.ANY)] * len(extra),
         out_specs=pl.BlockSpec(memory_space=pltpu.VMEM),
         scratch_shapes=[pltpu.VMEM(*item) for item in landed_shapes]
         + [pltpu.VMEM(*item) for item in staged_shapes]
+        + [pltpu.VMEM(item.shape, item.dtype) for item in extra]
+        + [pltpu.SemaphoreType.DMA((max(len(extra), 1),))]
         + semaphores
         + [pltpu.SemaphoreType.DMA((len(spec),))],
         compiler_params=pltpu.CompilerParams(

time: 196 us -> 196 us (level)
  no operation moved by 1% of the time
where the time goes in v10:
time: 196 us; the launch traced here: 195 us
  Pallas kernels  127 us (65%)
  local copies, waits for them, and re-layouts  37.9 us (19%)
  other arithmetic  17.7 us (9%)
  matrix products  10.9 us (6%)
    pallas_call x2, Pallas kernels, two_rounds(): pl.pallas_call(functools.partial(_two_round_kernel, (axis_a, n_a, gather_...  44.2 us
    pallas_call x1, Pallas kernels, fused_mlp(): pl.pallas_call(_mlp_kernel, out_shape=(jax.ShapeDtypeStruct((out_rows, do...  40.4 us
    pallas_call x1, Pallas kernels, chain(): pl.pallas_call(functools.partial(_chain_kernel, spec, len(extra)), out_sh...  23.5 us
    pallas_call x2, Pallas kernels, exchange(): pl.pallas_call(functools.partial(_exchange_kernel, axis, n, gather), out_...  19.2 us
    unnamed x30, local copies, waits for them, and re-layouts  11.2 us
    gather x2, local copies, waits for them, and re-layouts, body(): jnp.take(token_embedding_table, jnp.clip(local_ids, 0, vocab_rows - 1), a...  7.28 us
    dot_general x1, matrix products, body(): jnp.dot(spread_queries.reshape(group_rows * HEADS, head_cols), cache_k.T,...  4.83 us
    dot_general x1, matrix products, body(): jnp.dot(weights.astype(jnp.bfloat16).reshape(group_rows * HEADS, slots *...  4.22 us

profile of v10, /device:TPU:1, one launch (start us, length us, event | category | flops | bytes accessed | tf_op | source)
XLA Modules:
  0.0 195.0 jit_solution(8015233646957149837)
XLA Ops:
  0.0 0.8 compare_and_fusion.1
  0.8 4.9 %gather_fusion = bf16[128,3584]{1,0:T(8,128)(2,1)} fusion(bf16[250,3584]{1,0:T(8,128)(2,1)} %param.19, s32[1024]{0:T(1024)S(1)} %pad_clamp_fusion), kind=kCustom, calls=%fused_computation | custom fusion | bytes 1835520 | tf_op jit(solution)/shard_map/jit(_take)/gather | solution.py:393
  5.7 2.4 %gather.7 = bf16[8,16,28,128]{3,2,1,0:T(8,128)(2,1)} reshape(bf16[128,3584]{1,0:T(8,128)(2,1)} %gather_fusion) | data formatting | bytes 1835008 | tf_op jit(solution)/shard_map/jit(_take)/gather | solution.py:393
  8.3 2.4 %select_convert_fusion.x_ref = bf16[8,16,28,128]{3,2,1,0:T(8,128)(2,1)} fusion(bf16[8,16,28,128]{3,2,1,0:T(8,128)(2,1)} %gather.7, pred[8,16]{1,0:T(8,128)(4,1)S(1)} %broadcast_in_dim.158, pred[8,16]{1,0:T(8,128)(4,1)S(1)} %broadcast_in_dim.156), kind=kLoop, calls=%fused_computation.5 | loop fusion | flops 1835008 | bytes 1835264 | tf_op jit(solution)/shard_map/convert_element_type | solution.py:396
  10.6 27.8 %shard_map.163 = bf16[16,28,128]{2,1,0:T(8,128)(2,1)} custom-call(bf16[8,16,28,128]{3,2,1,0:T(8,128)(2,1)} %select_convert_fusion.x_ref), custom_call_target="tpu_custom_call" | custom-call | tf_op jit(solution)/shard_map/pallas_call | solution.py:121
  38.4 0.9 reduce_sum.89
  39.4 0.9 fusion.33
  40.3 0.7 fusion.32
  41.0 0.7 multiply_reduce_fusion.1
  42.4 0.6 fusion.24.x_ref
  43.1 9.6 %shard_map.164 = bf16[16,56,128]{2,1,0:T(8,128)(2,1)} custom-call(bf16[56,128]{1,0:T(8,128)(2,1)} %fusion.24.x_ref), custom_call_target="tpu_custom_call" | custom-call | tf_op jit(solution)/shard_map/pallas_call | solution.py:54
  52.7 1.9 reshape_reshape.3
  54.6 1.0 copy.155
  55.6 2.6 %copy.94.refs_0_ = bf16[896,672]{1,0:T(8,128)(2,1)} copy(bf16[896,672]{0,1:T(8,128)(2,1)} %param.21) | data formatting | bytes 2408448 | tf_op args[4]
  58.2 1.3 copy-done.1
  59.5 23.5 %shard_map.165 = bf16[16,16,672]{2,1,0:T(8,128)(2,1)S(1)} custom-call(bf16[8,16,896]{2,1,0:T(8,128)(2,1)S(1)} %bitcast.113, bf16[896,672]{1,0:T(8,128)(2,1)S(1)} %copy-done.1), custom_call_target="tpu_custom_call" | custom-call | tf_op jit(solution)/shard_map/pallas_call | solution.py:302
  83.0 0.9 copy.95
  83.8 1.5 reshape.399
  85.4 0.8 fusion.34
  86.2 1.1 reshape.408
  87.4 0.7 add_convert_fusion.2
  88.2 0.1 multiply_cosine_fusion
  88.3 0.8 subtract_convert_fusion
  89.1 1.1 reshape.407
  90.4 0.1 maximum_convert_fusion
  90.6 1.1 fusion.8
  91.7 0.2 copy.105
  91.9 0.1 fusion.14
  92.2 0.1 copy.129
  92.3 0.2 convert_element_type.113
  92.6 1.4 broadcast_select_fusion
  94.1 0.2 select_reduce_fusion
  94.6 0.3 fusion.30
  95.1 4.8 %fusion.4 = (f32[256]{0:T(256)S(1)}, f32[256,768]{1,0:T(8,128)S(1)}) fusion(pred[4,768]{1,0:T(4,128)(4,1)S(1)} %fusion.26, bf16[256,3584]{1,0:T(8,128)(2,1)} %bitcast.114, bf16[768,3584]{1,0:T(8,128)(2,1)} %bitcast.115), kind=kOutput, calls=%fused_computation.11 | convolution fusion | flops 1409875712 | bytes 8130560 | tf_op jit(solution)/shard_map/dot_general | solution.py:475
  99.9 0.3 fusion.6
  100.2 4.2 %fusion.3 = f32[16,3584]{1,0:T(8,128)S(1)} fusion(bf16[16,16,768]{2,1,0:T(8,128)(2,1)S(1)} %bitcast.116, bf16[768,3584,1]{1,0,2:T(8,128)(2,1)} %bitcast.128, pred[16,3584]{1,0:T(8,128)(4,1)S(1)} %iota_compare_fusion), kind=kOutput, calls=%fused_computation.7 | convolution fusion | flops 1411063808 | bytes 6184960 | tf_op jit(solution)/shard_map/dot_general | solution.py:486
  104.5 0.9 concatenate.43
  105.3 1.1 copy.99
  106.5 0.8 copy.101
  107.4 0.8 copy.100
  108.3 1.8 maximum_bitcast_fusion.1.x_ref
  110.1 9.6 %shard_map.166 = f32[16,16,256]{2,1,0:T(8,128)} custom-call(f32[16,16,256]{2,1,0:T(8,128)} %maximum_bitcast_fusion.1.x_ref), custom_call_target="tpu_custom_call" | custom-call | tf_op jit(solution)/shard_map/pallas_call | solution.py:54
  119.7 1.0 reshape.403
  120.8 0.9 fusion.35
  121.7 1.1 copy.123
  122.8 1.1 copy.126
  123.8 0.2 fusion.29
  124.3 0.1 fusion.7
  124.5 0.2 copy.111
  124.7 1.1 reshape.404
  125.8 0.2 fusion.12
  126.1 0.5 fusion
  126.6 0.9 copy.116.x_ref
  127.6 16.4 %shard_map.167 = bf16[16,56,128]{2,1,0:T(8,128)(2,1)} custom-call(f32[16,56,128]{2,1,0:T(8,128)} %copy.116.x_ref, bf16[56,128]{1,0:T(8,128)(2,1)} %bitcast.121), custom_call_target="tpu_custom_call" | custom-call | tf_op jit(solution)/shard_map/pallas_call | solution.py:121
  144.0 1.9 stack.6
  145.9 1.1 multiply_reduce_fusion
  147.1 1.1 multiply_convert_fusion
  148.1 1.0 copy.118
  149.2 1.4 copy-done.2
  150.6 1.4 copy-done.3
  152.0 0.9 copy-done.5
  153.0 0.9 copy-done.6
  153.9 40.4 %shard_map.168 = (f32[8,896]{1,0:T(8,128)S(1)}, bf16[8,2,16,896]{3,2,1,0:T(8,128)(2,1)S(1)}) custom-call(bf16[8,2,16,896]{3,2,1,0:T(8,128)(2,1)S(1)} %maximum_bitcast_fusion.x_ref, bf16[896,896]{1,0:T(8,128)(2,1)S(1)} %copy-done.2, bf16[896,896]{1,0:T(8,128)(2,1)S(1)} %copy-done.3, bf16[896,128]{1,0:T(8,128)(2,1)S(1)} %copy-done.4, ...), custom_call_target="tpu_custom_call" | custom-call | tf_op jit(solution)/shard_map/pallas_call | solution.py:213
  194.4 0.6 add_convert_fusion.1
  (56 shorter events, 2.1 us)
Async XLA Ops:
  0.0 126.1 %copy-start = (bf16[224,7168]{1,0:T(8,128)(2,1)S(1)}, bf16[224,7168]{1,0:T(8,128)(2,1)}, u32[]{:S(2)}) copy-start(bf16[224,7168]{1,0:T(8,128)(2,1)} %param.26) | copy-start | bytes 9633796
  5.7 36.7 %copy-start.7 = (bf16[7168]{0:T(1024)(128)(2,1)S(1)}, bf16[7168]{0:T(1024)(128)(2,1)}, u32[]{:S(2)}) copy-start(bf16[7168]{0:T(1024)(128)(2,1)} %param.20) | copy-start | bytes 43012
  58.2 1.3 copy-start.1
  87.3 6.7 %copy-start.10 = (s32[4]{0:T(128)S(1)}, s32[4]{0:T(128)}, u32[]{:S(2)}) copy-start(s32[4]{0:T(128)} %param.24) | copy-start | bytes 52
  87.3 6.8 %copy-start.9 = (s32[4,48]{1,0:T(4,128)S(1)}, s32[4,48]{1,0:T(4,128)}, u32[]{:S(2)}) copy-start(s32[4,48]{1,0:T(4,128)} %param.25) | copy-start | bytes 2308
  125.8 21.3 %copy-start.8 = (bf16[7168]{0:T(1024)(128)(2,1)S(1)}, bf16[7168]{0:T(1024)(128)(2,1)}, u32[]{:S(2)}) copy-start(bf16[7168]{0:T(1024)(128)(2,1)} %param.27) | copy-start | bytes 43012
  126.1 23.1 %copy-start.4 = (bf16[896,128]{1,0:T(8,128)(2,1)S(1)}, bf16[896,128]{1,0:T(8,128)(2,1)}, u32[]{:S(2)}) copy-start(bf16[896,128]{1,0:T(8,128)(2,1)} %down_map_hbm.1) | copy-start | bytes 688132
  149.2 1.4 copy-start.2
  150.6 1.4 copy-start.3
  152.0 0.9 copy-start.5
  153.0 0.9 copy-start.6

commit v11 on v10

--- a/solution.py
+++ b/solution.py
@@ -241,7 +241,7 @@
         ]
         + [pltpu.SemaphoreType.DMA((6,))],
         compiler_params=pltpu.CompilerParams(
-            collective_id=cid, has_side_effects=True, vmem_limit_bytes=48 * 1024 * 1024
+            collective_id=cid, has_side_effects=True
         ),
     )(both, gate_weight, up_weight, down_map, gate_map, up_map, down_weight)
 
@@ -312,7 +312,7 @@
         + semaphores
         + [pltpu.SemaphoreType.DMA((len(spec),))],
         compiler_params=pltpu.CompilerParams(
-            collective_id=cid, has_side_effects=True, vmem_limit_bytes=48 * 1024 * 1024
+            collective_id=cid, has_side_effects=True
         ),
     )(x, *extra)
 

time: 196 us -> 192 us (0.980)
  local copies, waits for them, and re-layouts: 37.9 us -> 31.3 us
  Pallas kernels: 127 us -> 129 us
    unnamed x30 -> x18, local copies, waits for them, and re-layouts: 11.2 us -> 5.16 us
where the time goes in v11:
time: 192 us; the launch traced here: 191 us
  Pallas kernels  129 us (67%)
  local copies, waits for them, and re-layouts  31.3 us (16%)
  other arithmetic  18.3 us (10%)
  matrix products  10.9 us (6%)
    pallas_call x2, Pallas kernels, two_rounds(): pl.pallas_call(functools.partial(_two_round_kernel, (axis_a, n_a, gather_...  44 us
    pallas_call x1, Pallas kernels, fused_mlp(): pl.pallas_call(_mlp_kernel, out_shape=(jax.ShapeDtypeStruct((out_rows, do...  41 us
    pallas_call x1, Pallas kernels, chain(): pl.pallas_call(functools.partial(_chain_kernel, spec, len(extra)), out_sh...  24.8 us
    pallas_call x2, Pallas kernels, exchange(): pl.pallas_call(functools.partial(_exchange_kernel, axis, n, gather), out_...  19.3 us
    gather x2, local copies, waits for them, and re-layouts, body(): jnp.take(token_embedding_table, jnp.clip(local_ids, 0, vocab_rows - 1), a...  7.28 us
    unnamed x18, local copies, waits for them, and re-layouts  5.16 us
    dot_general x1, matrix products, body(): jnp.dot(spread_queries.reshape(group_rows * HEADS, head_cols), cache_k.T,...  4.84 us
    dot_general x1, matrix products, body(): jnp.dot(weights.astype(jnp.bfloat16).reshape(group_rows * HEADS, slots *...  4.22 us

profile of v11, /device:TPU:1, one launch (start us, length us, event | category | flops | bytes accessed | tf_op | source)
XLA Modules:
  0.0 190.7 jit_solution(16537285549715836547)
XLA Ops:
  0.0 0.8 compare_and_fusion.1
  0.8 4.9 %gather_fusion = bf16[128,3584]{1,0:T(8,128)(2,1)} fusion(bf16[250,3584]{1,0:T(8,128)(2,1)} %param.19, s32[1024]{0:T(1024)S(1)} %pad_clamp_fusion), kind=kCustom, calls=%fused_computation | custom fusion | bytes 1835520 | tf_op jit(solution)/shard_map/jit(_take)/gather | solution.py:393
  5.7 2.4 %gather.7 = bf16[8,16,28,128]{3,2,1,0:T(8,128)(2,1)} reshape(bf16[128,3584]{1,0:T(8,128)(2,1)} %gather_fusion) | data formatting | bytes 1835008 | tf_op jit(solution)/shard_map/jit(_take)/gather | solution.py:393
  8.3 2.4 %select_convert_fusion.x_ref = bf16[8,16,28,128]{3,2,1,0:T(8,128)(2,1)} fusion(bf16[8,16,28,128]{3,2,1,0:T(8,128)(2,1)} %gather.7, pred[8,16]{1,0:T(8,128)(4,1)S(1)} %broadcast_in_dim.158, pred[8,16]{1,0:T(8,128)(4,1)S(1)} %broadcast_in_dim.156), kind=kLoop, calls=%fused_computation.5 | loop fusion | flops 1835008 | bytes 1835264 | tf_op jit(solution)/shard_map/convert_element_type | solution.py:396
  10.6 27.8 %shard_map.163 = bf16[16,28,128]{2,1,0:T(8,128)(2,1)} custom-call(bf16[8,16,28,128]{3,2,1,0:T(8,128)(2,1)} %select_convert_fusion.x_ref), custom_call_target="tpu_custom_call" | custom-call | tf_op jit(solution)/shard_map/pallas_call | solution.py:121
  38.4 0.9 reduce_sum.89
  39.4 0.9 fusion.33
  40.3 0.7 fusion.32
  41.0 0.7 multiply_reduce_fusion.1
  42.4 0.6 fusion.24.x_ref
  43.1 9.6 %shard_map.164 = bf16[16,56,128]{2,1,0:T(8,128)(2,1)} custom-call(bf16[56,128]{1,0:T(8,128)(2,1)} %fusion.24.x_ref), custom_call_target="tpu_custom_call" | custom-call | tf_op jit(solution)/shard_map/pallas_call | solution.py:54
  52.7 1.2 reshape_reshape.3
  53.9 0.7 copy.155
  54.6 2.6 %copy.94.refs_0_ = bf16[896,672]{1,0:T(8,128)(2,1)} copy(bf16[896,672]{0,1:T(8,128)(2,1)} %param.21) | data formatting | bytes 2408448 | tf_op args[4]
  57.2 24.8 %shard_map.165 = bf16[16,16,672]{2,1,0:T(8,128)(2,1)} custom-call(bf16[8,16,896]{2,1,0:T(8,128)(2,1)} %bitcast.115, bf16[896,672]{1,0:T(8,128)(2,1)} %copy.94.refs_0_), custom_call_target="tpu_custom_call" | custom-call | tf_op jit(solution)/shard_map/pallas_call | solution.py:302
  82.0 1.9 copy.95
  83.9 1.5 reshape.399
  85.4 0.8 fusion.34
  86.2 1.1 reshape.408
  87.5 0.7 add_convert_fusion.2
  88.2 0.1 multiply_cosine_fusion
  88.4 0.8 subtract_convert_fusion
  89.1 1.1 reshape.407
  90.4 0.1 multiply_subtract_fusion
  90.5 0.1 maximum_convert_fusion
  90.6 1.1 fusion.8
  91.8 0.2 copy.105
  91.9 0.1 fusion.14
  92.3 0.1 copy.129
  92.4 0.2 convert_element_type.113
  92.6 1.4 broadcast_select_fusion
  94.2 0.2 select_reduce_fusion
  94.6 0.3 fusion.30
  94.9 0.1 copy.91
  95.1 4.8 %fusion.4 = (f32[256]{0:T(256)S(1)}, f32[256,768]{1,0:T(8,128)S(1)}) fusion(pred[4,768]{1,0:T(4,128)(4,1)S(1)} %fusion.26, bf16[256,3584]{1,0:T(8,128)(2,1)} %bitcast.112, bf16[768,3584]{1,0:T(8,128)(2,1)} %bitcast.113), kind=kOutput, calls=%fused_computation.11 | convolution fusion | flops 1409875712 | bytes 8130560 | tf_op jit(solution)/shard_map/dot_general | solution.py:475
  100.0 0.3 fusion.6
  100.3 4.2 %fusion.3 = f32[16,3584]{1,0:T(8,128)S(1)} fusion(bf16[16,16,768]{2,1,0:T(8,128)(2,1)S(1)} %bitcast.116, bf16[768,3584,1]{1,0,2:T(8,128)(2,1)} %bitcast.128, pred[16,3584]{1,0:T(8,128)(4,1)S(1)} %iota_compare_fusion), kind=kOutput, calls=%fused_computation.7 | convolution fusion | flops 1411063808 | bytes 6184960 | tf_op jit(solution)/shard_map/dot_general | solution.py:486
  104.5 0.9 concatenate.43
  105.4 1.1 copy.99
  106.6 0.8 copy.101
  107.5 0.8 copy.100
  108.4 1.8 maximum_bitcast_fusion.1.x_ref
  110.2 9.7 %shard_map.166 = f32[16,16,256]{2,1,0:T(8,128)} custom-call(f32[16,16,256]{2,1,0:T(8,128)} %maximum_bitcast_fusion.1.x_ref), custom_call_target="tpu_custom_call" | custom-call | tf_op jit(solution)/shard_map/pallas_call | solution.py:54
  119.9 1.0 reshape.403
  120.9 0.9 fusion.35
  121.8 1.1 copy.123
  122.9 1.1 copy.126
  124.0 0.2 fusion.29
  124.1 0.1 copy.127
  124.3 0.1 copy.108
  124.5 0.1 fusion.7
  124.6 0.2 copy.111
  124.8 1.1 reshape.404
  125.9 0.2 fusion.12
  126.3 0.5 fusion
  126.8 0.9 copy.116.x_ref
  127.7 16.2 %shard_map.167 = bf16[16,56,128]{2,1,0:T(8,128)(2,1)} custom-call(f32[16,56,128]{2,1,0:T(8,128)} %copy.116.x_ref, bf16[56,128]{1,0:T(8,128)(2,1)} %bitcast.121), custom_call_target="tpu_custom_call" | custom-call | tf_op jit(solution)/shard_map/pallas_call | solution.py:121
  144.0 1.2 stack.6
  145.1 1.1 multiply_reduce_fusion
  146.4 0.1 multiply_convert_fusion
  146.5 0.8 maximum_bitcast_fusion.x_ref
  147.3 41.0 %shard_map.168 = (f32[8,896]{1,0:T(8,128)}, bf16[8,2,16,896]{3,2,1,0:T(8,128)(2,1)}) custom-call(bf16[8,2,16,896]{3,2,1,0:T(8,128)(2,1)} %maximum_bitcast_fusion.x_ref, bf16[896,896]{1,0:T(8,128)(2,1)} %gate_hbm.1, bf16[896,896]{1,0:T(8,128)(2,1)} %up_hbm.1, bf16[896,128]{1,0:T(8,128)(2,1)} %down_map_hbm.1, bf16[128,896]{1,0:T(8,128)(2,1)} %gate_map_hbm.1, ...), custom_call_target="tpu_custom_call" | custom-call | tf_op jit(solution)/shard_map/pallas_call | solution.py:213
  188.3 1.0 slice.43
  189.3 1.4 add_convert_fusion.1
  (44 shorter events, 1.6 us)
Async XLA Ops:
  0.0 126.2 %copy-start = (bf16[224,7168]{1,0:T(8,128)(2,1)S(1)}, bf16[224,7168]{1,0:T(8,128)(2,1)}, u32[]{:S(2)}) copy-start(bf16[224,7168]{1,0:T(8,128)(2,1)} %param.26) | copy-start | bytes 9633796
  5.7 36.7 %copy-start.1 = (bf16[7168]{0:T(1024)(128)(2,1)S(1)}, bf16[7168]{0:T(1024)(128)(2,1)}, u32[]{:S(2)}) copy-start(bf16[7168]{0:T(1024)(128)(2,1)} %param.20) | copy-start | bytes 43012
  87.4 6.7 %copy-start.4 = (s32[4]{0:T(128)S(1)}, s32[4]{0:T(128)}, u32[]{:S(2)}) copy-start(s32[4]{0:T(128)} %param.24) | copy-start | bytes 52
  87.4 6.8 %copy-start.3 = (s32[4,48]{1,0:T(4,128)S(1)}, s32[4,48]{1,0:T(4,128)}, u32[]{:S(2)}) copy-start(s32[4,48]{1,0:T(4,128)} %param.25) | copy-start | bytes 2308
  125.9 20.4 %copy-start.2 = (bf16[7168]{0:T(1024)(128)(2,1)S(1)}, bf16[7168]{0:T(1024)(128)(2,1)}, u32[]{:S(2)}) copy-start(bf16[7168]{0:T(1024)(128)(2,1)} %param.27) | copy-start | bytes 43012

commit v12 on v11

--- a/solution.py
+++ b/solution.py
@@ -396,27 +396,48 @@
     looked = jnp.where(present[:, None], looked, 0.0).astype(jnp.bfloat16)
     row_share = group_rows // seq_devices
     lanes = 128
-    by_group = looked.reshape(req_devices, seq_devices, row_share * looked.shape[1] // lanes, lanes)
-    row_parts = two_rounds(
+    tile_rows = row_share * looked.shape[1] // lanes
+    by_group = looked.reshape(req_devices, seq_devices, tile_rows, lanes)
+    own_hidden = lax.dynamic_slice_in_dim(hidden, seq_index * row_share, row_share, 0)
+    model_width = hidden.shape[1] + looked.shape[1]
+
+    def normalize(landed, hidden_tiles, gain_tiles):
+        emb = _block_sum(landed)
+        front = hidden_tiles[...].astype(jnp.float32)
+        squares = jnp.sum(front * front) + jnp.sum(emb * emb)
+        factor = lax.rsqrt(squares / model_width + EPSILON)
+        gains = gain_tiles[...].astype(jnp.float32)
+        return jnp.stack(
+            [
+                (front * factor * gains[0]).astype(jnp.bfloat16),
+                (emb * factor * gains[1]).astype(jnp.bfloat16),
+                emb.astype(jnp.bfloat16),
+            ]
+        )
+
+    gathered = chain(
         by_group,
-        ("req", False),
-        ("seq", False),
-        lambda landed: _block_sum(landed).astype(jnp.bfloat16),
-        by_group.shape[1:],
-        jnp.bfloat16,
-        10,
-    )
-    embedded_rows = (
-        jnp.sum(row_parts.astype(jnp.float32), axis=0)
-        .astype(jnp.bfloat16)
-        .reshape(row_share, looked.shape[1])
-    )
-    own_hidden = lax.dynamic_slice_in_dim(hidden, seq_index * row_share, row_share, 0)
+        [
+            (
+                "req",
+                False,
+                lambda landed, *rest: _block_sum(landed).astype(jnp.bfloat16),
+                ((seq_devices, tile_rows, lanes), jnp.bfloat16),
+            ),
+            ("seq", False, normalize, ((3, tile_rows, lanes), jnp.bfloat16)),
+            ("seq", True, None, None),
+        ],
+        12,
+        extra=(
+            own_hidden.reshape(tile_rows, lanes),
+            attention_norm_gain.reshape(2, tile_rows, lanes),
+        ),
+    )
+    normed = gathered[:, :2].reshape(group_rows, model_width)
+    embedded_rows = lax.dynamic_index_in_dim(gathered, seq_index, 0, keepdims=False)[2].reshape(
+        row_share, looked.shape[1]
+    )
     own_rows = jnp.concatenate([own_hidden, embedded_rows], axis=1)
-    normed_rows = rms_norm(own_rows, attention_norm_gain)
-    normed = exchange(normed_rows.reshape(-1, lanes), "seq", 12, gather=True).reshape(
-        group_rows, own_rows.shape[1]
-    )
     width_share = normed.shape[1] // req_devices
     to_owners = jnp.transpose(normed.reshape(group_rows, req_devices, width_share), (1, 0, 2))
     qkv_cols = query_key_value_weight.shape[1]

time: 192 us -> 199 us (1.036)
  local copies, waits for them, and re-layouts: 31.3 us -> 37.8 us
  other arithmetic: 18.3 us -> 23 us
  Pallas kernels: 129 us -> 127 us
    pallas_call x1 -> x2, Pallas kernels: 24.8 us -> 60.1 us  [chain(): pl.pallas_call(functools.partial(_chain_kernel, spec, len(extra)), out_sh...]
    pallas_call x2 -> x1, Pallas kernels: 44 us -> 16.7 us  [two_rounds(): pl.pallas_call(functools.partial(_two_round_kernel, (axis_a, n_a, gather_...]
    pallas_call x2 -> x1, Pallas kernels: 19.3 us -> 9.67 us  [exchange(): pl.pallas_call(functools.partial(_exchange_kernel, axis, n, gather), out_...]
    dot_general x1, matrix products: 4.22 us -> 1.65 us  [body(): jnp.dot(weights.astype(jnp.bfloat16).reshape(group_rows * HEADS, slots *...]
    unnamed x18 -> x25, local copies, waits for them, and re-layouts: 5.16 us -> 5.86 us
where the time goes in v12:
time: 199 us; the launch traced here: 197 us
  Pallas kernels  127 us (64%)
  local copies, waits for them, and re-layouts  37.8 us (19%)
  other arithmetic  23 us (12%)
  matrix products  9.49 us (5%)
    pallas_call x2, Pallas kernels, chain(): pl.pallas_call(functools.partial(_chain_kernel, spec, len(extra)), out_sh...  60.1 us
    pallas_call x1, Pallas kernels, fused_mlp(): pl.pallas_call(_mlp_kernel, out_shape=(jax.ShapeDtypeStruct((out_rows, do...  40.3 us
    pallas_call x1, Pallas kernels, two_rounds(): pl.pallas_call(functools.partial(_two_round_kernel, (axis_a, n_a, gather_...  16.7 us
    pallas_call x1, Pallas kernels, exchange(): pl.pallas_call(functools.partial(_exchange_kernel, axis, n, gather), out_...  9.67 us
    gather x2, local copies, waits for them, and re-layouts, body(): jnp.take(token_embedding_table, jnp.clip(local_ids, 0, vocab_rows - 1), a...  7.11 us
    unnamed x25, local copies, waits for them, and re-layouts  5.86 us
    dot_general x1, matrix products, body(): jnp.dot(spread_queries.reshape(group_rows * HEADS, head_cols), cache_k.T,...  4.38 us
    concatenate x7, local copies, waits for them, and re-layouts, body(): jnp.concatenate([local_out, local_max[..., None], local_sum[..., None], j...  4.37 us

profile of v12, /device:TPU:1, one launch (start us, length us, event | category | flops | bytes accessed | tf_op | source)
XLA Modules:
  0.0 197.4 jit_solution(6911598761145315588)
XLA Ops:
  0.0 0.6 iota_compare_fusion.1
  0.6 0.9 and_select_fusion
  1.6 0.6 pad.9.clone
  2.2 0.9 fusion.29
  3.3 0.7 compare_and_fusion.1
  4.1 0.7 add_convert_fusion.2
  4.8 0.9 select_reduce_fusion
  6.0 0.7 multiply_cosine_fusion
  6.8 1.3 fusion.25
  8.1 1.3 reshape.353.refs_1_
  9.4 1.5 fusion.31
  10.9 1.4 reshape.364
  12.3 0.7 iota_compare_fusion
  12.9 4.7 %gather_fusion = bf16[128,3584]{1,0:T(8,128)(2,1)} fusion(bf16[250,3584]{1,0:T(8,128)(2,1)} %param.19, s32[1024]{0:T(1024)S(1)} %pad_clamp_fusion), kind=kCustom, calls=%fused_computation | custom fusion | bytes 1835520 | tf_op jit(solution)/shard_map/jit(_take)/gather | solution.py:393
  17.6 2.4 %gather.7 = bf16[8,16,28,128]{3,2,1,0:T(8,128)(2,1)} reshape(bf16[128,3584]{1,0:T(8,128)(2,1)} %gather_fusion) | data formatting | bytes 1835008 | tf_op jit(solution)/shard_map/jit(_take)/gather | solution.py:393
  20.0 2.4 %select_convert_fusion.x_ref = bf16[8,16,28,128]{3,2,1,0:T(8,128)(2,1)} fusion(bf16[8,16,28,128]{3,2,1,0:T(8,128)(2,1)} %gather.7, pred[8,16]{1,0:T(8,128)(4,1)S(1)} %broadcast_in_dim.156, pred[8,16]{1,0:T(8,128)(4,1)S(1)} %broadcast_in_dim.154), kind=kLoop, calls=%fused_computation.5 | loop fusion | flops 1835008 | bytes 1835264 | tf_op jit(solution)/shard_map/convert_element_type | solution.py:396
  22.4 36.0 %shard_map.163 = bf16[16,3,28,128]{3,2,1,0:T(8,128)(2,1)} custom-call(bf16[8,16,28,128]{3,2,1,0:T(8,128)(2,1)} %select_convert_fusion.x_ref, bf16[28,128]{1,0:T(8,128)(2,1)} %bitcast.119, bf16[2,28,128]{2,1,0:T(8,128)(2,1)} %reshape.353.refs_1_), custom_call_target="tpu_custom_call" | custom-call | tf_op jit(solution)/shard_map/pallas_call | solution.py:302
  58.4 0.7 dynamic-slice_bitcast_fusion
  59.1 1.0 slice.40
  60.0 0.9 reshape_reshape.3
  61.0 1.6 copy.155
  62.6 0.7 maximum_reduce_fusion
  63.3 2.6 %copy.94.refs_0_ = bf16[896,672]{1,0:T(8,128)(2,1)} copy(bf16[896,672]{0,1:T(8,128)(2,1)} %param.21) | data formatting | bytes 2408448 | tf_op args[4]
  65.9 24.1 %shard_map.164 = bf16[16,16,672]{2,1,0:T(8,128)(2,1)} custom-call(bf16[8,16,896]{2,1,0:T(8,128)(2,1)} %bitcast.114, bf16[896,672]{1,0:T(8,128)(2,1)} %copy.94.refs_0_), custom_call_target="tpu_custom_call" | custom-call | tf_op jit(solution)/shard_map/pallas_call | solution.py:302
  90.0 1.9 copy.95
  91.9 1.5 reshape.354
  93.4 0.8 fusion.32
  94.2 1.8 reshape.359
  96.0 1.1 reshape.363
  97.2 1.4 subtract_convert_fusion
  98.7 1.1 reshape.362
  99.9 0.8 multiply_subtract_fusion
  100.7 0.1 maximum_convert_fusion
  100.9 1.1 fusion.8
  102.0 0.2 copy.105
  102.2 0.2 convert_element_type.87
  102.9 0.2 copy.111
  103.1 1.8 fusion.12
  104.9 1.2 broadcast_select_fusion
  106.1 4.4 %fusion.4 = (f32[256]{0:T(256)S(1)}, f32[256,768]{1,0:T(8,128)S(1)}) fusion(pred[4,768]{1,0:T(4,128)(4,1)S(1)} %copy-done.3, bf16[256,3584]{1,0:T(8,128)(2,1)S(1)} %bitcast.111, bf16[768,3584]{1,0:T(8,128)(2,1)} %bitcast.112), kind=kOutput, calls=%fused_computation.11 | convolution fusion | flops 1409875712 | bytes 8130560 | tf_op jit(solution)/shard_map/dot_general | solution.py:496
  110.5 0.3 fusion.6
  110.8 1.7 fusion.3
  112.7 0.9 concatenate.22
  113.5 1.1 copy.99
  114.6 0.8 copy.101
  115.5 0.8 copy.100
  116.3 1.8 maximum_bitcast_fusion.1.x_ref
  118.1 9.7 %shard_map.165 = f32[16,16,256]{2,1,0:T(8,128)} custom-call(f32[16,16,256]{2,1,0:T(8,128)} %maximum_bitcast_fusion.1.x_ref), custom_call_target="tpu_custom_call" | custom-call | tf_op jit(solution)/shard_map/pallas_call | solution.py:54
  127.8 1.0 reshape.358
  128.8 0.9 fusion.33
  129.7 1.1 copy.126
  130.8 1.1 copy.123
  131.9 0.2 fusion.28
  132.3 0.1 fusion.7
  132.4 0.8 fusion.23
  133.2 0.5 fusion
  133.8 0.9 copy.116.x_ref
  134.7 16.7 %shard_map.166 = bf16[16,56,128]{2,1,0:T(8,128)(2,1)} custom-call(f32[16,56,128]{2,1,0:T(8,128)} %copy.116.x_ref, bf16[56,128]{1,0:T(8,128)(2,1)} %bitcast.118), custom_call_target="tpu_custom_call" | custom-call | tf_op jit(solution)/shard_map/pallas_call | solution.py:121
  151.4 1.1 multiply_reduce_fusion
  152.6 1.2 stack.6
  154.0 0.8 maximum_bitcast_fusion.x_ref
  154.8 40.3 %shard_map.167 = (f32[8,896]{1,0:T(8,128)}, bf16[8,2,16,896]{3,2,1,0:T(8,128)(2,1)}) custom-call(bf16[8,2,16,896]{3,2,1,0:T(8,128)(2,1)} %maximum_bitcast_fusion.x_ref, bf16[896,896]{1,0:T(8,128)(2,1)} %gate_hbm.1, bf16[896,896]{1,0:T(8,128)(2,1)} %up_hbm.1, bf16[896,128]{1,0:T(8,128)(2,1)} %down_map_hbm.1, bf16[128,896]{1,0:T(8,128)(2,1)} %gate_map_hbm.1, ...), custom_call_target="tpu_custom_call" | custom-call | tf_op jit(solution)/shard_map/pallas_call | solution.py:213
  195.0 1.0 slice.52
  196.0 1.4 add_convert_fusion.1
  (50 shorter events, 1.9 us)
Async XLA Ops:
  0.0 133.2 %copy-start = (bf16[224,7168]{1,0:T(8,128)(2,1)S(1)}, bf16[224,7168]{1,0:T(8,128)(2,1)}, u32[]{:S(2)}) copy-start(bf16[224,7168]{1,0:T(8,128)(2,1)} %param.26) | copy-start | bytes 9633796
  94.2 8.1 %copy-start.5 = (pred[4,4]{1,0:T(4,128)(4,1)S(1)}, pred[4,4]{1,0:T(4,128)(4,1)}, u32[]{:S(2)}) copy-start(pred[4,4]{1,0:T(4,128)(4,1)} %iota_compare_fusion.1) | copy-start | bytes 52
  97.2 8.9 %copy-start.3 = (pred[4,768]{1,0:T(4,128)(4,1)S(1)}, pred[4,768]{1,0:T(4,128)(4,1)}, u32[]{:S(2)}) copy-start(pred[4,768]{1,0:T(4,128)(4,1)} %fusion.25) | copy-start | bytes 9220
  104.9 5.9 %slice-start = ((s8[5505024]{0:T(1024)(128)(4,1)}), s8[4194304]{0:T(1024)(128)(4,1)S(1)}, s32[]{:S(2)}) async-start(s8[5505024]{0:T(1024)(128)(4,1)} %bitcast.126), calls=%async_computation | async-start | bytes 8388608
  106.1 4.7 %copy-start.1 = (pred[16,3584]{1,0:T(8,128)(4,1)S(1)}, pred[16,3584]{1,0:T(8,128)(4,1)}, u32[]{:S(2)}) copy-start(pred[16,3584]{1,0:T(8,128)(4,1)} %iota_compare_fusion) | copy-start | bytes 172036
  106.1 4.7 %slice-start.1 = ((s8[5505024]{0:T(1024)(128)(4,1)}), s8[1310720]{0:T(1024)(128)(4,1)S(1)}, s32[]{:S(2)}) async-start(s8[5505024]{0:T(1024)(128)(4,1)} %bitcast.126), calls=%async_computation.1 | async-start | bytes 2621440
  110.8 5.5 %copy-start.4 = (f32[256]{0:T(256)S(1)}, f32[256]{0:T(256)}, u32[]{:S(2)}) copy-start(f32[256]{0:T(256)} %pad.9.clone) | copy-start | bytes 3076
  132.1 21.7 %copy-start.2 = (f32[8,896]{1,0:T(8,128)S(1)}, f32[8,896]{1,0:T(8,128)}, u32[]{:S(2)}) copy-start(f32[8,896]{1,0:T(8,128)} %reshape.364) | copy-start | bytes 86020

commit v13 on v11

--- a/solution.py
+++ b/solution.py
@@ -524,32 +524,44 @@
     )
     packed = packed.reshape(requests * steps_each, seq_devices, own_heads, 256)
     packed = jnp.transpose(packed, (1, 0, 2, 3)).reshape(seq_devices, group_rows * own_heads, 256)
-    arrived = exchange(packed, "seq", 0).reshape(seq_devices, requests, steps_each, own_heads, 256)
-    part_o = arrived[..., :HD]
-    part_m = arrived[..., HD]
-    part_l = arrived[..., HD + 1]
-    f_max, f_sum, f_out = own_slice(fresh_max), own_slice(fresh_sum), own_slice(fresh_out)
-    overall = jnp.maximum(jnp.max(part_m, axis=0), f_max)
-    part_factor = jnp.exp(part_m - overall[None])
-    fresh_factor = jnp.exp(f_max - overall)
-    denominator = jnp.sum(part_l * part_factor, axis=0) + f_sum * fresh_factor
-    numerator = jnp.sum(part_o * part_factor[..., None], axis=0) + f_out * fresh_factor[..., None]
-    attention = (
-        (numerator / denominator[..., None])
-        .astype(jnp.bfloat16)
-        .reshape(group_rows, own_heads * HD)
-    )
-    projected_out = jnp.dot(attention, attention_output_weight, preferred_element_type=jnp.float32)
-    model_width = projected_out.shape[1]
-    after_attn = two_rounds(
-        projected_out.reshape(seq_devices, row_share * model_width // lanes, lanes),
-        ("seq", False),
-        ("seq", True),
-        lambda landed, own: (own[...].astype(jnp.float32) + _block_sum(landed)).astype(jnp.bfloat16),
-        (row_share * model_width // lanes, lanes),
-        jnp.bfloat16,
+    model_width = attention_output_weight.shape[1]
+    head_rows = group_rows * own_heads
+    tile_rows = row_share * model_width // lanes
+
+    def merge_and_project(landed, fresh_max_ref, fresh_sum_ref, fresh_out_ref, weight, own):
+        part_o = landed[:, :, :HD]
+        part_m = landed[:, :, HD : HD + 1]
+        part_l = landed[:, :, HD + 1 : HD + 2]
+        f_max = fresh_max_ref[...]
+        overall = jnp.maximum(jnp.max(part_m, axis=0), f_max)
+        part_factor = jnp.exp(part_m - overall[None])
+        fresh_factor = jnp.exp(f_max - overall)
+        denominator = jnp.sum(part_l * part_factor, axis=0) + fresh_sum_ref[...] * fresh_factor
+        numerator = jnp.sum(part_o * part_factor, axis=0) + fresh_out_ref[...] * fresh_factor
+        attention = (numerator / denominator).astype(jnp.bfloat16).reshape(
+            group_rows, own_heads * HD
+        )
+        product = jnp.dot(attention, weight[...], preferred_element_type=jnp.float32)
+        return product.reshape(seq_devices, tile_rows, lanes)
+
+    def add_residual(landed, fresh_max_ref, fresh_sum_ref, fresh_out_ref, weight, own):
+        return (own[...].astype(jnp.float32) + _block_sum(landed)).astype(jnp.bfloat16)
+
+    after_attn = chain(
+        packed,
+        [
+            ("seq", False, merge_and_project, ((seq_devices, tile_rows, lanes), jnp.float32)),
+            ("seq", False, add_residual, ((tile_rows, lanes), jnp.bfloat16)),
+            ("seq", True, None, None),
+        ],
         1,
-        extra=(own_rows.reshape(-1, lanes),),
+        extra=(
+            own_slice(fresh_max).reshape(head_rows, 1),
+            own_slice(fresh_sum).reshape(head_rows, 1),
+            own_slice(fresh_out).reshape(head_rows, HD),
+            attention_output_weight,
+            own_rows.reshape(tile_rows, lanes),
+        ),
     ).reshape(group_rows, model_width)
     second_normed_state = rms_norm(after_attn, feedforward_norm_gain)
     both = jnp.stack([after_attn, second_normed_state]).reshape(2, group_rows, req_devices, width_share)

time: 192 us -> 166 us (0.86)
  local copies, waits for them, and re-layouts: 31.3 us -> 17 us
  other arithmetic: 18.3 us -> 12.7 us
  Pallas kernels: 129 us -> 125 us
    pallas_call x1 -> x2, Pallas kernels: 24.8 us -> 46.8 us  [chain(): pl.pallas_call(functools.partial(_chain_kernel, spec, len(extra)), out_sh...]
    pallas_call x2 -> x1, Pallas kernels: 44 us -> 27.9 us  [two_rounds(): pl.pallas_call(functools.partial(_two_round_kernel, (axis_a, n_a, gather_...]
    pallas_call x2 -> x1, Pallas kernels: 19.3 us -> 9.64 us  [exchange(): pl.pallas_call(functools.partial(_exchange_kernel, axis, n, gather), out_...]
    gather x2, local copies, waits for them, and re-layouts: 7.28 us -> 3.67 us  [body(): jnp.take(token_embedding_table, jnp.clip(local_ids, 0, vocab_rows - 1), a...]
    concatenate x7, local copies, waits for them, and re-layouts: 3.87 us -> 0.93 us  [body(): jnp.concatenate([local_out, local_max[..., None], local_sum[..., None], j...]
    unnamed x18 -> x16, local copies, waits for them, and re-layouts: 5.16 us -> 2.83 us
where the time goes in v13:
time: 166 us; the launch traced here: 165 us
  Pallas kernels  125 us (75%)
  local copies, waits for them, and re-layouts  17 us (10%)
  other arithmetic  12.7 us (8%)
  matrix products  9.53 us (6%)
    pallas_call x2, Pallas kernels, chain(): pl.pallas_call(functools.partial(_chain_kernel, spec, len(extra)), out_sh...  46.8 us
    pallas_call x1, Pallas kernels, fused_mlp(): pl.pallas_call(_mlp_kernel, out_shape=(jax.ShapeDtypeStruct((out_rows, do...  40.9 us
    pallas_call x1, Pallas kernels, two_rounds(): pl.pallas_call(functools.partial(_two_round_kernel, (axis_a, n_a, gather_...  27.9 us
    pallas_call x1, Pallas kernels, exchange(): pl.pallas_call(functools.partial(_exchange_kernel, axis, n, gather), out_...  9.64 us
    dot_general x1, matrix products, body(): jnp.dot(spread_queries.reshape(group_rows * HEADS, head_cols), cache_k.T,...  4.83 us
    dot_general x1, matrix products, body(): jnp.dot(weights.astype(jnp.bfloat16).reshape(group_rows * HEADS, slots *...  4.22 us
    gather x2, local copies, waits for them, and re-layouts, body(): jnp.take(token_embedding_table, jnp.clip(local_ids, 0, vocab_rows - 1), a...  3.67 us

profile of v13, /device:TPU:1, one launch (start us, length us, event | category | flops | bytes accessed | tf_op | source)
XLA Modules:
  0.0 165.5 jit_solution(2787796390234182490)
XLA Ops:
  0.0 0.8 compare_and_fusion.1
  0.8 0.7 copy-done
  1.5 2.1 %gather_fusion = bf16[128,3584]{1,0:T(8,128)(2,1)} fusion(bf16[250,3584]{1,0:T(8,128)(2,1)S(1)} %copy-done, s32[1024]{0:T(1024)S(1)} %pad_clamp_fusion), kind=kCustom, calls=%fused_computation | custom fusion | bytes 1835520 | tf_op jit(solution)/shard_map/jit(_take)/gather | solution.py:393
  3.6 1.6 gather.7
  5.2 0.1 broadcast_in_dim.152
  5.3 0.1 broadcast_in_dim.154
  5.4 1.3 select_convert_fusion.x_ref
  6.7 27.9 %shard_map.163 = bf16[16,28,128]{2,1,0:T(8,128)(2,1)} custom-call(bf16[8,16,28,128]{3,2,1,0:T(8,128)(2,1)} %select_convert_fusion.x_ref), custom_call_target="tpu_custom_call" | custom-call | tf_op jit(solution)/shard_map/pallas_call | solution.py:121
  34.6 0.9 reduce_sum.67
  35.5 0.9 fusion.24
  36.4 0.7 fusion.23
  37.1 0.7 multiply_reduce_fusion.1
  38.6 0.6 fusion.18.x_ref
  39.2 9.6 %shard_map.164 = bf16[16,56,128]{2,1,0:T(8,128)(2,1)} custom-call(bf16[56,128]{1,0:T(8,128)(2,1)} %fusion.18.x_ref), custom_call_target="tpu_custom_call" | custom-call | tf_op jit(solution)/shard_map/pallas_call | solution.py:54
  48.8 1.2 reshape_reshape.3
  50.0 0.7 copy.130
  50.7 1.9 %copy.80.refs_0_ = bf16[896,672]{1,0:T(8,128)(2,1)} copy(bf16[896,672]{0,1:T(8,128)(2,1)S(1)} %copy-done.1) | data formatting | bytes 2408448 | tf_op args[4]
  52.7 24.8 %shard_map.165 = bf16[16,16,672]{2,1,0:T(8,128)(2,1)} custom-call(bf16[8,16,896]{2,1,0:T(8,128)(2,1)} %bitcast.79, bf16[896,672]{1,0:T(8,128)(2,1)} %copy.80.refs_0_), custom_call_target="tpu_custom_call" | custom-call | tf_op jit(solution)/shard_map/pallas_call | solution.py:302
  77.5 1.1 copy.81
  78.7 0.5 reshape.357
  79.2 0.2 reshape.367
  79.4 0.1 fusion.26
  79.6 0.1 multiply_cosine_fusion
  79.7 0.1 subtract_convert_fusion
  79.8 0.2 reshape.366
  80.0 0.1 fusion.27
  80.1 0.1 multiply_subtract_fusion
  80.3 0.1 maximum_convert_fusion
  80.4 0.3 fusion.4
  80.7 0.2 copy.90
  80.9 0.1 fusion.10
  81.0 0.1 fusion.13
  81.1 0.2 copy.95
  81.3 0.2 reshape.363
  81.5 0.2 fusion.8
  81.7 0.6 reshape.364.refs_2_
  82.3 0.7 constant_dynamic-slice_fusion
  83.0 0.2 convert_element_type.110
  83.3 1.4 broadcast_select_fusion
  84.7 0.1 iota_compare_fusion.2
  84.8 0.2 select_reduce_fusion
  85.1 0.1 copy.78
  85.2 0.3 fusion.21
  85.5 0.1 copy.77
  85.6 0.1 broadcast_bitcast_fusion.1
  85.7 0.1 fusion.20
  85.8 4.8 %fusion.1 = (f32[256]{0:T(256)S(1)}, f32[256,768]{1,0:T(8,128)S(1)}) fusion(pred[4,768]{1,0:T(4,128)(4,1)S(1)} %fusion.20, bf16[256,3584]{1,0:T(8,128)(2,1)} %bitcast.76, bf16[768,3584]{1,0:T(8,128)(2,1)} %bitcast.77), kind=kOutput, calls=%fused_computation.8 | convolution fusion | flops 1409875712 | bytes 8130560 | tf_op jit(solution)/shard_map/dot_general | solution.py:475
  90.6 0.3 fusion.3
  90.9 4.2 %fusion = f32[16,3584]{1,0:T(8,128)S(1)} fusion(bf16[16,16,768]{2,1,0:T(8,128)(2,1)S(1)} %bitcast.80, bf16[768,3584,1]{1,0,2:T(8,128)(2,1)} %bitcast.88, pred[16,3584]{1,0:T(8,128)(4,1)S(1)} %iota_compare_fusion), kind=kOutput, calls=%fused_computation.4 | convolution fusion | flops 1411063808 | bytes 6184960 | tf_op jit(solution)/shard_map/dot_general | solution.py:486
  95.1 0.2 concatenate.43
  95.3 0.2 copy.85
  95.5 0.1 concatenate.45
  95.6 0.2 copy.87
  95.7 0.1 concatenate.44
  95.8 0.2 copy.86
  96.1 0.8 maximum_bitcast_fusion.1.x_ref
  96.9 21.9 %shard_map.166 = bf16[16,56,128]{2,1,0:T(8,128)(2,1)} custom-call(f32[16,16,256]{2,1,0:T(8,128)} %maximum_bitcast_fusion.1.x_ref, f32[16,1]{1,0:T(8,128)} %bitcast.87, f32[16,1]{1,0:T(8,128)} %bitcast.86, f32[16,224]{1,0:T(8,128)} %reshape.364.refs_2_, bf16[224,7168]{1,0:T(8,128)(2,1)} %refs_3_.1, bf16[56,128]{1,0:T(8,128)(2,1)} %bitcast.85), custom_call_target="tpu_custom_call" | custom-call | tf_op jit(solution)/shard_map/pallas_call | solution.py:302
  118.9 1.2 stack.6
  120.0 1.1 multiply_reduce_fusion
  121.3 0.1 multiply_convert_fusion
  121.4 0.8 maximum_bitcast_fusion.x_ref
  122.2 40.9 %shard_map.167 = (f32[8,896]{1,0:T(8,128)}, bf16[8,2,16,896]{3,2,1,0:T(8,128)(2,1)}) custom-call(bf16[8,2,16,896]{3,2,1,0:T(8,128)(2,1)} %maximum_bitcast_fusion.x_ref, bf16[896,896]{1,0:T(8,128)(2,1)} %gate_hbm.1, bf16[896,896]{1,0:T(8,128)(2,1)} %up_hbm.1, bf16[896,128]{1,0:T(8,128)(2,1)} %down_map_hbm.1, bf16[128,896]{1,0:T(8,128)(2,1)} %gate_map_hbm.1, ...), custom_call_target="tpu_custom_call" | custom-call | tf_op jit(solution)/shard_map/pallas_call | solution.py:213
  163.1 1.0 slice.31
  164.1 1.4 add_convert_fusion.1
  (31 shorter events, 0.5 us)
Async XLA Ops:
  0.0 1.5 copy-start
  5.2 33.4 %copy-start.2 = (bf16[7168]{0:T(1024)(128)(2,1)S(1)}, bf16[7168]{0:T(1024)(128)(2,1)}, u32[]{:S(2)}) copy-start(bf16[7168]{0:T(1024)(128)(2,1)} %param.20) | copy-start | bytes 43012
  6.7 44.1 %copy-start.1 = (bf16[896,672]{0,1:T(8,128)(2,1)S(1)}, bf16[896,672]{0,1:T(8,128)(2,1)}, u32[]{:S(2)}) copy-start(bf16[896,672]{0,1:T(8,128)(2,1)} %param.21) | copy-start | bytes 3612676
  77.5 2.0 %copy-start.5 = (s32[4]{0:T(128)S(1)}, s32[4]{0:T(128)}, u32[]{:S(2)}) copy-start(s32[4]{0:T(128)} %param.24) | copy-start | bytes 52
  80.4 4.4 %copy-start.4 = (s32[4,48]{1,0:T(4,128)S(1)}, s32[4,48]{1,0:T(4,128)}, u32[]{:S(2)}) copy-start(s32[4,48]{1,0:T(4,128)} %param.25) | copy-start | bytes 2308
  96.9 24.3 %copy-start.3 = (bf16[7168]{0:T(1024)(128)(2,1)S(1)}, bf16[7168]{0:T(1024)(128)(2,1)}, u32[]{:S(2)}) copy-start(bf16[7168]{0:T(1024)(128)(2,1)} %param.27) | copy-start | bytes 43012

commit v14 on v13

--- a/solution.py
+++ b/solution.py
@@ -414,11 +414,15 @@
     own_hidden = lax.dynamic_slice_in_dim(hidden, seq_index * row_share, row_share, 0)
     own_rows = jnp.concatenate([own_hidden, embedded_rows], axis=1)
     normed_rows = rms_norm(own_rows, attention_norm_gain)
-    normed = exchange(normed_rows.reshape(-1, lanes), "seq", 12, gather=True).reshape(
-        group_rows, own_rows.shape[1]
-    )
-    width_share = normed.shape[1] // req_devices
-    to_owners = jnp.transpose(normed.reshape(group_rows, req_devices, width_share), (1, 0, 2))
+    model_width = own_rows.shape[1]
+    width_share = model_width // req_devices
+
+    def to_owners(landed, weight):
+        rows = landed[...].reshape(group_rows, model_width)
+        return jnp.stack(
+            [rows[:, part * width_share : (part + 1) * width_share] for part in range(req_devices)]
+        )
+
     qkv_cols = query_key_value_weight.shape[1]
 
     def project(landed, weight):
@@ -427,8 +431,9 @@
         return product.reshape(req_devices, group_rows, qkv_cols)
 
     qkv_all = chain(
-        to_owners,
+        normed_rows.reshape(-1, lanes),
         [
+            ("seq", True, to_owners, ((req_devices, group_rows, width_share), jnp.bfloat16)),
             ("req", False, project, ((req_devices, group_rows, qkv_cols), jnp.float32)),
             (
                 "req",

time: 166 us -> 159 us (0.958)
  Pallas kernels: 125 us -> 120 us
  local copies, waits for them, and re-layouts: 17 us -> 15.1 us
    pallas_call x1 -> x0, Pallas kernels: 9.64 us -> none  [exchange(): pl.pallas_call(functools.partial(_exchange_kernel, axis, n, gather), out_...]
    pallas_call x2, Pallas kernels: 46.8 us -> 51.3 us  [chain(): pl.pallas_call(functools.partial(_chain_kernel, spec, len(extra)), out_sh...]
    another operation x2 -> x0, local copies, waits for them, and re-layouts: 1.9 us -> none  [body(): normed.reshape(group_rows, req_devices, width_share)]
where the time goes in v14:
time: 159 us; the launch traced here: 158 us
  Pallas kernels  120 us (75%)
  local copies, waits for them, and re-layouts  15.1 us (9%)
  other arithmetic  12.7 us (8%)
  matrix products  9.53 us (6%)
    pallas_call x2, Pallas kernels, chain(): pl.pallas_call(functools.partial(_chain_kernel, spec, len(extra)), out_sh...  51.3 us
    pallas_call x1, Pallas kernels, fused_mlp(): pl.pallas_call(_mlp_kernel, out_shape=(jax.ShapeDtypeStruct((out_rows, do...  40.8 us
    pallas_call x1, Pallas kernels, two_rounds(): pl.pallas_call(functools.partial(_two_round_kernel, (axis_a, n_a, gather_...  27.9 us
    dot_general x1, matrix products, body(): jnp.dot(spread_queries.reshape(group_rows * HEADS, head_cols), cache_k.T,...  4.83 us
    dot_general x1, matrix products, body(): jnp.dot(weights.astype(jnp.bfloat16).reshape(group_rows * HEADS, slots *...  4.22 us
    gather x2, local copies, waits for them, and re-layouts, body(): jnp.take(token_embedding_table, jnp.clip(local_ids, 0, vocab_rows - 1), a...  3.67 us

profile of v14, /device:TPU:1, one launch (start us, length us, event | category | flops | bytes accessed | tf_op | source)
XLA Modules:
  0.0 158.4 jit_solution(4286791281520794671)
XLA Ops:
  0.0 0.8 compare_and_fusion.1
  0.8 0.7 copy-done
  1.5 2.1 %gather_fusion = bf16[128,3584]{1,0:T(8,128)(2,1)} fusion(bf16[250,3584]{1,0:T(8,128)(2,1)S(1)} %copy-done, s32[1024]{0:T(1024)S(1)} %pad_clamp_fusion), kind=kCustom, calls=%fused_computation | custom fusion | bytes 1835520 | tf_op jit(solution)/shard_map/jit(_take)/gather | solution.py:393
  3.6 1.6 %gather.7 = bf16[8,16,28,128]{3,2,1,0:T(8,128)(2,1)S(1)} reshape(bf16[128,3584]{1,0:T(8,128)(2,1)} %gather_fusion) | data formatting | bytes 1835008 | tf_op jit(solution)/shard_map/jit(_take)/gather | solution.py:393
  5.2 0.1 broadcast_in_dim.152
  5.3 0.1 broadcast_in_dim.154
  5.4 1.3 select_convert_fusion.x_ref
  6.7 27.9 %shard_map.163 = bf16[16,28,128]{2,1,0:T(8,128)(2,1)} custom-call(bf16[8,16,28,128]{3,2,1,0:T(8,128)(2,1)} %select_convert_fusion.x_ref), custom_call_target="tpu_custom_call" | custom-call | tf_op jit(solution)/shard_map/pallas_call | solution.py:121
  34.6 0.9 reduce_sum.67
  35.5 0.9 fusion.24
  36.4 0.7 fusion.23
  37.1 0.7 multiply_reduce_fusion.1
  38.6 0.6 fusion.18.x_ref
  39.2 1.9 %copy.76.refs_0_ = bf16[896,672]{1,0:T(8,128)(2,1)} copy(bf16[896,672]{0,1:T(8,128)(2,1)S(1)} %copy-done.1) | data formatting | bytes 2408448 | tf_op args[4]
  41.1 29.9 %shard_map.164 = bf16[16,16,672]{2,1,0:T(8,128)(2,1)} custom-call(bf16[56,128]{1,0:T(8,128)(2,1)} %fusion.18.x_ref, bf16[896,672]{1,0:T(8,128)(2,1)} %copy.76.refs_0_), custom_call_target="tpu_custom_call" | custom-call | tf_op jit(solution)/shard_map/pallas_call | solution.py:302
  71.1 1.1 copy.77
  72.2 0.5 reshape.357
  72.7 0.2 reshape.367
  72.9 0.1 fusion.26
  73.0 0.1 add_convert_fusion.2
  73.1 0.1 multiply_cosine_fusion
  73.2 0.1 subtract_convert_fusion
  73.4 0.2 reshape.366
  73.5 0.1 fusion.27
  73.6 0.1 multiply_subtract_fusion
  73.8 0.1 maximum_convert_fusion
  73.9 0.3 fusion.4
  74.2 0.2 copy.86
  74.4 0.1 fusion.10
  74.5 0.1 fusion.13
  74.6 0.2 copy.91
  74.8 0.2 reshape.363
  75.0 0.2 fusion.8
  75.2 0.6 reshape.364.refs_2_
  75.8 0.7 constant_dynamic-slice_fusion
  76.5 0.2 convert_element_type.110
  76.8 1.4 broadcast_select_fusion
  78.2 0.1 iota_compare_fusion.2
  78.3 0.2 select_reduce_fusion
  78.6 0.1 copy.75
  78.7 0.1 broadcast_bitcast_fusion
  78.7 0.3 fusion.21
  79.0 0.1 copy.74
  79.1 0.1 broadcast_bitcast_fusion.1
  79.2 0.1 fusion.20
  79.3 4.8 %fusion.1 = (f32[256]{0:T(256)S(1)}, f32[256,768]{1,0:T(8,128)S(1)}) fusion(pred[4,768]{1,0:T(4,128)(4,1)S(1)} %fusion.20, bf16[256,3584]{1,0:T(8,128)(2,1)} %bitcast.73, bf16[768,3584]{1,0:T(8,128)(2,1)} %bitcast.74), kind=kOutput, calls=%fused_computation.8 | convolution fusion | flops 1409875712 | bytes 8130560 | tf_op jit(solution)/shard_map/dot_general | solution.py:480
  84.1 0.3 fusion.3
  84.4 4.2 %fusion = f32[16,3584]{1,0:T(8,128)S(1)} fusion(bf16[16,16,768]{2,1,0:T(8,128)(2,1)S(1)} %bitcast.76, bf16[768,3584,1]{1,0,2:T(8,128)(2,1)} %bitcast.84, pred[16,3584]{1,0:T(8,128)(4,1)S(1)} %iota_compare_fusion), kind=kOutput, calls=%fused_computation.4 | convolution fusion | flops 1411063808 | bytes 6184960 | tf_op jit(solution)/shard_map/dot_general | solution.py:491
  88.7 0.2 concatenate.43
  88.8 0.2 copy.81
  89.0 0.1 concatenate.45
  89.1 0.2 copy.83
  89.3 0.1 concatenate.44
  89.3 0.2 copy.82
  89.5 0.1 pad.7.clone
  89.6 0.8 maximum_bitcast_fusion.1.x_ref
  90.4 21.4 %shard_map.165 = bf16[16,56,128]{2,1,0:T(8,128)(2,1)} custom-call(f32[16,16,256]{2,1,0:T(8,128)} %maximum_bitcast_fusion.1.x_ref, f32[16,1]{1,0:T(8,128)} %bitcast.83, f32[16,1]{1,0:T(8,128)} %bitcast.82, f32[16,224]{1,0:T(8,128)} %reshape.364.refs_2_, bf16[224,7168]{1,0:T(8,128)(2,1)} %refs_3_.1, bf16[56,128]{1,0:T(8,128)(2,1)} %bitcast.81), custom_call_target="tpu_custom_call" | custom-call | tf_op jit(solution)/shard_map/pallas_call | solution.py:302
  111.9 1.2 stack.6
  113.1 1.1 multiply_reduce_fusion
  114.3 0.1 multiply_convert_fusion
  114.4 0.8 maximum_bitcast_fusion.x_ref
  115.3 40.8 %shard_map.166 = (f32[8,896]{1,0:T(8,128)}, bf16[8,2,16,896]{3,2,1,0:T(8,128)(2,1)}) custom-call(bf16[8,2,16,896]{3,2,1,0:T(8,128)(2,1)} %maximum_bitcast_fusion.x_ref, bf16[896,896]{1,0:T(8,128)(2,1)} %gate_hbm.1, bf16[896,896]{1,0:T(8,128)(2,1)} %up_hbm.1, bf16[896,128]{1,0:T(8,128)(2,1)} %down_map_hbm.1, bf16[128,896]{1,0:T(8,128)(2,1)} %gate_map_hbm.1, ...), custom_call_target="tpu_custom_call" | custom-call | tf_op jit(solution)/shard_map/pallas_call | solution.py:213
  156.1 1.0 slice.31
  157.0 1.4 add_convert_fusion.1
  (28 shorter events, 0.3 us)
Async XLA Ops:
  0.0 1.5 copy-start
  5.2 33.4 %copy-start.2 = (bf16[7168]{0:T(1024)(128)(2,1)S(1)}, bf16[7168]{0:T(1024)(128)(2,1)}, u32[]{:S(2)}) copy-start(bf16[7168]{0:T(1024)(128)(2,1)} %param.20) | copy-start | bytes 43012
  6.7 32.5 %copy-start.1 = (bf16[896,672]{0,1:T(8,128)(2,1)S(1)}, bf16[896,672]{0,1:T(8,128)(2,1)}, u32[]{:S(2)}) copy-start(bf16[896,672]{0,1:T(8,128)(2,1)} %param.21) | copy-start | bytes 3612676
  71.0 2.0 %copy-start.5 = (s32[4]{0:T(128)S(1)}, s32[4]{0:T(128)}, u32[]{:S(2)}) copy-start(s32[4]{0:T(128)} %param.24) | copy-start | bytes 52
  73.9 4.4 %copy-start.4 = (s32[4,48]{1,0:T(4,128)S(1)}, s32[4,48]{1,0:T(4,128)}, u32[]{:S(2)}) copy-start(s32[4,48]{1,0:T(4,128)} %param.25) | copy-start | bytes 2308
  90.4 23.8 %copy-start.3 = (bf16[7168]{0:T(1024)(128)(2,1)S(1)}, bf16[7168]{0:T(1024)(128)(2,1)}, u32[]{:S(2)}) copy-start(bf16[7168]{0:T(1024)(128)(2,1)} %param.27) | copy-start | bytes 43012

commit v15 on v14

--- a/solution.py
+++ b/solution.py
@@ -533,7 +533,7 @@
     head_rows = group_rows * own_heads
     tile_rows = row_share * model_width // lanes
 
-    def merge_and_project(landed, fresh_max_ref, fresh_sum_ref, fresh_out_ref, weight, own):
+    def merge_and_project(landed, fresh_max_ref, fresh_sum_ref, fresh_out_ref, weight, own, gain):
         part_o = landed[:, :, :HD]
         part_m = landed[:, :, HD : HD + 1]
         part_l = landed[:, :, HD + 1 : HD + 2]
@@ -549,14 +549,18 @@
         product = jnp.dot(attention, weight[...], preferred_element_type=jnp.float32)
         return product.reshape(seq_devices, tile_rows, lanes)
 
-    def add_residual(landed, fresh_max_ref, fresh_sum_ref, fresh_out_ref, weight, own):
-        return (own[...].astype(jnp.float32) + _block_sum(landed)).astype(jnp.bfloat16)
-
-    after_attn = chain(
+    def add_residual(landed, fresh_max_ref, fresh_sum_ref, fresh_out_ref, weight, own, gain):
+        after = (own[...].astype(jnp.float32) + _block_sum(landed)).astype(jnp.bfloat16)
+        widened = after.astype(jnp.float32)
+        factor = lax.rsqrt(jnp.sum(widened * widened) / model_width + EPSILON)
+        normed_two = (widened * factor * gain[...].astype(jnp.float32)).astype(jnp.bfloat16)
+        return jnp.stack([after, normed_two])
+
+    both_rows = chain(
         packed,
         [
             ("seq", False, merge_and_project, ((seq_devices, tile_rows, lanes), jnp.float32)),
-            ("seq", False, add_residual, ((tile_rows, lanes), jnp.bfloat16)),
+            ("seq", False, add_residual, ((2, tile_rows, lanes), jnp.bfloat16)),
             ("seq", True, None, None),
         ],
         1,
@@ -566,11 +570,11 @@
             own_slice(fresh_out).reshape(head_rows, HD),
             attention_output_weight,
             own_rows.reshape(tile_rows, lanes),
+            feedforward_norm_gain.reshape(tile_rows, lanes),
         ),
-    ).reshape(group_rows, model_width)
-    second_normed_state = rms_norm(after_attn, feedforward_norm_gain)
-    both = jnp.stack([after_attn, second_normed_state]).reshape(2, group_rows, req_devices, width_share)
-    both = jnp.transpose(both, (2, 0, 1, 3))
+    )
+    both = both_rows.reshape(group_rows, 2, req_devices, width_share)
+    both = jnp.transpose(both, (2, 1, 0, 3))
     down_sum, both_parts = fused_mlp(
         both, gate_weight, up_weight, adapter_down_map, adapter_gate_map, adapter_up_map, down_weight, 7
     )

time: 159 us -> 159 us (level)
  other arithmetic: 12.7 us -> 10.6 us
    reshape x0 -> x2, local copies, waits for them, and re-layouts: none -> 2.34 us  [body(): both = both_rows.reshape(group_rows, 2, req_devices, width_share)]
where the time goes in v15:
time: 159 us; the launch traced here: 158 us
  Pallas kernels  121 us (76%)
  local copies, waits for them, and re-layouts  16.2 us (10%)
  other arithmetic  10.6 us (7%)
  matrix products  9.53 us (6%)
    pallas_call x2, Pallas kernels, chain(): pl.pallas_call(functools.partial(_chain_kernel, spec, len(extra)), out_sh...  52.4 us
    pallas_call x1, Pallas kernels, fused_mlp(): pl.pallas_call(_mlp_kernel, out_shape=(jax.ShapeDtypeStruct((out_rows, do...  40.7 us
    pallas_call x1, Pallas kernels, two_rounds(): pl.pallas_call(functools.partial(_two_round_kernel, (axis_a, n_a, gather_...  27.9 us
    dot_general x1, matrix products, body(): jnp.dot(spread_queries.reshape(group_rows * HEADS, head_cols), cache_k.T,...  4.83 us
    dot_general x1, matrix products, body(): jnp.dot(weights.astype(jnp.bfloat16).reshape(group_rows * HEADS, slots *...  4.22 us
    gather x2, local copies, waits for them, and re-layouts, body(): jnp.take(token_embedding_table, jnp.clip(local_ids, 0, vocab_rows - 1), a...  3.67 us

profile of v15, /device:TPU:1, one launch (start us, length us, event | category | flops | bytes accessed | tf_op | source)
XLA Modules:
  0.0 158.3 jit_solution(1807853124202017500)
XLA Ops:
  0.0 0.8 compare_and_fusion.1
  0.8 0.7 copy-done
  1.5 2.1 %gather_fusion = bf16[128,3584]{1,0:T(8,128)(2,1)} fusion(bf16[250,3584]{1,0:T(8,128)(2,1)S(1)} %copy-done, s32[1024]{0:T(1024)S(1)} %pad_clamp_fusion), kind=kCustom, calls=%fused_computation | custom fusion | bytes 1835520 | tf_op jit(solution)/shard_map/jit(_take)/gather | solution.py:393
  3.6 1.6 %gather.7 = bf16[8,16,28,128]{3,2,1,0:T(8,128)(2,1)S(1)} reshape(bf16[128,3584]{1,0:T(8,128)(2,1)} %gather_fusion) | data formatting | bytes 1835008 | tf_op jit(solution)/shard_map/jit(_take)/gather | solution.py:393
  5.2 0.0 copy-start.2
  5.2 0.1 broadcast_in_dim.150
  5.3 0.1 broadcast_in_dim.152
  5.4 1.3 select_convert_fusion.x_ref
  6.7 27.9 %shard_map.163 = bf16[16,28,128]{2,1,0:T(8,128)(2,1)} custom-call(bf16[8,16,28,128]{3,2,1,0:T(8,128)(2,1)} %select_convert_fusion.x_ref), custom_call_target="tpu_custom_call" | custom-call | tf_op jit(solution)/shard_map/pallas_call | solution.py:121
  34.6 0.9 reduce_sum.58
  35.5 0.9 fusion.24
  36.4 0.7 fusion.23
  37.1 0.7 multiply_reduce_fusion
  38.6 0.6 fusion.18.x_ref
  39.2 1.9 %copy.73.refs_0_ = bf16[896,672]{1,0:T(8,128)(2,1)} copy(bf16[896,672]{0,1:T(8,128)(2,1)S(1)} %copy-done.1) | data formatting | bytes 2408448 | tf_op args[4]
  41.1 29.9 %shard_map.164 = bf16[16,16,672]{2,1,0:T(8,128)(2,1)} custom-call(bf16[56,128]{1,0:T(8,128)(2,1)} %fusion.18.x_ref, bf16[896,672]{1,0:T(8,128)(2,1)} %copy.73.refs_0_), custom_call_target="tpu_custom_call" | custom-call | tf_op jit(solution)/shard_map/pallas_call | solution.py:302
  71.1 1.1 copy.74
  72.2 0.5 reshape.308
  72.7 0.2 reshape.320
  72.9 0.1 fusion.26
  73.0 0.1 add_convert_fusion.2
  73.1 0.1 multiply_cosine_fusion
  73.2 0.1 subtract_convert_fusion
  73.4 0.2 reshape.319
  73.5 0.1 fusion.27
  73.6 0.1 multiply_subtract_fusion
  73.8 0.1 maximum_convert_fusion
  73.9 0.0 copy-start.3
  73.9 0.3 fusion.4
  74.2 0.2 copy.83
  74.4 0.1 fusion.10
  74.5 0.1 fusion.13
  74.6 0.2 copy.88
  74.8 0.2 reshape.314
  75.0 0.2 fusion.8
  75.2 0.6 reshape.315.refs_2_
  75.8 0.7 constant_dynamic-slice_fusion
  76.5 0.2 convert_element_type.84
  76.8 1.4 broadcast_select_fusion
  78.2 0.1 iota_compare_fusion.2
  78.3 0.2 select_reduce_fusion
  78.6 0.1 copy.72
  78.7 0.1 broadcast_bitcast_fusion
  78.7 0.3 fusion.21
  79.0 0.1 copy.71
  79.1 0.1 broadcast_bitcast_fusion.1
  79.2 0.1 fusion.20
  79.3 4.8 %fusion.1 = (f32[256]{0:T(256)S(1)}, f32[256,768]{1,0:T(8,128)S(1)}) fusion(pred[4,768]{1,0:T(4,128)(4,1)S(1)} %fusion.20, bf16[256,3584]{1,0:T(8,128)(2,1)} %bitcast.77, bf16[768,3584]{1,0:T(8,128)(2,1)} %bitcast.78), kind=kOutput, calls=%fused_computation.8 | convolution fusion | flops 1409875712 | bytes 8130560 | tf_op jit(solution)/shard_map/dot_general | solution.py:480
  84.1 0.3 fusion.3
  84.4 4.2 %fusion = f32[16,3584]{1,0:T(8,128)S(1)} fusion(bf16[16,16,768]{2,1,0:T(8,128)(2,1)S(1)} %bitcast.81, bf16[768,3584,1]{1,0,2:T(8,128)(2,1)} %bitcast.90, pred[16,3584]{1,0:T(8,128)(4,1)S(1)} %iota_compare_fusion), kind=kOutput, calls=%fused_computation.4 | convolution fusion | flops 1411063808 | bytes 6184960 | tf_op jit(solution)/shard_map/dot_general | solution.py:491
  88.7 0.2 concatenate.42
  88.8 0.2 copy.78
  89.0 0.1 concatenate.44
  89.1 0.2 copy.80
  89.3 0.1 concatenate.43
  89.3 0.2 copy.79
  89.5 0.1 pad.5.clone
  89.6 0.8 maximum_bitcast_fusion.x_ref
  90.4 22.5 %shard_map.165 = bf16[16,2,56,128]{3,2,1,0:T(8,128)(2,1)} custom-call(f32[16,16,256]{2,1,0:T(8,128)} %maximum_bitcast_fusion.x_ref, f32[16,1]{1,0:T(8,128)} %bitcast.88, f32[16,1]{1,0:T(8,128)} %bitcast.87, f32[16,224]{1,0:T(8,128)} %reshape.315.refs_2_, bf16[224,7168]{1,0:T(8,128)(2,1)} %refs_3_.1, bf16[56,128]{1,0:T(8,128)(2,1)} %bitcast.85, ...), custom_call_target="tpu_custom_call" | custom-call | tf_op jit(solution)/shard_map/pallas_call | solution.py:302
  112.9 1.5 reshape.318
  114.4 0.9 copy.121
  115.3 40.7 %shard_map.166 = (f32[8,896]{1,0:T(8,128)}, bf16[8,2,16,896]{3,2,1,0:T(8,128)(2,1)}) custom-call(bf16[8,2,16,896]{3,2,1,0:T(8,128)(2,1)} %bitcast.79, bf16[896,896]{1,0:T(8,128)(2,1)} %gate_hbm.1, bf16[896,896]{1,0:T(8,128)(2,1)} %up_hbm.1, bf16[896,128]{1,0:T(8,128)(2,1)} %down_map_hbm.1, bf16[128,896]{1,0:T(8,128)(2,1)} %gate_map_hbm.1, ...), custom_call_target="tpu_custom_call" | custom-call | tf_op jit(solution)/shard_map/pallas_call | solution.py:213
  156.0 1.0 slice.31
  156.9 1.4 add_convert_fusion.1
  (21 shorter events, 0.2 us)
Async XLA Ops:
  0.0 1.5 copy-start
  5.2 33.4 %copy-start.2 = (bf16[7168]{0:T(1024)(128)(2,1)S(1)}, bf16[7168]{0:T(1024)(128)(2,1)}, u32[]{:S(2)}) copy-start(bf16[7168]{0:T(1024)(128)(2,1)} %param.20) | copy-start | bytes 43012
  6.7 32.5 %copy-start.1 = (bf16[896,672]{0,1:T(8,128)(2,1)S(1)}, bf16[896,672]{0,1:T(8,128)(2,1)}, u32[]{:S(2)}) copy-start(bf16[896,672]{0,1:T(8,128)(2,1)} %param.21) | copy-start | bytes 3612676
  71.0 2.0 %copy-start.4 = (s32[4]{0:T(128)S(1)}, s32[4]{0:T(128)}, u32[]{:S(2)}) copy-start(s32[4]{0:T(128)} %param.24) | copy-start | bytes 52
  73.9 4.4 %copy-start.3 = (s32[4,48]{1,0:T(4,128)S(1)}, s32[4,48]{1,0:T(4,128)}, u32[]{:S(2)}) copy-start(s32[4,48]{1,0:T(4,128)} %param.25) | copy-start | bytes 2308

commit v16 on v15

--- a/solution.py
+++ b/solution.py
@@ -199,7 +199,16 @@
     )
     for copy in _start_round("seq", n_seq, False, staged3, landed3, send3, recv3, local_sems.at[3]):
         copy.wait()
-    out_ref[...] = _block_sum(landed3)
+    out_rows = landed3.shape[1]
+    group_rows = spread_ref.shape[2]
+    first_row = lax.axis_index("seq") * out_rows
+    group_rows_all = spread_ref[first_row // group_rows, 0].astype(jnp.float32)
+    chunk = (first_row % group_rows) // out_rows
+    residual = group_rows_all[:out_rows]
+    for index in range(1, group_rows // out_rows):
+        piece = group_rows_all[index * out_rows : (index + 1) * out_rows]
+        residual = jnp.where(chunk == index, piece, residual)
+    out_ref[...] = (residual + _block_sum(landed3)).astype(out_ref.dtype)
 
 
 def fused_mlp(both, gate_weight, up_weight, down_map, gate_map, up_map, down_weight, cid):
@@ -213,7 +222,7 @@
     return pl.pallas_call(
         _mlp_kernel,
         out_shape=(
-            jax.ShapeDtypeStruct((out_rows, down_weight.shape[1]), jnp.float32),
+            jax.ShapeDtypeStruct((out_rows, down_weight.shape[1]), jnp.bfloat16),
             jax.ShapeDtypeStruct(both.shape, both.dtype),
         ),
         in_specs=[pl.BlockSpec(memory_space=vmem)] + [pl.BlockSpec(memory_space=pl.ANY)] * 6,
@@ -575,13 +584,10 @@
     )
     both = both_rows.reshape(group_rows, 2, req_devices, width_share)
     both = jnp.transpose(both, (2, 1, 0, 3))
-    down_sum, both_parts = fused_mlp(
+    block_out, _ = fused_mlp(
         both, gate_weight, up_weight, adapter_down_map, adapter_gate_map, adapter_up_map, down_weight, 7
     )
-    residual_cols = both_parts[:, 0].reshape(req_devices * group_rows, width_share)
-    out_rows = residual_cols.shape[0] // seq_devices
-    residual_rows = lax.dynamic_slice_in_dim(residual_cols, seq_index * out_rows, out_rows, 0)
-    return (residual_rows.astype(jnp.float32) + down_sum).astype(jnp.bfloat16)
+    return block_out
 
 
 def solution(mesh):

time: 159 us -> 158 us (level)
    unnamed x14 -> x15, local copies, waits for them, and re-layouts: 2.82 us -> 4.14 us
where the time goes in v16:
time: 158 us; the launch traced here: 157 us
  Pallas kernels  121 us (77%)
  local copies, waits for them, and re-layouts  16.5 us (10%)
  matrix products  9.53 us (6%)
  other arithmetic  9.27 us (6%)
    pallas_call x2, Pallas kernels, chain(): pl.pallas_call(functools.partial(_chain_kernel, spec, len(extra)), out_sh...  52.4 us
    pallas_call x1, Pallas kernels, fused_mlp(): pl.pallas_call(_mlp_kernel, out_shape=(jax.ShapeDtypeStruct((out_rows, do...  40.7 us
    pallas_call x1, Pallas kernels, two_rounds(): pl.pallas_call(functools.partial(_two_round_kernel, (axis_a, n_a, gather_...  27.9 us
    dot_general x1, matrix products, body(): jnp.dot(spread_queries.reshape(group_rows * HEADS, head_cols), cache_k.T,...  4.83 us
    dot_general x1, matrix products, body(): jnp.dot(weights.astype(jnp.bfloat16).reshape(group_rows * HEADS, slots *...  4.22 us
    unnamed x15, local copies, waits for them, and re-layouts  4.14 us
    gather x2, local copies, waits for them, and re-layouts, body(): jnp.take(token_embedding_table, jnp.clip(local_ids, 0, vocab_rows - 1), a...  3.67 us

profile of v16, /device:TPU:1, one launch (start us, length us, event | category | flops | bytes accessed | tf_op | source)
XLA Modules:
  0.0 157.3 jit_solution(1520586522398673068)
XLA Ops:
  0.0 0.8 compare_and_fusion.1
  0.8 0.7 copy-done
  1.5 2.1 %gather_fusion = bf16[128,3584]{1,0:T(8,128)(2,1)} fusion(bf16[250,3584]{1,0:T(8,128)(2,1)S(1)} %copy-done, s32[1024]{0:T(1024)S(1)} %pad_clamp_fusion), kind=kCustom, calls=%fused_computation | custom fusion | bytes 1835520 | tf_op jit(solution)/shard_map/jit(_take)/gather | solution.py:402
  3.6 1.6 %gather.7 = bf16[8,16,28,128]{3,2,1,0:T(8,128)(2,1)S(1)} reshape(bf16[128,3584]{1,0:T(8,128)(2,1)} %gather_fusion) | data formatting | bytes 1835008 | tf_op jit(solution)/shard_map/jit(_take)/gather | solution.py:402
  5.2 0.0 copy-start.2
  5.2 0.1 broadcast_in_dim.150
  5.3 0.1 broadcast_in_dim.152
  5.4 1.3 select_convert_fusion.x_ref
  6.7 27.9 %shard_map.163 = bf16[16,28,128]{2,1,0:T(8,128)(2,1)} custom-call(bf16[8,16,28,128]{3,2,1,0:T(8,128)(2,1)} %select_convert_fusion.x_ref), custom_call_target="tpu_custom_call" | custom-call | tf_op jit(solution)/shard_map/pallas_call | solution.py:121
  34.6 0.9 reduce_sum.58
  35.5 0.9 fusion.24
  36.4 0.7 fusion.23
  37.1 0.7 multiply_reduce_fusion
  38.6 0.6 fusion.18.x_ref
  39.2 1.9 %copy.73.refs_0_ = bf16[896,672]{1,0:T(8,128)(2,1)} copy(bf16[896,672]{0,1:T(8,128)(2,1)S(1)} %copy-done.1) | data formatting | bytes 2408448 | tf_op args[4]
  41.1 29.9 %shard_map.164 = bf16[16,16,672]{2,1,0:T(8,128)(2,1)} custom-call(bf16[56,128]{1,0:T(8,128)(2,1)} %fusion.18.x_ref, bf16[896,672]{1,0:T(8,128)(2,1)} %copy.73.refs_0_), custom_call_target="tpu_custom_call" | custom-call | tf_op jit(solution)/shard_map/pallas_call | solution.py:311
  71.0 0.0 copy-start.4
  71.1 1.1 copy.74
  72.2 0.5 reshape.308
  72.7 0.2 reshape.320
  72.9 0.1 fusion.26
  73.0 0.1 add_convert_fusion.1
  73.1 0.1 multiply_cosine_fusion
  73.2 0.1 subtract_convert_fusion
  73.4 0.2 reshape.319
  73.5 0.1 fusion.27
  73.6 0.1 multiply_subtract_fusion
  73.8 0.1 maximum_convert_fusion
  73.9 0.0 copy-start.3
  73.9 0.3 fusion.4
  74.2 0.2 copy.83
  74.4 0.1 fusion.10
  74.5 0.1 fusion.13
  74.6 0.2 copy.88
  74.8 0.2 reshape.314
  75.0 0.2 fusion.8
  75.2 0.6 reshape.315.refs_2_
  75.8 0.7 constant_dynamic-slice_fusion
  76.5 0.2 convert_element_type.78
  76.8 1.4 broadcast_select_fusion
  78.2 0.1 iota_compare_fusion.2
  78.3 0.2 select_reduce_fusion
  78.6 0.1 copy.72
  78.7 0.1 broadcast_bitcast_fusion
  78.7 0.3 fusion.21
  79.0 0.1 copy.71
  79.1 0.1 broadcast_bitcast_fusion.1
  79.2 0.1 fusion.20
  79.3 4.8 %fusion.1 = (f32[256]{0:T(256)S(1)}, f32[256,768]{1,0:T(8,128)S(1)}) fusion(pred[4,768]{1,0:T(4,128)(4,1)S(1)} %fusion.20, bf16[256,3584]{1,0:T(8,128)(2,1)} %bitcast.76, bf16[768,3584]{1,0:T(8,128)(2,1)} %bitcast.77), kind=kOutput, calls=%fused_computation.8 | convolution fusion | flops 1409875712 | bytes 8130560 | tf_op jit(solution)/shard_map/dot_general | solution.py:489
  84.1 0.3 fusion.3
  84.4 4.2 %fusion = f32[16,3584]{1,0:T(8,128)S(1)} fusion(bf16[16,16,768]{2,1,0:T(8,128)(2,1)S(1)} %bitcast.80, bf16[768,3584,1]{1,0,2:T(8,128)(2,1)} %bitcast.88, pred[16,3584]{1,0:T(8,128)(4,1)S(1)} %iota_compare_fusion), kind=kOutput, calls=%fused_computation.4 | convolution fusion | flops 1411063808 | bytes 6184960 | tf_op jit(solution)/shard_map/dot_general | solution.py:500
  88.7 0.2 concatenate.42
  88.8 0.2 copy.78
  89.0 0.1 concatenate.44
  89.1 0.2 copy.80
  89.3 0.1 concatenate.43
  89.3 0.2 copy.79
  89.5 0.1 pad.5.clone
  89.6 0.8 maximum_bitcast_fusion.x_ref
  90.4 22.5 %shard_map.165 = bf16[16,2,56,128]{3,2,1,0:T(8,128)(2,1)} custom-call(f32[16,16,256]{2,1,0:T(8,128)} %maximum_bitcast_fusion.x_ref, f32[16,1]{1,0:T(8,128)} %bitcast.86, f32[16,1]{1,0:T(8,128)} %bitcast.85, f32[16,224]{1,0:T(8,128)} %reshape.315.refs_2_, bf16[224,7168]{1,0:T(8,128)(2,1)} %refs_3_.1, bf16[56,128]{1,0:T(8,128)(2,1)} %bitcast.83, ...), custom_call_target="tpu_custom_call" | custom-call | tf_op jit(solution)/shard_map/pallas_call | solution.py:311
  113.0 1.5 reshape.318
  114.4 0.9 copy.121
  115.3 40.7 %shard_map.166 = (bf16[8,896]{1,0:T(8,128)(2,1)}, bf16[8,2,16,896]{3,2,1,0:T(8,128)(2,1)}) custom-call(bf16[8,2,16,896]{3,2,1,0:T(8,128)(2,1)} %bitcast.78, bf16[896,896]{1,0:T(8,128)(2,1)} %gate_hbm.1, bf16[896,896]{1,0:T(8,128)(2,1)} %up_hbm.1, bf16[896,128]{1,0:T(8,128)(2,1)} %down_map_hbm.1, bf16[128,896]{1,0:T(8,128)(2,1)} %gate_map_hbm.1, ...), custom_call_target="tpu_custom_call" | custom-call | tf_op jit(solution)/shard_map/pallas_call | solution.py:222
  156.0 1.3 copy.124
  (20 shorter events, 0.2 us)
Async XLA Ops:
  0.0 1.5 copy-start
  5.2 33.4 %copy-start.2 = (bf16[7168]{0:T(1024)(128)(2,1)S(1)}, bf16[7168]{0:T(1024)(128)(2,1)}, u32[]{:S(2)}) copy-start(bf16[7168]{0:T(1024)(128)(2,1)} %param.20) | copy-start | bytes 43012
  6.7 32.5 %copy-start.1 = (bf16[896,672]{0,1:T(8,128)(2,1)S(1)}, bf16[896,672]{0,1:T(8,128)(2,1)}, u32[]{:S(2)}) copy-start(bf16[896,672]{0,1:T(8,128)(2,1)} %param.21) | copy-start | bytes 3612676
  71.0 2.0 %copy-start.4 = (s32[4]{0:T(128)S(1)}, s32[4]{0:T(128)}, u32[]{:S(2)}) copy-start(s32[4]{0:T(128)} %param.24) | copy-start | bytes 52
  73.9 4.4 %copy-start.3 = (s32[4,48]{1,0:T(4,128)S(1)}, s32[4,48]{1,0:T(4,128)}, u32[]{:S(2)}) copy-start(s32[4,48]{1,0:T(4,128)} %param.25) | copy-start | bytes 2308

commit v17 on v16

--- a/solution.py
+++ b/solution.py
@@ -149,7 +149,7 @@
     x_ref, gate_hbm, up_hbm, down_map_hbm, gate_map_hbm, up_map_hbm, down_hbm,
     out_ref, spread_ref, landed1, staged1, staged2, landed2, staged3, landed3,
     send0, recv0, send1, recv1, send2, recv2, send3, recv3, local_sems,
-    gate_ref, up_ref, down_map_ref, gate_map_ref, up_map_ref, down_ref, weight_sems,
+    gate_ref, up_ref, down_map_ref, gate_map_ref, up_map_ref, down_ref, weight_sems, staged0,
 ):
     n_req = spread_ref.shape[0]
     n_seq = landed3.shape[0]
@@ -165,7 +165,12 @@
         load.start()
         loads.append(load)
     _greet([("req", n_req), ("seq", n_seq)])
-    for copy in _start_round("req", n_req, False, x_ref, spread_ref, send0, recv0, local_sems.at[0]):
+    share = staged0.shape[3]
+    for kind in range(staged0.shape[1]):
+        full_rows = x_ref[:, kind].reshape(staged0.shape[2], n_req * share)
+        for part in range(n_req):
+            staged0[part, kind] = full_rows[:, part * share : (part + 1) * share]
+    for copy in _start_round("req", n_req, False, staged0, spread_ref, send0, recv0, local_sems.at[0]):
         copy.wait()
     for load in loads[:3]:
         load.wait()
@@ -213,7 +218,8 @@
 
 def fused_mlp(both, gate_weight, up_weight, down_map, gate_map, up_map, down_weight, cid):
     n_req, n_seq = lax.axis_size("req"), lax.axis_size("seq")
-    group_rows = both.shape[2]
+    group_rows = both.shape[0]
+    spread_shape = (n_req, both.shape[1], group_rows, both.shape[2] * both.shape[3] // n_req)
     rows = n_req * group_rows
     units = gate_weight.shape[1]
     wide = 2 * units + down_map.shape[1]
@@ -223,7 +229,7 @@
         _mlp_kernel,
         out_shape=(
             jax.ShapeDtypeStruct((out_rows, down_weight.shape[1]), jnp.bfloat16),
-            jax.ShapeDtypeStruct(both.shape, both.dtype),
+            jax.ShapeDtypeStruct(spread_shape, both.dtype),
         ),
         in_specs=[pl.BlockSpec(memory_space=vmem)] + [pl.BlockSpec(memory_space=pl.ANY)] * 6,
         out_specs=(pl.BlockSpec(memory_space=vmem), pl.BlockSpec(memory_space=vmem)),
@@ -248,7 +254,7 @@
             vmem(weight.shape, weight.dtype)
             for weight in (gate_weight, up_weight, down_map, gate_map, up_map, down_weight)
         ]
-        + [pltpu.SemaphoreType.DMA((6,))],
+        + [pltpu.SemaphoreType.DMA((6,)), vmem(spread_shape, both.dtype)],
         compiler_params=pltpu.CompilerParams(
             collective_id=cid, has_side_effects=True
         ),
@@ -582,10 +588,8 @@
             feedforward_norm_gain.reshape(tile_rows, lanes),
         ),
     )
-    both = both_rows.reshape(group_rows, 2, req_devices, width_share)
-    both = jnp.transpose(both, (2, 1, 0, 3))
     block_out, _ = fused_mlp(
-        both, gate_weight, up_weight, adapter_down_map, adapter_gate_map, adapter_up_map, down_weight, 7
+        both_rows, gate_weight, up_weight, adapter_down_map, adapter_gate_map, adapter_up_map, down_weight, 7
     )
     return block_out
 

time: 158 us -> 156 us (0.987)
  local copies, waits for them, and re-layouts: 16.5 us -> 14.2 us
    reshape x2 -> x0, local copies, waits for them, and re-layouts: 2.34 us -> none  [body(): both = both_rows.reshape(group_rows, 2, req_devices, width_share)]
where the time goes in v17:
time: 156 us; the launch traced here: 155 us
  Pallas kernels  121 us (78%)
  local copies, waits for them, and re-layouts  14.2 us (9%)
  matrix products  9.53 us (6%)
  other arithmetic  9.27 us (6%)
    pallas_call x2, Pallas kernels, chain(): pl.pallas_call(functools.partial(_chain_kernel, spec, len(extra)), out_sh...  52.2 us
    pallas_call x1, Pallas kernels, fused_mlp(): pl.pallas_call(_mlp_kernel, out_shape=(jax.ShapeDtypeStruct((out_rows, do...  41.1 us
    pallas_call x1, Pallas kernels, two_rounds(): pl.pallas_call(functools.partial(_two_round_kernel, (axis_a, n_a, gather_...  27.9 us
    dot_general x1, matrix products, body(): jnp.dot(spread_queries.reshape(group_rows * HEADS, head_cols), cache_k.T,...  4.83 us
    dot_general x1, matrix products, body(): jnp.dot(weights.astype(jnp.bfloat16).reshape(group_rows * HEADS, slots *...  4.22 us
    unnamed x15, local copies, waits for them, and re-layouts  4.14 us
    gather x2, local copies, waits for them, and re-layouts, body(): jnp.take(token_embedding_table, jnp.clip(local_ids, 0, vocab_rows - 1), a...  3.67 us

profile of v17, /device:TPU:1, one launch (start us, length us, event | category | flops | bytes accessed | tf_op | source)
XLA Modules:
  0.0 155.2 jit_solution(7172662967022685171)
XLA Ops:
  0.0 0.0 copy-start
  0.0 0.8 compare_and_fusion.1
  0.8 0.7 copy-done
  1.5 2.1 %gather_fusion = bf16[128,3584]{1,0:T(8,128)(2,1)} fusion(bf16[250,3584]{1,0:T(8,128)(2,1)S(1)} %copy-done, s32[1024]{0:T(1024)S(1)} %pad_clamp_fusion), kind=kCustom, calls=%fused_computation | custom fusion | bytes 1835520 | tf_op jit(solution)/shard_map/jit(_take)/gather | solution.py:408
  3.6 1.6 %gather.7 = bf16[8,16,28,128]{3,2,1,0:T(8,128)(2,1)S(1)} reshape(bf16[128,3584]{1,0:T(8,128)(2,1)} %gather_fusion) | data formatting | bytes 1835008 | tf_op jit(solution)/shard_map/jit(_take)/gather | solution.py:408
  5.2 0.0 copy-start.2
  5.2 0.1 broadcast_in_dim.150
  5.3 0.1 broadcast_in_dim.152
  5.4 1.3 select_convert_fusion.x_ref
  6.7 27.9 %shard_map.163 = bf16[16,28,128]{2,1,0:T(8,128)(2,1)} custom-call(bf16[8,16,28,128]{3,2,1,0:T(8,128)(2,1)} %select_convert_fusion.x_ref), custom_call_target="tpu_custom_call" | custom-call | tf_op jit(solution)/shard_map/pallas_call | solution.py:121
  34.6 0.9 reduce_sum.58
  35.5 0.9 fusion.24
  36.4 0.7 fusion.23
  37.1 0.7 multiply_reduce_fusion
  38.6 0.0 copy-done.2
  38.6 0.6 fusion.18.x_ref
  39.2 1.9 %copy.70.refs_0_ = bf16[896,672]{1,0:T(8,128)(2,1)} copy(bf16[896,672]{0,1:T(8,128)(2,1)S(1)} %copy-done.1) | data formatting | bytes 2408448 | tf_op args[4]
  41.1 29.9 %shard_map.164 = bf16[16,16,672]{2,1,0:T(8,128)(2,1)} custom-call(bf16[56,128]{1,0:T(8,128)(2,1)} %fusion.18.x_ref, bf16[896,672]{1,0:T(8,128)(2,1)} %copy.70.refs_0_), custom_call_target="tpu_custom_call" | custom-call | tf_op jit(solution)/shard_map/pallas_call | solution.py:317
  71.0 0.0 copy-start.4
  71.1 1.1 copy.71
  72.2 0.5 reshape.305
  72.7 0.2 reshape.316
  72.9 0.1 fusion.26
  73.0 0.1 add_convert_fusion.1
  73.1 0.1 multiply_cosine_fusion
  73.2 0.1 subtract_convert_fusion
  73.4 0.2 reshape.315
  73.5 0.1 fusion.27
  73.6 0.1 multiply_subtract_fusion
  73.8 0.1 maximum_convert_fusion
  73.9 0.0 copy-start.3
  73.9 0.3 fusion.4
  74.2 0.2 copy.80
  74.4 0.1 fusion.10
  74.5 0.1 fusion.13
  74.6 0.2 copy.85
  74.8 0.2 reshape.311
  75.0 0.2 fusion.8
  75.2 0.6 reshape.312.refs_2_
  75.8 0.7 constant_dynamic-slice_fusion
  76.5 0.2 convert_element_type.78
  76.8 1.4 broadcast_select_fusion
  78.2 0.1 iota_compare_fusion.2
  78.3 0.2 select_reduce_fusion
  78.6 0.1 copy.69
  78.7 0.1 broadcast_bitcast_fusion
  78.8 0.3 fusion.21
  79.0 0.1 copy.68
  79.1 0.1 broadcast_bitcast_fusion.1
  79.2 0.1 fusion.20
  79.3 4.8 %fusion.1 = (f32[256]{0:T(256)S(1)}, f32[256,768]{1,0:T(8,128)S(1)}) fusion(pred[4,768]{1,0:T(4,128)(4,1)S(1)} %fusion.20, bf16[256,3584]{1,0:T(8,128)(2,1)} %bitcast.71, bf16[768,3584]{1,0:T(8,128)(2,1)} %bitcast.72), kind=kOutput, calls=%fused_computation.8 | convolution fusion | flops 1409875712 | bytes 8130560 | tf_op jit(solution)/shard_map/dot_general | solution.py:495
  84.1 0.3 fusion.3
  84.4 4.2 %fusion = f32[16,3584]{1,0:T(8,128)S(1)} fusion(bf16[16,16,768]{2,1,0:T(8,128)(2,1)S(1)} %bitcast.74, bf16[768,3584,1]{1,0,2:T(8,128)(2,1)} %bitcast.82, pred[16,3584]{1,0:T(8,128)(4,1)S(1)} %iota_compare_fusion), kind=kOutput, calls=%fused_computation.4 | convolution fusion | flops 1411063808 | bytes 6184960 | tf_op jit(solution)/shard_map/dot_general | solution.py:506
  88.7 0.2 concatenate.42
  88.8 0.2 copy.75
  89.0 0.1 concatenate.44
  89.1 0.2 copy.77
  89.3 0.1 concatenate.43
  89.3 0.2 copy.76
  89.5 0.1 pad.5.clone
  89.6 0.8 maximum_bitcast_fusion.x_ref
  90.4 22.3 %shard_map.165.x_ref = bf16[16,2,56,128]{3,2,1,0:T(8,128)(2,1)} custom-call(f32[16,16,256]{2,1,0:T(8,128)} %maximum_bitcast_fusion.x_ref, f32[16,1]{1,0:T(8,128)} %bitcast.80, f32[16,1]{1,0:T(8,128)} %bitcast.79, f32[16,224]{1,0:T(8,128)} %reshape.312.refs_2_, bf16[224,7168]{1,0:T(8,128)(2,1)} %refs_3_.1, bf16[56,128]{1,0:T(8,128)(2,1)} %bitcast.77, ...), custom_call_target="tpu_custom_call" | custom-call | tf_op jit(solution)/shard_map/pallas_call | solution.py:317
  112.7 41.1 %shard_map.166 = (bf16[8,896]{1,0:T(8,128)(2,1)}, bf16[8,2,16,896]{3,2,1,0:T(8,128)(2,1)}) custom-call(bf16[16,2,56,128]{3,2,1,0:T(8,128)(2,1)} %shard_map.165.x_ref, bf16[896,896]{1,0:T(8,128)(2,1)} %gate_hbm.1, bf16[896,896]{1,0:T(8,128)(2,1)} %up_hbm.1, bf16[896,128]{1,0:T(8,128)(2,1)} %down_map_hbm.1, bf16[128,896]{1,0:T(8,128)(2,1)} %gate_map_hbm.1, ...), custom_call_target="tpu_custom_call" | custom-call | tf_op jit(solution)/shard_map/pallas_call | solution.py:228
  153.9 1.3 copy.118
  (18 shorter events, 0.2 us)
Async XLA Ops:
  0.0 1.5 copy-start
  5.2 33.4 %copy-start.2 = (bf16[7168]{0:T(1024)(128)(2,1)S(1)}, bf16[7168]{0:T(1024)(128)(2,1)}, u32[]{:S(2)}) copy-start(bf16[7168]{0:T(1024)(128)(2,1)} %param.20) | copy-start | bytes 43012
  6.7 32.5 %copy-start.1 = (bf16[896,672]{0,1:T(8,128)(2,1)S(1)}, bf16[896,672]{0,1:T(8,128)(2,1)}, u32[]{:S(2)}) copy-start(bf16[896,672]{0,1:T(8,128)(2,1)} %param.21) | copy-start | bytes 3612676
  71.0 2.0 %copy-start.4 = (s32[4]{0:T(128)S(1)}, s32[4]{0:T(128)}, u32[]{:S(2)}) copy-start(s32[4]{0:T(128)} %param.24) | copy-start | bytes 52
  73.9 4.4 %copy-start.3 = (s32[4,48]{1,0:T(4,128)S(1)}, s32[4,48]{1,0:T(4,128)}, u32[]{:S(2)}) copy-start(s32[4,48]{1,0:T(4,128)} %param.25) | copy-start | bytes 2308

commit v18 on v17

--- a/solution.py
+++ b/solution.py
@@ -261,7 +261,7 @@
     )(both, gate_weight, up_weight, down_map, gate_map, up_map, down_weight)
 
 
-def _chain_kernel(spec, n_extra, x_ref, *refs):
+def _chain_kernel(spec, n_extra, pre, x_ref, *refs):
     extra_hbm = refs[:n_extra]
     y_ref = refs[n_extra]
     scratch = refs[n_extra + 1 :]
@@ -270,12 +270,18 @@
     staged = scratch[count - 1 : 2 * count - 2]
     extra = scratch[2 * count - 2 : 2 * count - 2 + n_extra]
     extra_sems = scratch[2 * count - 2 + n_extra]
-    sems = scratch[2 * count - 1 + n_extra :]
+    sems = scratch[2 * count - 1 + n_extra : len(scratch) - (pre is not None)]
     loads = []
     for index in range(n_extra):
         load = pltpu.make_async_copy(extra_hbm[index], extra[index], extra_sems.at[index])
         load.start()
         loads.append(load)
+    if pre is not None:
+        for load in loads:
+            load.wait()
+        loads = []
+        scratch[-1][...] = pre(x_ref, *extra)
+        x_ref = scratch[-1]
     axes = []
     for axis, n, _, _ in spec:
         if (axis, n) not in axes:
@@ -296,7 +302,7 @@
             source = staged[k]
 
 
-def chain(x, rounds, cid, extra=()):
+def chain(x, rounds, cid, extra=(), pre=None):
     spec, landed_shapes, staged_shapes = [], [], []
     block = (x.shape, x.dtype)
     for index, (axis, gather, mid, made) in enumerate(rounds):
@@ -315,7 +321,7 @@
     for n in sizes:
         semaphores += [pltpu.SemaphoreType.DMA((n,)), pltpu.SemaphoreType.DMA((n,))]
     return pl.pallas_call(
-        functools.partial(_chain_kernel, spec, len(extra)),
+        functools.partial(_chain_kernel, spec, len(extra), pre),
         out_shape=jax.ShapeDtypeStruct(*out),
         in_specs=[pl.BlockSpec(memory_space=pltpu.VMEM)]
         + [pl.BlockSpec(memory_space=pl.ANY)] * len(extra),
@@ -325,7 +331,8 @@
         + [pltpu.VMEM(item.shape, item.dtype) for item in extra]
         + [pltpu.SemaphoreType.DMA((max(len(extra), 1),))]
         + semaphores
-        + [pltpu.SemaphoreType.DMA((len(spec),))],
+        + [pltpu.SemaphoreType.DMA((len(spec),))]
+        + ([pltpu.VMEM(x.shape, x.dtype)] if pre is not None else []),
         compiler_params=pltpu.CompilerParams(
             collective_id=cid, has_side_effects=True
         ),
@@ -428,11 +435,15 @@
     )
     own_hidden = lax.dynamic_slice_in_dim(hidden, seq_index * row_share, row_share, 0)
     own_rows = jnp.concatenate([own_hidden, embedded_rows], axis=1)
-    normed_rows = rms_norm(own_rows, attention_norm_gain)
     model_width = own_rows.shape[1]
     width_share = model_width // req_devices
 
-    def to_owners(landed, weight):
+    def normalize(joined_tiles, weight, gain):
+        widened = joined_tiles[...].astype(jnp.float32)
+        factor = lax.rsqrt(jnp.sum(widened * widened) / model_width + EPSILON)
+        return (widened * factor * gain[...].astype(jnp.float32)).astype(jnp.bfloat16)
+
+    def to_owners(landed, weight, gain):
         rows = landed[...].reshape(group_rows, model_width)
         return jnp.stack(
             [rows[:, part * width_share : (part + 1) * width_share] for part in range(req_devices)]
@@ -440,26 +451,27 @@
 
     qkv_cols = query_key_value_weight.shape[1]
 
-    def project(landed, weight):
+    def project(landed, weight, gain):
         flat = landed[...].reshape(req_devices * group_rows, width_share)
         product = jnp.dot(flat, weight[...], preferred_element_type=jnp.float32)
         return product.reshape(req_devices, group_rows, qkv_cols)
 
     qkv_all = chain(
-        normed_rows.reshape(-1, lanes),
+        own_rows.reshape(-1, lanes),
         [
             ("seq", True, to_owners, ((req_devices, group_rows, width_share), jnp.bfloat16)),
             ("req", False, project, ((req_devices, group_rows, qkv_cols), jnp.float32)),
             (
                 "req",
                 False,
-                lambda landed, weight: _block_sum(landed).astype(jnp.bfloat16),
+                lambda landed, weight, gain: _block_sum(landed).astype(jnp.bfloat16),
                 ((group_rows, qkv_cols), jnp.bfloat16),
             ),
             ("seq", True, None, None),
         ],
         4,
-        extra=(query_key_value_weight,),
+        extra=(query_key_value_weight, attention_norm_gain.reshape(-1, lanes)),
+        pre=normalize,
     )
     projected = jnp.transpose(qkv_all, (1, 0, 2)).reshape(group_rows, seq_devices * qkv_all.shape[2])
     head_cols = HEADS * HD

time: 156 us -> 155 us (level)
  Pallas kernels: 121 us -> 123 us
    unnamed x15 -> x13, local copies, waits for them, and re-layouts: 4.14 us -> 4.13 us
where the time goes in v18:
time: 155 us
  Pallas kernels  123 us (79%)
  local copies, waits for them, and re-layouts  14.1 us (9%)
  matrix products  9.53 us (6%)
  other arithmetic  7.92 us (5%)
    pallas_call x2, Pallas kernels, chain(): pl.pallas_call(functools.partial(_chain_kernel, spec, len(extra), pre), o...  53.7 us
    pallas_call x1, Pallas kernels, fused_mlp(): pl.pallas_call(_mlp_kernel, out_shape=(jax.ShapeDtypeStruct((out_rows, do...  41.3 us
    pallas_call x1, Pallas kernels, two_rounds(): pl.pallas_call(functools.partial(_two_round_kernel, (axis_a, n_a, gather_...  27.8 us
    dot_general x1, matrix products, body(): jnp.dot(spread_queries.reshape(group_rows * HEADS, head_cols), cache_k.T,...  4.83 us
    dot_general x1, matrix products, body(): jnp.dot(weights.astype(jnp.bfloat16).reshape(group_rows * HEADS, slots *...  4.22 us
    unnamed x13, local copies, waits for them, and re-layouts  4.13 us
    gather x2, local copies, waits for them, and re-layouts, body(): jnp.take(token_embedding_table, jnp.clip(local_ids, 0, vocab_rows - 1), a...  3.67 us

profile of v18, /device:TPU:1, one launch (start us, length us, event | category | flops | bytes accessed | tf_op | source)
XLA Modules:
  0.0 154.6 jit_solution(5128768122545626972)
XLA Ops:
  0.0 0.0 copy-start
  0.0 0.8 compare_and_fusion.1
  0.8 0.7 copy-done
  1.5 2.1 %gather_fusion = bf16[128,3584]{1,0:T(8,128)(2,1)} fusion(bf16[250,3584]{1,0:T(8,128)(2,1)S(1)} %copy-done, s32[1024]{0:T(1024)S(1)} %pad_clamp_fusion), kind=kCustom, calls=%fused_computation | custom fusion | bytes 1835520 | tf_op jit(solution)/shard_map/jit(_take)/gather | solution.py:415
  3.6 1.6 %gather.7 = bf16[8,16,28,128]{3,2,1,0:T(8,128)(2,1)S(1)} reshape(bf16[128,3584]{1,0:T(8,128)(2,1)} %gather_fusion) | data formatting | bytes 1835008 | tf_op jit(solution)/shard_map/jit(_take)/gather | solution.py:415
  5.2 0.1 broadcast_in_dim.148
  5.3 0.1 broadcast_in_dim.150
  5.4 1.3 select_convert_fusion.x_ref
  6.7 0.0 copy-start.1
  6.7 27.8 %shard_map.163 = bf16[16,28,128]{2,1,0:T(8,128)(2,1)} custom-call(bf16[8,16,28,128]{3,2,1,0:T(8,128)(2,1)} %select_convert_fusion.x_ref), custom_call_target="tpu_custom_call" | custom-call | tf_op jit(solution)/shard_map/pallas_call | solution.py:121
  34.5 0.9 reduce_sum.49
  35.5 0.8 constant_dynamic-slice_fusion.2
  36.3 0.7 maximum_reduce_fusion
  37.0 0.0 copy-done.1
  37.0 1.9 %copy.70.refs_0_ = bf16[896,672]{1,0:T(8,128)(2,1)} copy(bf16[896,672]{0,1:T(8,128)(2,1)S(1)} %copy-done.1) | data formatting | bytes 2408448 | tf_op args[4]
  39.0 31.5 %shard_map.164 = bf16[16,16,672]{2,1,0:T(8,128)(2,1)} custom-call(bf16[56,128]{1,0:T(8,128)(2,1)} %bitcast.73, bf16[896,672]{1,0:T(8,128)(2,1)} %copy.70.refs_0_, bf16[56,128]{1,0:T(8,128)(2,1)} %bitcast.79), custom_call_target="tpu_custom_call" | custom-call | tf_op jit(solution)/shard_map/pallas_call | solution.py:323
  70.4 0.0 copy-start.3
  70.5 1.1 copy.71
  71.6 0.5 reshape.260
  72.1 0.2 reshape.269
  72.3 0.1 fusion.24
  72.4 0.0 copy-done.3
  72.4 0.1 add_convert_fusion.1
  72.5 0.1 multiply_cosine_fusion
  72.7 0.1 multiply_subtract_fusion
  72.8 0.1 maximum_convert_fusion
  72.9 0.2 reshape.270
  73.1 0.1 fusion.23
  73.2 0.1 subtract_convert_fusion
  73.3 0.0 copy-start.2
  73.3 0.3 fusion.4
  73.6 0.2 copy.80
  73.8 0.1 fusion.10
  73.9 0.1 fusion.13
  74.0 0.2 copy.85
  74.2 0.2 reshape.266
  74.4 0.2 fusion.8
  74.6 0.6 reshape.267.refs_2_
  75.3 0.7 constant_dynamic-slice_fusion
  76.0 0.2 convert_element_type.54
  76.2 1.4 broadcast_select_fusion
  77.7 0.1 iota_compare_fusion.2
  77.7 0.0 copy-done.2
  77.7 0.2 select_reduce_fusion
  78.0 0.1 copy.69
  78.1 0.1 broadcast_bitcast_fusion
  78.2 0.3 fusion.20
  78.4 0.1 copy.68
  78.5 0.1 broadcast_bitcast_fusion.1
  78.6 0.1 fusion.19
  78.7 4.8 %fusion.1 = (f32[256]{0:T(256)S(1)}, f32[256,768]{1,0:T(8,128)S(1)}) fusion(pred[4,768]{1,0:T(4,128)(4,1)S(1)} %fusion.19, bf16[256,3584]{1,0:T(8,128)(2,1)} %bitcast.69, bf16[768,3584]{1,0:T(8,128)(2,1)} %bitcast.70), kind=kOutput, calls=%fused_computation.8 | convolution fusion | flops 1409875712 | bytes 8130560 | tf_op jit(solution)/shard_map/dot_general | solution.py:507
  83.5 0.3 fusion.3
  83.8 4.2 %fusion = f32[16,3584]{1,0:T(8,128)S(1)} fusion(bf16[16,16,768]{2,1,0:T(8,128)(2,1)S(1)} %bitcast.72, bf16[768,3584,1]{1,0,2:T(8,128)(2,1)} %bitcast.81, pred[16,3584]{1,0:T(8,128)(4,1)S(1)} %iota_compare_fusion), kind=kOutput, calls=%fused_computation.4 | convolution fusion | flops 1411063808 | bytes 6184960 | tf_op jit(solution)/shard_map/dot_general | solution.py:518
  88.1 0.2 concatenate.22
  88.2 0.2 copy.75
  88.4 0.1 concatenate.24
  88.5 0.2 copy.77
  88.7 0.1 concatenate.23
  88.7 0.2 copy.76
  88.9 0.1 pad.5.clone
  89.0 0.8 maximum_bitcast_fusion.x_ref
  89.9 22.2 %shard_map.165.x_ref = bf16[16,2,56,128]{3,2,1,0:T(8,128)(2,1)} custom-call(f32[16,16,256]{2,1,0:T(8,128)} %maximum_bitcast_fusion.x_ref, f32[16,1]{1,0:T(8,128)} %bitcast.77, f32[16,1]{1,0:T(8,128)} %bitcast.76, f32[16,224]{1,0:T(8,128)} %reshape.267.refs_2_, bf16[224,7168]{1,0:T(8,128)(2,1)} %refs_3_.1, bf16[56,128]{1,0:T(8,128)(2,1)} %bitcast.74, ...), custom_call_target="tpu_custom_call" | custom-call | tf_op jit(solution)/shard_map/pallas_call | solution.py:323
  112.1 41.3 %shard_map.166 = (bf16[8,896]{1,0:T(8,128)(2,1)}, bf16[8,2,16,896]{3,2,1,0:T(8,128)(2,1)}) custom-call(bf16[16,2,56,128]{3,2,1,0:T(8,128)(2,1)} %shard_map.165.x_ref, bf16[896,896]{1,0:T(8,128)(2,1)} %gate_hbm.1, bf16[896,896]{1,0:T(8,128)(2,1)} %up_hbm.1, bf16[896,128]{1,0:T(8,128)(2,1)} %down_map_hbm.1, bf16[128,896]{1,0:T(8,128)(2,1)} %gate_map_hbm.1, ...), custom_call_target="tpu_custom_call" | custom-call | tf_op jit(solution)/shard_map/pallas_call | solution.py:228
  153.3 1.3 copy.118
  (14 shorter events, 0.2 us)
Async XLA Ops:
  0.0 1.5 copy-start
  6.7 30.4 %copy-start.1 = (bf16[896,672]{0,1:T(8,128)(2,1)S(1)}, bf16[896,672]{0,1:T(8,128)(2,1)}, u32[]{:S(2)}) copy-start(bf16[896,672]{0,1:T(8,128)(2,1)} %param.21) | copy-start | bytes 3612676
  70.4 2.0 %copy-start.3 = (s32[4]{0:T(128)S(1)}, s32[4]{0:T(128)}, u32[]{:S(2)}) copy-start(s32[4]{0:T(128)} %param.24) | copy-start | bytes 52
  73.3 4.4 %copy-start.2 = (s32[4,48]{1,0:T(4,128)S(1)}, s32[4,48]{1,0:T(4,128)}, u32[]{:S(2)}) copy-start(s32[4,48]{1,0:T(4,128)} %param.25) | copy-start | bytes 2308

commit v19 on v18

--- a/solution.py
+++ b/solution.py
@@ -412,10 +412,8 @@
     first_id = (seq_index * req_devices + req_index) * vocab_rows
     local_ids = given_token_index - first_id
     present = (local_ids >= 0) & (local_ids < vocab_rows)
-    looked = jnp.take(token_embedding_table, jnp.clip(local_ids, 0, vocab_rows - 1), axis=0).astype(
-        jnp.float32
-    )
-    looked = jnp.where(present[:, None], looked, 0.0).astype(jnp.bfloat16)
+    looked = jnp.take(token_embedding_table, jnp.clip(local_ids, 0, vocab_rows - 1), axis=0)
+    looked = jnp.where(present[:, None], looked, jnp.zeros((), looked.dtype))
     row_share = group_rows // seq_devices
     lanes = 128
     by_group = looked.reshape(req_devices, seq_devices, row_share * looked.shape[1] // lanes, lanes)

time: 155 us -> 155 us (level)
  no operation moved by 1% of the time
where the time goes in v19:
time: 155 us
  Pallas kernels  123 us (79%)
  local copies, waits for them, and re-layouts  14.1 us (9%)
  matrix products  9.52 us (6%)
  other arithmetic  7.85 us (5%)
    pallas_call x2, Pallas kernels, chain(): pl.pallas_call(functools.partial(_chain_kernel, spec, len(extra), pre), o...  53.7 us
    pallas_call x1, Pallas kernels, fused_mlp(): pl.pallas_call(_mlp_kernel, out_shape=(jax.ShapeDtypeStruct((out_rows, do...  41.2 us
    pallas_call x1, Pallas kernels, two_rounds(): pl.pallas_call(functools.partial(_two_round_kernel, (axis_a, n_a, gather_...  27.8 us
    dot_general x1, matrix products, body(): jnp.dot(spread_queries.reshape(group_rows * HEADS, head_cols), cache_k.T,...  4.83 us
    dot_general x1, matrix products, body(): jnp.dot(weights.astype(jnp.bfloat16).reshape(group_rows * HEADS, slots *...  4.22 us
    unnamed x13, local copies, waits for them, and re-layouts  4.13 us
    gather x2, local copies, waits for them, and re-layouts, body(): jnp.take(token_embedding_table, jnp.clip(local_ids, 0, vocab_rows - 1), a...  3.67 us

profile of v19, /device:TPU:1, one launch (start us, length us, event | category | flops | bytes accessed | tf_op | source)
XLA Modules:
  0.0 154.5 jit_solution(8330136504662911032)
XLA Ops:
  0.0 0.0 copy-start
  0.0 0.8 compare_and_fusion.1
  0.8 0.7 copy-done
  1.5 2.1 %gather_fusion = bf16[128,3584]{1,0:T(8,128)(2,1)} fusion(bf16[250,3584]{1,0:T(8,128)(2,1)S(1)} %copy-done, s32[1024]{0:T(1024)S(1)} %pad_clamp_fusion), kind=kCustom, calls=%fused_computation | custom fusion | bytes 1835520 | tf_op jit(solution)/shard_map/jit(_take)/gather | solution.py:415
  3.6 1.6 %gather.7 = bf16[8,16,28,128]{3,2,1,0:T(8,128)(2,1)S(1)} reshape(bf16[128,3584]{1,0:T(8,128)(2,1)} %gather_fusion) | data formatting | bytes 1835008 | tf_op jit(solution)/shard_map/jit(_take)/gather | solution.py:415
  5.2 0.1 broadcast_in_dim.148
  5.3 0.1 broadcast_in_dim.150
  5.4 1.3 select_select_fusion.x_ref
  6.6 0.0 copy-start.1
  6.6 27.8 %shard_map.163 = bf16[16,28,128]{2,1,0:T(8,128)(2,1)} custom-call(bf16[8,16,28,128]{3,2,1,0:T(8,128)(2,1)} %select_select_fusion.x_ref), custom_call_target="tpu_custom_call" | custom-call | tf_op jit(solution)/shard_map/pallas_call | solution.py:121
  34.5 0.9 reduce_sum.49
  35.4 0.8 constant_dynamic-slice_fusion.2
  36.3 0.7 maximum_reduce_fusion
  37.0 0.0 copy-done.1
  37.0 1.9 %copy.70.refs_0_ = bf16[896,672]{1,0:T(8,128)(2,1)} copy(bf16[896,672]{0,1:T(8,128)(2,1)S(1)} %copy-done.1) | data formatting | bytes 2408448 | tf_op args[4]
  38.9 31.5 %shard_map.164 = bf16[16,16,672]{2,1,0:T(8,128)(2,1)} custom-call(bf16[56,128]{1,0:T(8,128)(2,1)} %bitcast.73, bf16[896,672]{1,0:T(8,128)(2,1)} %copy.70.refs_0_, bf16[56,128]{1,0:T(8,128)(2,1)} %bitcast.79), custom_call_target="tpu_custom_call" | custom-call | tf_op jit(solution)/shard_map/pallas_call | solution.py:323
  70.4 0.0 copy-start.3
  70.4 1.1 copy.71
  71.5 0.5 reshape.260
  72.1 0.2 reshape.269
  72.3 0.1 fusion.24
  72.4 0.0 copy-done.3
  72.4 0.1 add_convert_fusion.1
  72.4 0.1 multiply_cosine_fusion
  72.6 0.1 multiply_subtract_fusion
  72.7 0.1 maximum_convert_fusion
  72.9 0.2 reshape.270
  73.0 0.1 fusion.23
  73.1 0.1 subtract_convert_fusion
  73.3 0.3 fusion.4
  73.5 0.2 copy.80
  73.7 0.0 copy-start.2
  73.7 0.1 fusion.10
  73.8 0.1 fusion.13
  74.0 0.2 copy.85
  74.1 0.2 reshape.266
  74.3 0.2 fusion.8
  74.6 0.6 reshape.267.refs_2_
  75.2 0.7 constant_dynamic-slice_fusion
  75.9 0.2 convert_element_type.44
  76.1 1.4 broadcast_select_fusion
  77.6 0.1 iota_compare_fusion.2
  77.7 0.0 copy-done.2
  77.7 0.2 select_reduce_fusion
  77.9 0.1 copy.69
  78.0 0.1 broadcast_bitcast_fusion
  78.1 0.3 fusion.20
  78.3 0.1 copy.68
  78.5 0.1 broadcast_bitcast_fusion.1
  78.5 0.1 fusion.19
  78.6 4.8 %fusion.1 = (f32[256]{0:T(256)S(1)}, f32[256,768]{1,0:T(8,128)S(1)}) fusion(pred[4,768]{1,0:T(4,128)(4,1)S(1)} %fusion.19, bf16[256,3584]{1,0:T(8,128)(2,1)} %bitcast.69, bf16[768,3584]{1,0:T(8,128)(2,1)} %bitcast.70), kind=kOutput, calls=%fused_computation.8 | convolution fusion | flops 1409875712 | bytes 8130560 | tf_op jit(solution)/shard_map/dot_general | solution.py:505
  83.4 0.3 fusion.3
  83.8 4.2 %fusion = f32[16,3584]{1,0:T(8,128)S(1)} fusion(bf16[16,16,768]{2,1,0:T(8,128)(2,1)S(1)} %bitcast.72, bf16[768,3584,1]{1,0,2:T(8,128)(2,1)} %bitcast.81, pred[16,3584]{1,0:T(8,128)(4,1)S(1)} %iota_compare_fusion), kind=kOutput, calls=%fused_computation.3 | convolution fusion | flops 1411063808 | bytes 6184960 | tf_op jit(solution)/shard_map/dot_general | solution.py:516
  88.0 0.2 concatenate.22
  88.2 0.2 copy.75
  88.3 0.1 concatenate.24
  88.4 0.2 copy.77
  88.6 0.1 concatenate.23
  88.7 0.2 copy.76
  88.9 0.1 pad.5.clone
  88.9 0.8 maximum_bitcast_fusion.x_ref
  89.8 22.3 %shard_map.165.x_ref = bf16[16,2,56,128]{3,2,1,0:T(8,128)(2,1)} custom-call(f32[16,16,256]{2,1,0:T(8,128)} %maximum_bitcast_fusion.x_ref, f32[16,1]{1,0:T(8,128)} %bitcast.77, f32[16,1]{1,0:T(8,128)} %bitcast.76, f32[16,224]{1,0:T(8,128)} %reshape.267.refs_2_, bf16[224,7168]{1,0:T(8,128)(2,1)} %refs_3_.1, bf16[56,128]{1,0:T(8,128)(2,1)} %bitcast.74, ...), custom_call_target="tpu_custom_call" | custom-call | tf_op jit(solution)/shard_map/pallas_call | solution.py:323
  112.1 41.2 %shard_map.166 = (bf16[8,896]{1,0:T(8,128)(2,1)}, bf16[8,2,16,896]{3,2,1,0:T(8,128)(2,1)}) custom-call(bf16[16,2,56,128]{3,2,1,0:T(8,128)(2,1)} %shard_map.165.x_ref, bf16[896,896]{1,0:T(8,128)(2,1)} %gate_hbm.1, bf16[896,896]{1,0:T(8,128)(2,1)} %up_hbm.1, bf16[896,128]{1,0:T(8,128)(2,1)} %down_map_hbm.1, bf16[128,896]{1,0:T(8,128)(2,1)} %gate_map_hbm.1, ...), custom_call_target="tpu_custom_call" | custom-call | tf_op jit(solution)/shard_map/pallas_call | solution.py:228
  153.2 1.3 copy.118
  (14 shorter events, 0.2 us)
Async XLA Ops:
  0.0 1.5 copy-start
  6.6 30.4 %copy-start.1 = (bf16[896,672]{0,1:T(8,128)(2,1)S(1)}, bf16[896,672]{0,1:T(8,128)(2,1)}, u32[]{:S(2)}) copy-start(bf16[896,672]{0,1:T(8,128)(2,1)} %param.21) | copy-start | bytes 3612676
  70.4 2.0 %copy-start.3 = (s32[4]{0:T(128)S(1)}, s32[4]{0:T(128)}, u32[]{:S(2)}) copy-start(s32[4]{0:T(128)} %param.24) | copy-start | bytes 52
  73.7 4.0 %copy-start.2 = (s32[4,48]{1,0:T(4,128)S(1)}, s32[4,48]{1,0:T(4,128)}, u32[]{:S(2)}) copy-start(s32[4,48]{1,0:T(4,128)} %param.25) | copy-start | bytes 2308
